TPU v7x, 32 devices: a whole 2x2x4 slice. The times are simulated.
32 devices in a mesh: leaf: 16 (over z, y, x), chip: 2 (over core).
Axes of the slice: x: 2, y: 2, z: 4, core: 2. Of those that a mesh axis runs over, the one named last changes fastest.
Arguments:
- points: bfloat16 [524288, 64], P(('leaf', 'chip')), may hold values from -14 to 14
- direction: float32 [524288, 16], P(('leaf', 'chip')), may hold values from -6 to 6
- ridge: float32 [16], replicated, may hold values from 0.3 to 3
- leaf_basis: bfloat16 [2048, 256, 128], P(('leaf', 'chip')), may hold values from -0.375 to 0.375
- local_basis: bfloat16 [2016, 256, 128], P(('leaf', 'chip')), may hold values from -1 to 1
- top_basis: bfloat16 [31, 256, 128], replicated, may hold values from -1 to 1
- leaf_pick: int32 [2048, 128], P(('leaf', 'chip')), may hold values from 0 to 255, as said below
- local_pick: int32 [2016, 128], P(('leaf', 'chip')), may hold values from 0 to 255, as said below
- top_pick: int32 [31, 128], replicated, may hold values from 0 to 255, as said below
- near_list: int32 [2048, 10], P(('leaf', 'chip')), may hold values from 0 to 2047, as said below
Outputs:
- product: float32 [524288, 16], P(('leaf', 'chip'))
Inputs may be any that keep to these rules, and one draw needn't show every extreme that they name: `leaf_pick`: each row names 128 different points of a leaf. `local_pick`: each row names 128 different rows of the children's stacked skeletons. `top_pick`: each row names 128 different rows of the children's stacked skeletons. `near_list`: the first entry of leaf i's list is i; every entry is a leaf of the same device subtree or of the subtree numbered one lower or one higher (subtrees numbered by leaf index times 32 / 16 plus chip index).
All inputs are finite; a program needn't handle non-finite values.
Results may differ from a plain program's by a relative error of at most 0.0065.
Values may be sent and summed in bfloat16 or wider, within the bound.
No kernel may reach another device: no remote copies, remote signals or barrier semaphores. Data moves between devices by JAX's collectives and lax.ppermute only.
A program may use at most 128 MiB of HBM per device.

v0:
```python
import jax
import jax.numpy as jnp
from jax import lax
from jax.sharding import PartitionSpec as P

inverse_width = 1.0 / 32.0


def shifted(array, axis, by):
    devices = lax.axis_size(axis)
    pairs = [(i, i + by) for i in range(devices) if 0 <= i + by < devices]
    return lax.ppermute(array, axis, pairs)


def from_partner(block, axis, distance):
    count = lax.axis_size(axis)
    route = []
    for low in range(count):
        high = low | 1 << distance
        if high != low and high < count:
            route += [(low, high), (high, low)]
    return lax.ppermute(block, axis, route)


def kernel_tile(left, right_points):
    cross_product = jnp.einsum(
        "...pd,...qd->...pq", left, right_points, preferred_element_type=jnp.float32
    )
    left_square_norm = jnp.sum(jnp.square(left.astype(jnp.float32)), -1)
    right_square_norm = jnp.sum(jnp.square(right_points.astype(jnp.float32)), -1)
    return jnp.exp(
        (2.0 * cross_product - left_square_norm[..., :, None] - right_square_norm[..., None, :])
        * inverse_width
    ).astype(jnp.bfloat16)


def select_rows(table, pick):
    width = table.shape[1]
    columns = lax.broadcasted_iota(jnp.int32, (1, 1, width), 2)
    selector = (pick[:, :, None] == columns).astype(table.dtype)
    return jnp.einsum("nkw,nwd->nkd", selector, table, preferred_element_type=jnp.float32).astype(
        table.dtype
    )


def pair_terms(coeff, skel):
    count, rank, cols = coeff.shape
    tiles = kernel_tile(skel[0::2], skel[1::2])
    left_term = jnp.einsum("npq,nqr->npr", tiles, coeff[1::2], preferred_element_type=jnp.float32)
    right_term = jnp.einsum("npq,npr->nqr", tiles, coeff[0::2], preferred_element_type=jnp.float32)
    return jnp.stack([left_term, right_term], 1).reshape(count, rank, cols)


def climb(coeff, skel, basis, pick):
    count, rank, cols = coeff.shape
    stacked = coeff.reshape(count // 2, 2 * rank, cols)
    parent = jnp.einsum("npk,npr->nkr", basis, stacked, preferred_element_type=jnp.float32).astype(
        jnp.bfloat16
    )
    joined = skel.reshape(count // 2, 2 * rank, skel.shape[2])
    return (parent, select_rows(joined, pick))


def near_term(coords, weights, near_list, point_position):
    count, leaf, dim = coords.shape
    packed = jnp.concatenate([coords, weights], -1)
    width = packed.shape[2]
    lower = shifted(packed, ("leaf", "chip"), 1)
    upper = shifted(packed, ("leaf", "chip"), -1)
    pool = jnp.concatenate([lower, packed, upper], 0)
    flat_pool = pool.reshape(3 * count, leaf * width)
    own_squares = jnp.sum(jnp.square(coords.astype(jnp.float32)), -1)
    owner = near_list // count
    column_ids = (owner - point_position + 1) * count + near_list % count
    pool_index = lax.broadcasted_iota(jnp.int32, (1, 3 * count), 1)

    def visit(total, column):
        selector = (column[:, None] == pool_index).astype(jnp.bfloat16)
        fetched = jnp.dot(selector, flat_pool, preferred_element_type=jnp.float32).astype(
            jnp.bfloat16
        )
        fetched = fetched.reshape(count, leaf, width)
        fetched_points = fetched[..., :dim]
        fetched_sq = jnp.sum(jnp.square(fetched_points.astype(jnp.float32)), -1)
        cross_product = jnp.einsum(
            "lpd,lqd->lpq", coords, fetched_points, preferred_element_type=jnp.float32
        )
        tiles = jnp.exp(
            (2.0 * cross_product - own_squares[:, :, None] - fetched_sq[:, None, :]) * inverse_width
        ).astype(jnp.bfloat16)
        return (
            total
            + jnp.einsum(
                "lpq,lqr->lpr", tiles, fetched[..., dim:], preferred_element_type=jnp.float32
            ),
            None,
        )

    start = jnp.zeros((count, leaf, weights.shape[2]), jnp.float32)
    total, _ = lax.scan(visit, start, column_ids.T)
    return total


def shards(
    points,
    direction,
    ridge,
    leaf_basis,
    local_basis,
    top_basis,
    leaf_pick,
    local_pick,
    top_pick,
    near_list,
):
    count, leaf, rank = leaf_basis.shape
    dim = points.shape[1]
    cols = direction.shape[1]
    coords = points.reshape(count, leaf, dim)
    weights = direction.astype(jnp.bfloat16).reshape(count, leaf, cols)
    chips = lax.axis_size("chip")
    subtrees = lax.axis_size("leaf") * chips
    point_position = lax.axis_index("leaf") * chips + lax.axis_index("chip")
    near = near_term(coords, weights, near_list, point_position)
    coeff = jnp.einsum(
        "lpk,lpr->lkr", leaf_basis, weights, preferred_element_type=jnp.float32
    ).astype(jnp.bfloat16)
    skel = select_rows(coords, leaf_pick)
    local_depth = count.bit_length() - 1
    local_terms = []
    for depth in range(local_depth, 0, -1):
        local_terms.append(pair_terms(coeff, skel))
        lo = 2 ** (depth - 1) - 1
        hi = 2**depth - 1
        coeff, skel = climb(coeff, skel, local_basis[lo:hi], local_pick[lo:hi])
    top_depth = subtrees.bit_length() - 1
    bits = [point_position >> step & 1 for step in range(top_depth)]
    top_terms = []
    mine = jnp.concatenate([coeff[0], skel[0]], -1)
    for step in range(top_depth):
        if step == 0:
            other = from_partner(mine, "chip", 0)
        else:
            other = from_partner(mine, "leaf", step - 1)
        tile = kernel_tile(mine[None, :, cols:], other[None, :, cols:])[0]
        top_terms.append(jnp.dot(tile, other[:, :cols], preferred_element_type=jnp.float32))
        if step + 1 < top_depth:
            left = jnp.where(bits[step] == 0, mine, other)
            right_points = jnp.where(bits[step] == 0, other, mine)
            parent_depth = top_depth - 1 - step
            node = 2**parent_depth - 1 + (point_position >> step + 1)
            basis = lax.dynamic_index_in_dim(top_basis, node, 0, keepdims=True)
            pick = lax.dynamic_index_in_dim(top_pick, node, 0, keepdims=True)
            stacked = jnp.stack([left, right_points], 0)
            up_coeff, up_skel = climb(stacked[:, :, :cols], stacked[:, :, cols:], basis, pick)
            mine = jnp.concatenate([up_coeff[0], up_skel[0]], -1)
    value = jnp.zeros((rank, cols), jnp.bfloat16)
    for step in range(top_depth - 1, -1, -1):
        parent_depth = top_depth - 1 - step
        node = 2**parent_depth - 1 + (point_position >> step + 1)
        basis = lax.dynamic_index_in_dim(top_basis, node, 0, keepdims=False)
        down = jnp.dot(basis, value, preferred_element_type=jnp.float32)
        half = lax.dynamic_slice_in_dim(down, bits[step] * rank, rank, 0)
        value = (top_terms[step] + half).astype(jnp.bfloat16)
    values = value[None]
    for depth in range(1, local_depth + 1):
        lo = 2 ** (depth - 1) - 1
        hi = 2**depth - 1
        down = jnp.einsum(
            "npk,nkr->npr", local_basis[lo:hi], values, preferred_element_type=jnp.float32
        )
        down = down.reshape(-1, rank, cols)
        values = (local_terms[local_depth - depth] + down).astype(jnp.bfloat16)
    far = jnp.einsum("lpk,lkr->lpr", leaf_basis, values, preferred_element_type=jnp.float32)
    return ridge[None, :] * direction + near.reshape(-1, cols) + far.reshape(-1, cols)


def solution(mesh):
    return jax.shard_map(
        shards,
        mesh=mesh,
        in_specs=(
            P(("leaf", "chip"), None),
            P(("leaf", "chip"), None),
            P(),
            P(("leaf", "chip"), None, None),
            P(("leaf", "chip"), None, None),
            P(),
            P(("leaf", "chip"), None),
            P(("leaf", "chip"), None),
            P(),
            P(("leaf", "chip"), None),
        ),
        out_specs=P(("leaf", "chip"), None),
        check_vma=False,
    )
```

profile of v0, /device:TPU:0, one launch (start us, length us, event | category | flops | bytes accessed | tf_op | source)
XLA Modules:
  0.0 484.8 jit_solution(8232504541302003712)
XLA Ops:
  129.6 15.5 %copy.128 = bf16[192,256,80]{0,2,1:T(8,128)(2,1)} copy(bf16[192,256,80]{1,0,2:T(8,128)(2,1)} %pad_maximum_fusion) | data formatting | bytes 15728640 | tf_op jit(solution)/shard_map/concatenate | solution.py:70
  145.1 12.7 %copy.129 = bf16[192,20480]{1,0:T(8,128)(2,1)} copy(bf16[192,20480]{0,1:T(8,128)(2,1)} %bitcast.350) | data formatting | bytes 15728640
  157.8 323.1 %while.11 = (s32[]{:T(128)}, f32[64,256,16]{1,2,0:T(8,128)}, s32[10,64]{1,0:T(8,128)}, bf16[192,20480]{1,0:T(8,128)(2,1)}, bf16[64,256,64]{1,2,0:T(8,128)(2,1)},...) while((s32[]{:T(128)}, f32[64,256,16]{1,2,0:T(8,128)}, s32[10,64]{1,0:T(8,128)}, ...), condition=%wide.region_3.4_spmd.clone, body=%wide.region_1.3_spmd.clone.sunk | while | flops 1200353280 | bytes 34800480 | solution.py:100
  165.2 7.2 %reshape.649 = bf16[64,256,80]{2,1,0:T(8,128)(2,1)} reshape(bf16[64,20480]{1,0:T(8,128)(2,1)} %convolution_convert_fusion.20) | data formatting | bytes 5242880 | tf_op jit(solution)/shard_map/while/body/eval_jaxpr/reshape | solution.py:82
  179.4 11.0 %fusion.361 = f32[64,256,16]{1,2,0:T(8,128)} fusion(bf16[64,256,64]{1,2,0:T(8,128)(2,1)} %get-tuple-element.187, f32[64,256]{1,0:T(8,128)S(1)} %multiply_reduce_fusion.25, f32[64,256]{1,0:T(8,128)S(1)} %get-tuple-element.188, bf16[64,256,80]{2,1,0:T(8,128)(2,1)} %reshape.649, f32[64,256,16]{1,2,0:T(8,128)} %get-tuple-element.176, pred[]{:T(512)S(6)} %compare.6), kind=kOutput, calls=%fused_computation.6.clone.1 | convolution fusion | flops 692584448 | bytes 12713985 | tf_op jit(solution)/shard_map/while/body/eval_jaxpr/lpq,lqr->lpr/dot_general | solution.py:93
  191.1 6.4 %convolution_convert_fusion.20 = bf16[64,20480]{1,0:T(8,128)(2,1)} fusion(bf16[192,20480]{1,0:T(8,128)(2,1)} %get-tuple-element.186, s32[64]{0:T(128)S(1)} %dynamic-slice_bitcast_fusion.2), kind=kOutput, calls=%fused_computation.1.clone.1 | convolution fusion | flops 504639488 | bytes 10486016 | tf_op jit(solution)/shard_map/while/body/eval_jaxpr/dot_general | solution.py:79
  197.4 7.2 %reshape.649 = bf16[64,256,80]{2,1,0:T(8,128)(2,1)} reshape(bf16[64,20480]{1,0:T(8,128)(2,1)} %convolution_convert_fusion.20) | data formatting | bytes 5242880 | tf_op jit(solution)/shard_map/while/body/eval_jaxpr/reshape | solution.py:82
  211.7 11.0 %fusion.361 = f32[64,256,16]{1,2,0:T(8,128)} fusion(bf16[64,256,64]{1,2,0:T(8,128)(2,1)} %get-tuple-element.187, f32[64,256]{1,0:T(8,128)S(1)} %multiply_reduce_fusion.25, f32[64,256]{1,0:T(8,128)S(1)} %get-tuple-element.188, bf16[64,256,80]{2,1,0:T(8,128)(2,1)} %reshape.649, f32[64,256,16]{1,2,0:T(8,128)} %get-tuple-element.176, pred[]{:T(512)S(6)} %compare.6), kind=kOutput, calls=%fused_computation.6.clone.1 | convolution fusion | flops 692584448 | bytes 12713985 | tf_op jit(solution)/shard_map/while/body/eval_jaxpr/lpq,lqr->lpr/dot_general | solution.py:93
  223.4 6.4 %convolution_convert_fusion.20 = bf16[64,20480]{1,0:T(8,128)(2,1)} fusion(bf16[192,20480]{1,0:T(8,128)(2,1)} %get-tuple-element.186, s32[64]{0:T(128)S(1)} %dynamic-slice_bitcast_fusion.2), kind=kOutput, calls=%fused_computation.1.clone.1 | convolution fusion | flops 504639488 | bytes 10486016 | tf_op jit(solution)/shard_map/while/body/eval_jaxpr/dot_general | solution.py:79
  229.7 7.2 %reshape.649 = bf16[64,256,80]{2,1,0:T(8,128)(2,1)} reshape(bf16[64,20480]{1,0:T(8,128)(2,1)} %convolution_convert_fusion.20) | data formatting | bytes 5242880 | tf_op jit(solution)/shard_map/while/body/eval_jaxpr/reshape | solution.py:82
  244.0 11.0 %fusion.361 = f32[64,256,16]{1,2,0:T(8,128)} fusion(bf16[64,256,64]{1,2,0:T(8,128)(2,1)} %get-tuple-element.187, f32[64,256]{1,0:T(8,128)S(1)} %multiply_reduce_fusion.25, f32[64,256]{1,0:T(8,128)S(1)} %get-tuple-element.188, bf16[64,256,80]{2,1,0:T(8,128)(2,1)} %reshape.649, f32[64,256,16]{1,2,0:T(8,128)} %get-tuple-element.176, pred[]{:T(512)S(6)} %compare.6), kind=kOutput, calls=%fused_computation.6.clone.1 | convolution fusion | flops 692584448 | bytes 12713985 | tf_op jit(solution)/shard_map/while/body/eval_jaxpr/lpq,lqr->lpr/dot_general | solution.py:93
  255.6 6.4 %convolution_convert_fusion.20 = bf16[64,20480]{1,0:T(8,128)(2,1)} fusion(bf16[192,20480]{1,0:T(8,128)(2,1)} %get-tuple-element.186, s32[64]{0:T(128)S(1)} %dynamic-slice_bitcast_fusion.2), kind=kOutput, calls=%fused_computation.1.clone.1 | convolution fusion | flops 504639488 | bytes 10486016 | tf_op jit(solution)/shard_map/while/body/eval_jaxpr/dot_general | solution.py:79
  262.0 7.2 %reshape.649 = bf16[64,256,80]{2,1,0:T(8,128)(2,1)} reshape(bf16[64,20480]{1,0:T(8,128)(2,1)} %convolution_convert_fusion.20) | data formatting | bytes 5242880 | tf_op jit(solution)/shard_map/while/body/eval_jaxpr/reshape | solution.py:82
  276.3 11.0 %fusion.361 = f32[64,256,16]{1,2,0:T(8,128)} fusion(bf16[64,256,64]{1,2,0:T(8,128)(2,1)} %get-tuple-element.187, f32[64,256]{1,0:T(8,128)S(1)} %multiply_reduce_fusion.25, f32[64,256]{1,0:T(8,128)S(1)} %get-tuple-element.188, bf16[64,256,80]{2,1,0:T(8,128)(2,1)} %reshape.649, f32[64,256,16]{1,2,0:T(8,128)} %get-tuple-element.176, pred[]{:T(512)S(6)} %compare.6), kind=kOutput, calls=%fused_computation.6.clone.1 | convolution fusion | flops 692584448 | bytes 12713985 | tf_op jit(solution)/shard_map/while/body/eval_jaxpr/lpq,lqr->lpr/dot_general | solution.py:93
  287.9 6.4 %convolution_convert_fusion.20 = bf16[64,20480]{1,0:T(8,128)(2,1)} fusion(bf16[192,20480]{1,0:T(8,128)(2,1)} %get-tuple-element.186, s32[64]{0:T(128)S(1)} %dynamic-slice_bitcast_fusion.2), kind=kOutput, calls=%fused_computation.1.clone.1 | convolution fusion | flops 504639488 | bytes 10486016 | tf_op jit(solution)/shard_map/while/body/eval_jaxpr/dot_general | solution.py:79
  294.3 7.2 %reshape.649 = bf16[64,256,80]{2,1,0:T(8,128)(2,1)} reshape(bf16[64,20480]{1,0:T(8,128)(2,1)} %convolution_convert_fusion.20) | data formatting | bytes 5242880 | tf_op jit(solution)/shard_map/while/body/eval_jaxpr/reshape | solution.py:82
  308.5 11.0 %fusion.361 = f32[64,256,16]{1,2,0:T(8,128)} fusion(bf16[64,256,64]{1,2,0:T(8,128)(2,1)} %get-tuple-element.187, f32[64,256]{1,0:T(8,128)S(1)} %multiply_reduce_fusion.25, f32[64,256]{1,0:T(8,128)S(1)} %get-tuple-element.188, bf16[64,256,80]{2,1,0:T(8,128)(2,1)} %reshape.649, f32[64,256,16]{1,2,0:T(8,128)} %get-tuple-element.176, pred[]{:T(512)S(6)} %compare.6), kind=kOutput, calls=%fused_computation.6.clone.1 | convolution fusion | flops 692584448 | bytes 12713985 | tf_op jit(solution)/shard_map/while/body/eval_jaxpr/lpq,lqr->lpr/dot_general | solution.py:93
  320.2 6.4 %convolution_convert_fusion.20 = bf16[64,20480]{1,0:T(8,128)(2,1)} fusion(bf16[192,20480]{1,0:T(8,128)(2,1)} %get-tuple-element.186, s32[64]{0:T(128)S(1)} %dynamic-slice_bitcast_fusion.2), kind=kOutput, calls=%fused_computation.1.clone.1 | convolution fusion | flops 504639488 | bytes 10486016 | tf_op jit(solution)/shard_map/while/body/eval_jaxpr/dot_general | solution.py:79
  326.5 7.2 %reshape.649 = bf16[64,256,80]{2,1,0:T(8,128)(2,1)} reshape(bf16[64,20480]{1,0:T(8,128)(2,1)} %convolution_convert_fusion.20) | data formatting | bytes 5242880 | tf_op jit(solution)/shard_map/while/body/eval_jaxpr/reshape | solution.py:82
  340.8 11.0 %fusion.361 = f32[64,256,16]{1,2,0:T(8,128)} fusion(bf16[64,256,64]{1,2,0:T(8,128)(2,1)} %get-tuple-element.187, f32[64,256]{1,0:T(8,128)S(1)} %multiply_reduce_fusion.25, f32[64,256]{1,0:T(8,128)S(1)} %get-tuple-element.188, bf16[64,256,80]{2,1,0:T(8,128)(2,1)} %reshape.649, f32[64,256,16]{1,2,0:T(8,128)} %get-tuple-element.176, pred[]{:T(512)S(6)} %compare.6), kind=kOutput, calls=%fused_computation.6.clone.1 | convolution fusion | flops 692584448 | bytes 12713985 | tf_op jit(solution)/shard_map/while/body/eval_jaxpr/lpq,lqr->lpr/dot_general | solution.py:93
  352.5 6.4 %convolution_convert_fusion.20 = bf16[64,20480]{1,0:T(8,128)(2,1)} fusion(bf16[192,20480]{1,0:T(8,128)(2,1)} %get-tuple-element.186, s32[64]{0:T(128)S(1)} %dynamic-slice_bitcast_fusion.2), kind=kOutput, calls=%fused_computation.1.clone.1 | convolution fusion | flops 504639488 | bytes 10486016 | tf_op jit(solution)/shard_map/while/body/eval_jaxpr/dot_general | solution.py:79
  358.8 7.2 %reshape.649 = bf16[64,256,80]{2,1,0:T(8,128)(2,1)} reshape(bf16[64,20480]{1,0:T(8,128)(2,1)} %convolution_convert_fusion.20) | data formatting | bytes 5242880 | tf_op jit(solution)/shard_map/while/body/eval_jaxpr/reshape | solution.py:82
  373.1 11.0 %fusion.361 = f32[64,256,16]{1,2,0:T(8,128)} fusion(bf16[64,256,64]{1,2,0:T(8,128)(2,1)} %get-tuple-element.187, f32[64,256]{1,0:T(8,128)S(1)} %multiply_reduce_fusion.25, f32[64,256]{1,0:T(8,128)S(1)} %get-tuple-element.188, bf16[64,256,80]{2,1,0:T(8,128)(2,1)} %reshape.649, f32[64,256,16]{1,2,0:T(8,128)} %get-tuple-element.176, pred[]{:T(512)S(6)} %compare.6), kind=kOutput, calls=%fused_computation.6.clone.1 | convolution fusion | flops 692584448 | bytes 12713985 | tf_op jit(solution)/shard_map/while/body/eval_jaxpr/lpq,lqr->lpr/dot_general | solution.py:93
  384.7 6.4 %convolution_convert_fusion.20 = bf16[64,20480]{1,0:T(8,128)(2,1)} fusion(bf16[192,20480]{1,0:T(8,128)(2,1)} %get-tuple-element.186, s32[64]{0:T(128)S(1)} %dynamic-slice_bitcast_fusion.2), kind=kOutput, calls=%fused_computation.1.clone.1 | convolution fusion | flops 504639488 | bytes 10486016 | tf_op jit(solution)/shard_map/while/body/eval_jaxpr/dot_general | solution.py:79
  391.1 7.2 %reshape.649 = bf16[64,256,80]{2,1,0:T(8,128)(2,1)} reshape(bf16[64,20480]{1,0:T(8,128)(2,1)} %convolution_convert_fusion.20) | data formatting | bytes 5242880 | tf_op jit(solution)/shard_map/while/body/eval_jaxpr/reshape | solution.py:82
  405.4 11.0 %fusion.361 = f32[64,256,16]{1,2,0:T(8,128)} fusion(bf16[64,256,64]{1,2,0:T(8,128)(2,1)} %get-tuple-element.187, f32[64,256]{1,0:T(8,128)S(1)} %multiply_reduce_fusion.25, f32[64,256]{1,0:T(8,128)S(1)} %get-tuple-element.188, bf16[64,256,80]{2,1,0:T(8,128)(2,1)} %reshape.649, f32[64,256,16]{1,2,0:T(8,128)} %get-tuple-element.176, pred[]{:T(512)S(6)} %compare.6), kind=kOutput, calls=%fused_computation.6.clone.1 | convolution fusion | flops 692584448 | bytes 12713985 | tf_op jit(solution)/shard_map/while/body/eval_jaxpr/lpq,lqr->lpr/dot_general | solution.py:93
  417.0 6.4 %convolution_convert_fusion.20 = bf16[64,20480]{1,0:T(8,128)(2,1)} fusion(bf16[192,20480]{1,0:T(8,128)(2,1)} %get-tuple-element.186, s32[64]{0:T(128)S(1)} %dynamic-slice_bitcast_fusion.2), kind=kOutput, calls=%fused_computation.1.clone.1 | convolution fusion | flops 504639488 | bytes 10486016 | tf_op jit(solution)/shard_map/while/body/eval_jaxpr/dot_general | solution.py:79
  423.4 7.2 %reshape.649 = bf16[64,256,80]{2,1,0:T(8,128)(2,1)} reshape(bf16[64,20480]{1,0:T(8,128)(2,1)} %convolution_convert_fusion.20) | data formatting | bytes 5242880 | tf_op jit(solution)/shard_map/while/body/eval_jaxpr/reshape | solution.py:82
  437.6 11.0 %fusion.361 = f32[64,256,16]{1,2,0:T(8,128)} fusion(bf16[64,256,64]{1,2,0:T(8,128)(2,1)} %get-tuple-element.187, f32[64,256]{1,0:T(8,128)S(1)} %multiply_reduce_fusion.25, f32[64,256]{1,0:T(8,128)S(1)} %get-tuple-element.188, bf16[64,256,80]{2,1,0:T(8,128)(2,1)} %reshape.649, f32[64,256,16]{1,2,0:T(8,128)} %get-tuple-element.176, pred[]{:T(512)S(6)} %compare.6), kind=kOutput, calls=%fused_computation.6.clone.1 | convolution fusion | flops 692584448 | bytes 12713985 | tf_op jit(solution)/shard_map/while/body/eval_jaxpr/lpq,lqr->lpr/dot_general | solution.py:93
  449.3 6.4 %convolution_convert_fusion.20 = bf16[64,20480]{1,0:T(8,128)(2,1)} fusion(bf16[192,20480]{1,0:T(8,128)(2,1)} %get-tuple-element.186, s32[64]{0:T(128)S(1)} %dynamic-slice_bitcast_fusion.2), kind=kOutput, calls=%fused_computation.1.clone.1 | convolution fusion | flops 504639488 | bytes 10486016 | tf_op jit(solution)/shard_map/while/body/eval_jaxpr/dot_general | solution.py:79
  455.6 7.2 %reshape.649 = bf16[64,256,80]{2,1,0:T(8,128)(2,1)} reshape(bf16[64,20480]{1,0:T(8,128)(2,1)} %convolution_convert_fusion.20) | data formatting | bytes 5242880 | tf_op jit(solution)/shard_map/while/body/eval_jaxpr/reshape | solution.py:82
  469.9 11.0 %fusion.361 = f32[64,256,16]{1,2,0:T(8,128)} fusion(bf16[64,256,64]{1,2,0:T(8,128)(2,1)} %get-tuple-element.187, f32[64,256]{1,0:T(8,128)S(1)} %multiply_reduce_fusion.25, f32[64,256]{1,0:T(8,128)S(1)} %get-tuple-element.188, bf16[64,256,80]{2,1,0:T(8,128)(2,1)} %reshape.649, f32[64,256,16]{1,2,0:T(8,128)} %get-tuple-element.176, pred[]{:T(512)S(6)} %compare.6), kind=kOutput, calls=%fused_computation.6.clone.1 | convolution fusion | flops 692584448 | bytes 12713985 | tf_op jit(solution)/shard_map/while/body/eval_jaxpr/lpq,lqr->lpr/dot_general | solution.py:93
  (258 shorter events, 216.3 us)
Async XLA Ops:
  0.0 69.0 %copy-start = (bf16[31,256,128]{2,1,0:T(8,128)(2,1)S(1)}, bf16[31,256,128]{2,1,0:T(8,128)(2,1)}, u32[]{:S(2)}) copy-start(bf16[31,256,128]{2,1,0:T(8,128)(2,1)} %param.17) | copy-start | bytes 6094852
  3.9 8.5 %copy-start.29 = (s32[63,128]{1,0:T(8,128)S(1)}, s32[63,128]{1,0:T(8,128)}, u32[]{:S(2)}) copy-start(s32[63,128]{1,0:T(8,128)} %param.19) | copy-start | bytes 96772
  3.9 9.7 %copy-start.4 = (bf16[16384,64]{0,1:T(8,128)(2,1)S(1)}, bf16[16384,64]{0,1:T(8,128)(2,1)}, u32[]{:S(2)}) copy-start(bf16[16384,64]{0,1:T(8,128)(2,1)} %param.12) | copy-start | bytes 6291460
  4.0 9.7 %copy-start.32 = (s32[64,128]{1,0:T(8,128)S(1)}, s32[64,128]{1,0:T(8,128)}, u32[]{:S(2)}) copy-start(s32[64,128]{1,0:T(8,128)} %param.18) | copy-start | bytes 98308
  4.0 12.0 %copy-start.2 = (bf16[64,256,80]{1,0,2:T(8,128)(2,1)}, bf16[64,256,80]{1,0,2:T(8,128)(2,1)S(1)}, u32[]{:S(2)}) copy-start(bf16[64,256,80]{1,0,2:T(8,128)(2,1)S(1)} %constant_dynamic-update-slice_fusion) | copy-start | bytes 7864324
  7.1 113.4 %collective-permute-start = (bf16[64,256,80]{1,2,0:T(8,128)(2,1)}, bf16[64,256,80]{1,2,0:T(8,128)(2,1)}, u32[]{:S(2)}, u32[]{:S(2)}) collective-permute-start(bf16[64,256,80]{1,2,0:T(8,128)(2,1)} %copy.124), channel_id=1, source_target_pairs={{0,1},{1,2},{2,3},{3,4},{4,5},{5,6},{6,7},{7,8},{8,9},{9,10},{10,1... | collective-permute-start | bytes 7864328 | tf_op jit(solution)/shard_map/ppermute | solution.py:12
  11.0 112.3 %collective-permute-start.1 = (bf16[64,256,80]{1,2,0:T(8,128)(2,1)}, bf16[64,256,80]{1,2,0:T(8,128)(2,1)}, u32[]{:S(2)}, u32[]{:S(2)}) collective-permute-start(bf16[64,256,80]{1,2,0:T(8,128)(2,1)} %copy.124), channel_id=1, source_target_pairs={{1,0},{2,1},{3,2},{4,3},{5,4},{6,5},{7,6},{8,7},{9,8},{10,9},{11,1... | collective-permute-start | bytes 7864328 | tf_op jit(solution)/shard_map/ppermute | solution.py:12
  34.9 4.1 copy-start.13
  40.7 23.1 %copy-start.8 = (bf16[64,128,64]{1,2,0:T(8,128)(2,1)S(1)}, bf16[64,128,64]{1,2,0:T(8,128)(2,1)}, u32[]{:S(2)}) copy-start(bf16[64,128,64]{1,2,0:T(8,128)(2,1)} %copy-done.7) | copy-start | bytes 3145732
  41.8 3.8 copy-start.27
  42.9 4.4 copy-start.28
  45.6 33.4 %collective-permute-start.2 = (bf16[128,80]{0,1:T(8,128)(2,1)}, bf16[128,80]{0,1:T(8,128)(2,1)}, u32[]{:S(2)}, u32[]{:S(2)}) collective-permute-start(bf16[128,80]{0,1:T(8,128)(2,1)} %pad_maximum_fusion.6), channel_id=1, source_target_pairs={{0,1},{1,0},{2,3},{3,2},{4,5},{5,4},{6,7},{7,6},{8,9},{9,8},{10,11... | collective-permute-start | bytes 61448 | tf_op jit(solution)/shard_map/ppermute | solution.py:22
  47.3 14.5 %copy-start.10 = (bf16[32,128,64]{1,2,0:T(8,128)(2,1)S(1)}, bf16[32,128,64]{1,2,0:T(8,128)(2,1)}, u32[]{:S(2)}) copy-start(bf16[32,128,64]{1,2,0:T(8,128)(2,1)} %copy-done.9) | copy-start | bytes 1572868
  47.3 15.2 %copy-start.14 = (bf16[32,128,16]{1,2,0:T(8,128)(2,1)S(1)}, bf16[32,128,16]{1,2,0:T(8,128)(2,1)}, u32[]{:S(2)}) copy-start(bf16[32,128,16]{1,2,0:T(8,128)(2,1)} %copy-done.13) | copy-start | bytes 393220
  64.1 5.7 %copy-start.25 = (f32[2,1,128,16]{2,3,0,1:T(8,128)S(1)}, f32[2,1,128,16]{2,3,0,1:T(8,128)}, u32[]{:S(2)}) copy-start(f32[2,1,128,16]{2,3,0,1:T(8,128)} %convolution_bitcast_fusion.15) | copy-start | bytes 49156
  65.5 4.3 copy-start.26
  65.5 4.9 %copy-start.18 = (f32[4,1,128,16]{2,3,0,1:T(8,128)S(1)}, f32[4,1,128,16]{2,3,0,1:T(8,128)}, u32[]{:S(2)}) copy-start(f32[4,1,128,16]{2,3,0,1:T(8,128)} %convolution_bitcast_fusion.12) | copy-start | bytes 98308
  65.5 4.9 %copy-start.19 = (f32[4,1,128,16]{2,3,0,1:T(8,128)S(1)}, f32[4,1,128,16]{2,3,0,1:T(8,128)}, u32[]{:S(2)}) copy-start(f32[4,1,128,16]{2,3,0,1:T(8,128)} %convolution_bitcast_fusion.10) | copy-start | bytes 98308
  65.5 4.9 %copy-start.15 = (f32[8,1,128,16]{2,3,0,1:T(8,128)S(1)}, f32[8,1,128,16]{2,3,0,1:T(8,128)}, u32[]{:S(2)}) copy-start(f32[8,1,128,16]{2,3,0,1:T(8,128)} %convolution_bitcast_fusion.7) | copy-start | bytes 196612
  65.5 4.9 %copy-start.12 = (f32[16,1,128,16]{2,3,0,1:T(8,128)S(1)}, f32[16,1,128,16]{2,3,0,1:T(8,128)}, u32[]{:S(2)}) copy-start(f32[16,1,128,16]{2,3,0,1:T(8,128)} %convolution_bitcast_fusion.4) | copy-start | bytes 393220
  70.4 5.7 %copy-start.17 = (f32[2,2,128,16]{2,3,0,1:T(8,128)S(1)}, f32[2,2,128,16]{2,3,0,1:T(8,128)}, u32[]{:S(2)}) copy-start(f32[2,2,128,16]{2,3,0,1:T(8,128)} %pad_maximum_fusion.5) | copy-start | bytes 98308
  70.5 8.5 %copy-start.23 = (bf16[128,64]{0,1:T(8,128)(2,1)S(1)}, bf16[128,64]{0,1:T(8,128)(2,1)}, u32[]{:S(2)}) copy-start(bf16[128,64]{0,1:T(8,128)(2,1)} %copy-done.22) | copy-start | bytes 49156
  72.9 32.6 %slice-start = ((bf16[63,256,128]{2,1,0:T(8,128)(2,1)}), bf16[1,256,128]{2,1,0:T(8,128)(2,1)S(1)}, s32[]{:S(2)}) async-start(bf16[63,256,128]{2,1,0:T(8,128)(2,1)} %param.16), calls=%async_computation | async-start | bytes 131072 | tf_op jit(solution)/shard_map/slice | solution.py:170
  80.7 3.8 collective-permute-start.3
  85.6 4.4 collective-permute-start.4
  91.1 4.8 collective-permute-start.5
  96.9 4.9 %collective-permute-start.6 = (bf16[128,80]{0,1:T(8,128)(2,1)S(1)}, bf16[128,80]{0,1:T(8,128)(2,1)S(1)}, u32[]{:S(2)}, u32[]{:S(2)}) collective-permute-start(bf16[128,80]{0,1:T(8,128)(2,1)S(1)} %pad_maximum_fusion.10), channel_id=1, source_target_pairs={{0,16},{16,0},{2,18},{18,2},{4,20},{20,4},{6,22},{22,6},{8,24},{24... | collective-permute-start | bytes 61448 | tf_op jit(solution)/shard_map/ppermute | solution.py:22
  120.5 5.5 %copy-start.3 = (bf16[64,256,80]{1,0,2:T(8,128)(2,1)S(1)}, bf16[64,256,80]{1,0,2:T(8,128)(2,1)}, u32[]{:S(2)}) copy-start(bf16[64,256,80]{1,0,2:T(8,128)(2,1)} %copy-done.2) | copy-start | bytes 7864324
  145.1 12.7 %copy-start.24 = (f32[64,256]{1,0:T(8,128)S(1)}, f32[64,256]{1,0:T(8,128)}, u32[]{:S(2)}) copy-start(f32[64,256]{1,0:T(8,128)} %reduce_sum.219) | copy-start | bytes 196612
  157.8 324.5 %copy-start.6 = (f32[16384,16]{0,1:T(8,128)S(1)}, f32[16384,16]{0,1:T(8,128)}, u32[]{:S(2)}) copy-start(f32[16384,16]{0,1:T(8,128)} %param.13) | copy-start | bytes 3145732
  157.8 324.5 %copy-start.31 = (f32[16]{0:T(128)S(1)}, f32[16]{0:T(128)}, u32[]{:S(2)}) copy-start(f32[16]{0:T(128)} %param.14) | copy-start | bytes 196
  480.9 3.9 copy-start.1
  (9 other events, 13.9 us)
where the time goes:
time: 490 us; the launch traced here: 485 us
  matrix products  231 us (47%)
  local copies, waits for them, and re-layouts  189 us (39%)
  other arithmetic  40.3 us (8%)
  starting transfers between devices  17.5 us (4%)
  waiting for transfers between devices  6.61 us (1%)
    dot_general x10, matrix products, visit(): jnp.einsum('lpq,lqr->lpr', tiles, fetched[..., dim:], preferred_element_t...  110 us
    reshape x10, local copies, waits for them, and re-layouts, visit(): fetched = fetched.reshape(count, leaf, width)  72.2 us
    dot_general x10, matrix products, visit(): jnp.dot(selector, flat_pool, preferred_element_type=jnp.float32)  63.5 us
    while x10, local copies, waits for them, and re-layouts  47.8 us
    reduce_sum x10, other arithmetic, visit(): fetched_sq = jnp.sum(jnp.square(fetched_points.astype(jnp.float32)), -1)  22.6 us
    unnamed x70, local copies, waits for them, and re-layouts  19 us
    concatenate x1, local copies, waits for them, and re-layouts, near_term(): pool = jnp.concatenate([lower, packed, upper], 0)  15.5 us
    dot_general x11, matrix products, select_rows(): jnp.einsum('nkw,nwd->nkd', selector, table, preferred_element_type=jnp.fl...  13.4 us
  transfers between devices with their start and end apart: 7, of which 4 were waited for; matrix products, arithmetic and copies ran while one was open for 18% of the time, Pallas kernels for 0%

commit v1 on v0

v1 whole, which is shorter than its diff:
```python
import functools
import math

import jax
import jax.numpy as jnp
from jax import lax
from jax.experimental import pallas as pl
from jax.experimental.pallas import tpu as pltpu
from jax.sharding import PartitionSpec as P

f32 = jnp.float32
bf16 = jnp.bfloat16
AXES = ("leaf", "chip")
SCALE = math.log2(math.e) / 32.0
FEAT = 128
GROUP = 8


def dot(a, b, ca=1, cb=0):
    return lax.dot_general(a, b, (((ca,), (cb,)), ((), ())), preferred_element_type=f32)


def square_rows(xf):
    n = jnp.sum(xf * xf, axis=0, keepdims=True)
    hi = n.astype(bf16).astype(f32)
    rest = n - hi
    mid = rest.astype(bf16).astype(f32)
    low = rest - mid
    row = lax.broadcasted_iota(jnp.int32, (16, xf.shape[1]), 0)
    zero = jnp.zeros((), f32)
    neg = jnp.where(row == 0, -hi, jnp.where(row == 1, -mid, jnp.where(row == 2, -low, zero)))
    ones = jnp.where(row < 3, jnp.ones((), f32), zero)
    return neg.astype(bf16), ones.astype(bf16)


def feature_pair(x):
    dim, width = x.shape
    xf = x.astype(f32)
    neg, ones = square_rows(xf)
    pad = jnp.zeros((FEAT - dim - 32, width), bf16)
    left = jnp.concatenate([(xf + xf).astype(bf16), ones, neg, pad], 0)
    right = jnp.concatenate([x, neg, ones, pad], 0)
    return left, right


def swap_form(left, dim):
    half = (left[:dim].astype(f32) * 0.5).astype(bf16)
    return jnp.concatenate([half, left[dim + 16 : dim + 32], left[dim : dim + 16], left[dim + 32 :]], 0)


def selector(pick_row, width):
    rows = lax.broadcasted_iota(jnp.int32, (width, pick_row.shape[1]), 0)
    return jnp.where(rows == pick_row, jnp.ones((), f32), jnp.zeros((), f32)).astype(bf16)


def gauss(right_rows, left_cols):
    s = dot(right_rows, left_cols)
    return jnp.exp2(s * SCALE).astype(bf16)


def grouped(count, group, fn):
    group = min(group, count)

    def body(t, carry):
        for u in range(group):
            fn(t * group + u)
        return carry

    if count == group:
        body(0, 0)
    else:
        lax.fori_loop(0, count // group, body, 0)


def lanes(start, width):
    if isinstance(start, int):
        return pl.ds(start * width, width)
    return pl.ds(pl.multiple_of(start * width, width), width)


def up_kernel(dims, xt, wt, leaf_pick, local_pick, leaf_hbm, local_hbm, at, b, terms, root, lb, nb, coeff, skel, sems):
    count, leaf, rank, dim, cols = dims
    get_leaf = pltpu.make_async_copy(leaf_hbm, lb, sems.at[0])
    get_local = pltpu.make_async_copy(local_hbm, nb, sems.at[1])
    get_leaf.start()
    get_local.start()

    def prepare(l):
        left, right = feature_pair(xt[:, lanes(l, leaf)])
        at[l] = left
        b[l] = right.T

    grouped(count, 4, prepare)
    get_leaf.wait()
    base = count - 1

    def leaf_step(l):
        c = dot(wt[:, lanes(l, leaf)], lb[l])
        coeff[:, lanes(base + l, rank)] = c.astype(bf16)
        sel = selector(leaf_pick[pl.ds(l, 1), :], leaf)
        skel[:, lanes(base + l, rank)] = dot(at[l], sel).astype(bf16)

    grouped(count, 4, leaf_step)
    get_local.wait()
    depth = count.bit_length() - 1
    for d in range(depth, 0, -1):
        off = 2**d - 1
        up = 2 ** (d - 1) - 1

        def pair_step(m):
            both = pl.ds((off + 2 * m) * rank, 2 * rank)
            if not isinstance(m, int):
                both = pl.ds(pl.multiple_of((off + 2 * m) * rank, rank), 2 * rank)
            c2 = coeff[:, both]
            s2 = skel[:, both]
            left, right = s2[:, :rank], s2[:, rank:]
            c = dot(c2, nb[up + m])
            sel = selector(local_pick[pl.ds(up + m, 1), :], 2 * rank)
            s = dot(s2, sel)
            coeff[:, lanes(up + m, rank)] = c.astype(bf16)
            skel[:, lanes(up + m, rank)] = s.astype(bf16)
            g = gauss(swap_form(right, dim).T, left)
            term_left = dot(c2[:, rank:], g)
            term_right = dot(c2[:, :rank], g, 1, 1)
            terms[:, lanes(2**d - 2 + 2 * m, rank)] = term_left
            terms[:, lanes(2**d - 1 + 2 * m, rank)] = term_right

        grouped(2 ** (d - 1), 4, pair_step)
    root[:cols, :] = coeff[:, :rank]
    root[cols:, :] = skel[:dim, :rank]


def upward(xt, wt, leaf_pick, local_pick, leaf_basis, local_basis):
    count, leaf, rank = leaf_basis.shape
    dim, cols = xt.shape[0], wt.shape[0]
    vm = pl.BlockSpec(memory_space=pltpu.VMEM)
    hbm = pl.BlockSpec(memory_space=pl.ANY)
    return pl.pallas_call(
        functools.partial(up_kernel, (count, leaf, rank, dim, cols)),
        in_specs=[vm, vm, vm, vm, hbm, hbm],
        out_specs=[vm] * 4,
        out_shape=[
            jax.ShapeDtypeStruct((count, FEAT, leaf), bf16),
            jax.ShapeDtypeStruct((count, leaf, FEAT), bf16),
            jax.ShapeDtypeStruct((cols, (2 * count - 2) * rank), f32),
            jax.ShapeDtypeStruct((cols + dim, rank), bf16),
        ],
        scratch_shapes=[
            pltpu.VMEM(leaf_basis.shape, bf16),
            pltpu.VMEM(local_basis.shape, bf16),
            pltpu.VMEM((cols, (2 * count - 1) * rank), bf16),
            pltpu.VMEM((FEAT, (2 * count - 1) * rank), bf16),
            pltpu.SemaphoreType.DMA((2,)),
        ],
        compiler_params=pltpu.CompilerParams(vmem_limit_bytes=48 << 20),
        name="upward",
    )(xt, wt, leaf_pick, local_pick, leaf_basis, local_basis)


def near_pairs(count, entries, lst, pair, at, b, w, acc, tiles):
    h = GROUP
    for u in range(h):
        pair[u] = count * count

    def scan(i, pos):
        for e in range(entries):
            pair[pos + e] = i * count + lst[e, i]
        return pos + lst[entries, i]

    end = lax.fori_loop(0, count, scan, h)
    for u in range(3 * h):
        pair[end + u] = count * count
    total = end - h
    tiles[...] = jnp.zeros_like(tiles)
    acc[...] = jnp.zeros_like(acc)

    def first(k, slot):
        code = pair[k]
        i = code // count
        v = code - i * count
        tiles[slot] = gauss(b[v], at[jnp.where(i < count, i, 0)])

    def second(k, slot):
        code = pair[k]
        i = code // count
        v = code - i * count
        leaf = b.shape[1]
        return i, dot(w[:, lanes(v, leaf)], tiles[slot])

    def body(t, carry):
        for phase in range(2):
            k = (2 * t + phase) * h
            got = []
            for u in range(h):
                first(k + h + u, (1 - phase) * h + u)
                got.append(second(k + u, phase * h + u))
            for i, o in got:
                acc[i] += o
        return carry

    phases = (total + h - 1) // h + 1
    lax.fori_loop(0, (phases + 1) // 2, body, 0)


def near_scratch(count, entries, leaf, cols):
    return [
        pltpu.SMEM((count * entries + entries + 4 * GROUP,), jnp.int32),
        pltpu.VMEM((count + 1, cols, leaf), f32),
        pltpu.VMEM((2 * GROUP, leaf, leaf), bf16),
    ]


def near_own_kernel(count, entries, lst, at, b, w, out, pair, acc, tiles):
    near_pairs(count, entries, lst, pair, at, b, w, acc, tiles)
    leaf = b.shape[1]
    grouped(count, 4, lambda l: out.__setitem__((slice(None), lanes(l, leaf)), acc[l]))


def near_back_kernel(count, entries, lst, xlow, b, w, out, pair, acc, tiles, at):
    leaf = b.shape[1]

    def prepare(l):
        at[l] = feature_pair(xlow[:, lanes(l, leaf)])[0]

    grouped(count, 4, prepare)
    near_pairs(count, entries, lst, pair, at, b, w, acc, tiles)
    grouped(count, 4, lambda l: out.__setitem__((slice(None), lanes(l, leaf)), acc[l].astype(bf16)))


def near_low_kernel(count, entries, lst, at, xlow, w, add1, add2, out, pair, acc, tiles, b):
    leaf = at.shape[2]

    def prepare(l):
        b[l] = feature_pair(xlow[:, lanes(l, leaf)])[1].T

    grouped(count, 4, prepare)
    near_pairs(count, entries, lst, pair, at, b, w, acc, tiles)

    def finish(l):
        s = lanes(l, leaf)
        out[:, s] = acc[l] + add1[:, s] + add2[:, s]

    grouped(count, 4, finish)


def near_call(kernel, lst, operands, count, entries, leaf, cols, dtype, extra, name):
    vm = pl.BlockSpec(memory_space=pltpu.VMEM)
    return pl.pallas_call(
        functools.partial(kernel, count, entries),
        grid_spec=pltpu.PrefetchScalarGridSpec(
            num_scalar_prefetch=1,
            grid=(1,),
            in_specs=[vm] * len(operands),
            out_specs=vm,
            scratch_shapes=near_scratch(count, entries, leaf, cols) + extra,
        ),
        out_shape=jax.ShapeDtypeStruct((cols, count * leaf), dtype),
        compiler_params=pltpu.CompilerParams(vmem_limit_bytes=40 << 20),
        name=name,
    )(lst, *operands)


def down_kernel(dims, pos_ref, gathered, top_pick, ridge, dt, terms, top_hbm, local_hbm, leaf_hbm, out,
                tb, nb, lb, tcoeff, tskel, value, sems):
    count, leaf, rank, dim, cols, subtrees = dims
    get_top = pltpu.make_async_copy(top_hbm, tb, sems.at[0])
    get_local = pltpu.make_async_copy(local_hbm, nb, sems.at[1])
    get_leaf = pltpu.make_async_copy(leaf_hbm, lb, sems.at[2])
    get_top.start()
    get_local.start()
    get_leaf.start()
    pos = pos_ref[0]
    depth = subtrees.bit_length() - 1
    for s in range(subtrees):
        tcoeff[:, lanes(subtrees - 1 + s, rank)] = gathered[s, :cols]
        tskel[:, lanes(subtrees - 1 + s, rank)] = gathered[s, cols:]
    get_top.wait()
    for d in range(depth - 1, 0, -1):
        off = 2 ** (d + 1) - 1
        up = 2**d - 1

        def climb(m):
            start = (off + 2 * m) * rank
            if not isinstance(m, int):
                start = pl.multiple_of(start, rank)
            both = pl.ds(start, 2 * rank)
            c = dot(tcoeff[:, both], tb[up + m])
            sel = selector(top_pick[pl.ds(up + m, 1), :], 2 * rank)
            s = dot(tskel[:, both], sel)
            tcoeff[:, lanes(up + m, rank)] = c.astype(bf16)
            tskel[:, lanes(up + m, rank)] = s.astype(bf16)

        grouped(2**d, 4, climb)
    top_terms = {}
    for d in range(depth, 0, -1):
        mine = pos >> (depth - d)
        other = mine ^ 1
        half = lambda v: (v.astype(f32) * 0.5).astype(bf16)
        own_left = feature_pair(half(tskel[:, lanes(2**d - 1 + mine, rank)]))[0]
        sib_right = feature_pair(half(tskel[:, lanes(2**d - 1 + other, rank)]))[1]
        g = gauss(sib_right.T, own_left)
        top_terms[d] = dot(tcoeff[:, lanes(2**d - 1 + other, rank)], g)
    v = jnp.zeros((cols, rank), bf16)
    for d in range(1, depth + 1):
        parent = pos >> (depth - d + 1)
        down = dot(v, tb[2 ** (d - 1) - 1 + parent], 1, 1)
        right = ((pos >> (depth - d)) & 1) == 1
        v = (top_terms[d] + jnp.where(right, down[:, rank:], down[:, :rank])).astype(bf16)
    value[:, lanes(0, rank)] = v
    get_local.wait()
    local_depth = count.bit_length() - 1
    for d in range(1, local_depth + 1):
        up = 2 ** (d - 1) - 1

        def descend(m):
            down = dot(value[:, lanes(up + m, rank)], nb[up + m], 1, 1)
            start_t, start_v = (2**d - 2 + 2 * m) * rank, (2**d - 1 + 2 * m) * rank
            if not isinstance(m, int):
                start_t, start_v = pl.multiple_of(start_t, rank), pl.multiple_of(start_v, rank)
            value[:, pl.ds(start_v, 2 * rank)] = (terms[:, pl.ds(start_t, 2 * rank)] + down).astype(bf16)

        grouped(2 ** (d - 1), 4, descend)
    get_leaf.wait()
    scale = ridge[...]

    def finish(l):
        s = lanes(l, leaf)
        far = dot(value[:, lanes(count - 1 + l, rank)], lb[l], 1, 1)
        out[:, s] = scale * dt[:, s] + far

    grouped(count, 4, finish)


def downward(pos, gathered, top_pick, ridge, dt, terms, top_basis, local_basis, leaf_basis, dim):
    count, leaf, rank = leaf_basis.shape
    cols = dt.shape[0]
    subtrees = gathered.shape[0]
    vm = pl.BlockSpec(memory_space=pltpu.VMEM)
    hbm = pl.BlockSpec(memory_space=pl.ANY)
    return pl.pallas_call(
        functools.partial(down_kernel, (count, leaf, rank, dim, cols, subtrees)),
        grid_spec=pltpu.PrefetchScalarGridSpec(
            num_scalar_prefetch=1,
            grid=(1,),
            in_specs=[vm] * 5 + [hbm] * 3,
            out_specs=vm,
            scratch_shapes=[
                pltpu.VMEM(top_basis.shape, bf16),
                pltpu.VMEM(local_basis.shape, bf16),
                pltpu.VMEM(leaf_basis.shape, bf16),
                pltpu.VMEM((cols, (2 * subtrees - 1) * rank), bf16),
                pltpu.VMEM((dim, (2 * subtrees - 1) * rank), bf16),
                pltpu.VMEM((cols, (2 * count - 1) * rank), bf16),
                pltpu.SemaphoreType.DMA((3,)),
            ],
        ),
        out_shape=jax.ShapeDtypeStruct(dt.shape, f32),
        compiler_params=pltpu.CompilerParams(vmem_limit_bytes=48 << 20),
        name="downward",
    )(pos, gathered, top_pick, ridge, dt, terms, top_basis, local_basis, leaf_basis)


def class_list(ids, low, count):
    entries = ids.shape[0]
    local = ids - low
    inside = (local >= 0) & (local < count)
    ones = inside.astype(jnp.int32)
    row = [jnp.zeros_like(ones[0])]
    for e in range(entries):
        row.append(row[-1] + ones[e])
    out = []
    for k in range(entries):
        acc = jnp.zeros_like(ones[0])
        for e in range(k, entries):
            acc = acc + jnp.where(inside[e] & (row[e] == k), local[e], 0)
        out.append(acc)
    out.append(row[-1])
    return jnp.stack(out, 0)


def shards(points, direction, ridge, leaf_basis, local_basis, top_basis, leaf_pick, local_pick, top_pick, near_list):
    count, leaf, rank = leaf_basis.shape
    dim, cols = points.shape[1], direction.shape[1]
    entries = near_list.shape[1]
    chips = lax.axis_size("chip")
    subtrees = lax.axis_size("leaf") * chips
    pos = lax.axis_index("leaf") * chips + lax.axis_index("chip")
    upper = [(i, i + 1) for i in range(subtrees - 1)]
    lower = [(i + 1, i) for i in range(subtrees - 1)]

    xt, dt, ids = points.T, direction.T, near_list.T
    x_low = lax.ppermute(xt, AXES, upper)
    wt = dt.astype(bf16)
    list_up = class_list(ids, (pos + 1) * count, count)
    extra = jnp.pad(list_up.astype(bf16), ((0, cols - entries - 1), (0, 128 - count)))
    w_low_all = lax.ppermute(jnp.concatenate([wt, extra], 1), AXES, upper)
    list_own = class_list(ids, pos * count, count)
    list_low = class_list(ids, (pos - 1) * count, count)

    at, b, terms, root = upward(xt, wt, leaf_pick, local_pick, leaf_basis, local_basis)
    spread = jnp.broadcast_to(root[None], (subtrees,) + root.shape)
    gathered = lax.all_to_all(spread, AXES, 0, 0)
    call = functools.partial(near_call, count=count, entries=entries, leaf=leaf, cols=cols)
    near = call(near_own_kernel, list_own, (at, b, wt), dtype=f32, extra=[], name="near_own")

    w_low = w_low_all[:, : count * leaf]
    list_back = w_low_all[: entries + 1, count * leaf : count * leaf + count].astype(jnp.int32)
    back = call(
        near_back_kernel, list_back, (x_low, b, wt), dtype=bf16,
        extra=[pltpu.VMEM((count, FEAT, leaf), bf16)], name="near_back",
    )
    returned = lax.ppermute(back, AXES, lower)
    part = downward(
        pos[None], gathered, top_pick, ridge[:, None], dt, terms, top_basis, local_basis, leaf_basis, dim
    )
    out = call(
        near_low_kernel, list_low, (at, x_low, w_low, near, part), dtype=f32,
        extra=[pltpu.VMEM((count, leaf, FEAT), bf16)], name="near_low",
    )
    return (out + returned.astype(f32)).T


def solution(mesh):
    split = P(AXES, None)
    split3 = P(AXES, None, None)
    return jax.shard_map(
        shards,
        mesh=mesh,
        in_specs=(split, split, P(), split3, split3, P(), split, split, P(), split),
        out_specs=split,
        check_vma=False,
    )
```

time: 490 us -> 134 us (0.27)
  the two profiles are of different devices: /device:TPU:0 before, /device:TPU:31 now
where the time goes in v1:
time: 134 us; the launch traced here: 133 us
  Pallas kernels  96 us (72%)
  local copies, waits for them, and re-layouts  16.4 us (12%)
  starting transfers between devices  14.5 us (11%)
  other arithmetic  6.06 us (5%)
    pallas_call x3, Pallas kernels, near_call(): pl.pallas_call(functools.partial(kernel, count, entries), grid_spec=pltpu...  57.8 us
    pallas_call x1, Pallas kernels, upward(): pl.pallas_call(functools.partial(up_kernel, (count, leaf, rank, dim, cols...  22.6 us
    pallas_call x1, Pallas kernels, downward(): pl.pallas_call(functools.partial(down_kernel, (count, leaf, rank, dim, co...  15.6 us
    unnamed x30, local copies, waits for them, and re-layouts  14.2 us
    all_to_all x1, starting transfers between devices, shards(): gathered = lax.all_to_all(spread, AXES, 0, 0)  8.06 us
    ppermute x1, starting transfers between devices, shards(): returned = lax.ppermute(back, AXES, lower)  3.89 us
  transfers between devices with their start and end apart: 4, of which 0 were waited for; matrix products, arithmetic and copies ran while one was open for 2% of the time, Pallas kernels for 72%

profile of v1, /device:TPU:31, one launch (start us, length us, event | category | flops | bytes accessed | tf_op | source)
XLA Modules:
  0.0 133.3 jit_solution(13458082081715483698)
XLA Ops:
  0.0 0.7 fusion.148
  0.9 1.3 bitcast_convert_fusion.wt.w
  2.2 0.1 stack.8
  2.3 0.8 fusion.1
  3.1 1.3 collective-permute-start.1
  4.4 1.3 collective-permute-start
  5.7 0.0 copy-start.7
  5.7 1.6 %copy-done.7 = bf16[16384,64]{0,1:T(8,128)(2,1)S(1)} copy-done((bf16[16384,64]{0,1:T(8,128)(2,1)S(1)}, bf16[16384,64]{0,1:T(8,128)(2,1)}, u32[]{:S(2)}) %copy-start.7) | copy-done | bytes 2097176
  7.3 22.6 %upward.1 = (bf16[64,128,256]{2,1,0:T(8,128)(2,1)}, bf16[64,256,128]{2,1,0:T(8,128)(2,1)}, f32[16,16128]{1,0:T(8,128)S(1)}, bf16[80,128]{1,0:T(8,128)(2,1)S(1)}) custom-call(bf16[64,16384]{1,0:T(8,128)(2,1)S(1)} %bitcast.18, bf16[16,16384]{1,0:T(8,128)(2,1)S(1)} %bitcast_convert_fusion.wt.w, s32[64,128]{1,0:T(8,128)S(1)} %copy-done.11, ...), custom_call_target="tpu_custom_call" | custom-call | tf_op jit(solution)/shard_map/upward/pallas_call | solution.py:138
  30.0 1.0 copy-done.9
  31.0 0.9 broadcast_in_dim.182
  31.9 8.1 %all-to-all-start = ((bf16[32,80,128]{2,1,0:T(8,128)(2,1)}), bf16[32,80,128]{2,1,0:T(8,128)(2,1)S(1)}, u32[]{:S(2)}, u32[]{:S(2)}) async-start(bf16[32,80,128]{2,1,0:T(8,128)(2,1)} %broadcast_in_dim.182), calls=%async_computation | async-start | bytes 1310720 | tf_op jit(solution)/shard_map/all_to_all | solution.py:402
  40.3 0.0 collective-permute-done.1
  40.3 0.7 slice_convert_fusion.lst
  41.0 0.0 collective-permute-done.xlow
  41.0 2.2 %copy-done.2 = bf16[64,256,128]{2,1,0:T(8,128)(2,1)S(1)} copy-done((bf16[64,256,128]{2,1,0:T(8,128)(2,1)S(1)}, bf16[64,256,128]{2,1,0:T(8,128)(2,1)}, u32[]{:S(2)}) %copy-start.2) | copy-done | bytes 4194328
  43.2 15.3 %near_back.1 = bf16[16,16384]{1,0:T(8,128)(2,1)} custom-call(s32[11,64]{1,0:T(8,128)S(1)} %slice_convert_fusion.lst, bf16[64,16384]{1,0:T(8,128)(2,1)S(1)} %collective-permute-done.xlow, bf16[64,256,128]{2,1,0:T(8,128)(2,1)S(1)} %copy-done.2, bf16[16,16384]{1,0:T(8,128)(2,1)S(1)} %bitcast_convert_fusion.wt.w), custom_call_target="tpu_custom_call" | custom-call | tf_op jit(solution)/shard_map/near_back/pallas_call | solution.py:248
  58.5 3.9 %collective-permute-start.2 = (bf16[16,16384]{1,0:T(8,128)(2,1)}, bf16[16,16384]{1,0:T(8,128)(2,1)}, u32[]{:S(2)}, u32[]{:S(2)}) collective-permute-start(bf16[16,16384]{1,0:T(8,128)(2,1)} %near_back.1), channel_id=1, source_target_pairs={{1,0},{2,1},{3,2},{4,3},{5,4},{6,5},{7,6},{8,7},{9,8},{10,9},{11,1... | collective-permute-start | bytes 1572872 | tf_op jit(solution)/shard_map/ppermute | solution.py:412
  62.4 0.1 copy.11.ridge
  62.5 2.2 %copy-done = bf16[64,128,256]{2,1,0:T(8,128)(2,1)S(1)} copy-done((bf16[64,128,256]{2,1,0:T(8,128)(2,1)S(1)}, bf16[64,128,256]{2,1,0:T(8,128)(2,1)}, u32[]{:S(2)}) %copy-start) | copy-done | bytes 4194328
  64.7 2.2 %copy-done.3 = bf16[64,256,128]{2,1,0:T(8,128)(2,1)S(1)} copy-done((bf16[64,256,128]{2,1,0:T(8,128)(2,1)S(1)}, bf16[64,256,128]{2,1,0:T(8,128)(2,1)}, u32[]{:S(2)}) %copy-start.3) | copy-done | bytes 4194328
  66.9 26.4 %near_own.1.add1 = f32[16,16384]{1,0:T(8,128)S(1)} custom-call(s32[11,64]{1,0:T(8,128)S(1)} %stack.9.lst, bf16[64,128,256]{2,1,0:T(8,128)(2,1)S(1)} %copy-done, bf16[64,256,128]{2,1,0:T(8,128)(2,1)S(1)} %copy-done.3, bf16[16,16384]{1,0:T(8,128)(2,1)S(1)} %bitcast_convert_fusion.wt.w), custom_call_target="tpu_custom_call" | custom-call | tf_op jit(solution)/shard_map/near_own/pallas_call | solution.py:248
  93.3 0.0 copy-start.5
  93.3 1.0 copy-done.5
  94.4 1.1 slice.336.w
  95.5 0.0 copy-start.4
  95.5 1.2 copy-done.4
  96.7 1.6 %copy-done.8 = bf16[31,256,128]{2,1,0:T(8,128)(2,1)S(1)} copy-done((bf16[31,256,128]{2,1,0:T(8,128)(2,1)S(1)}, bf16[31,256,128]{2,1,0:T(8,128)(2,1)}, u32[]{:S(2)}) %copy-start.8) | copy-done | bytes 2031640
  98.3 1.2 copy-done.10
  99.5 15.6 %downward.1.add2 = f32[16,16384]{1,0:T(8,128)S(1)} custom-call(s32[1]{0:T(128)} %bitcast.5.pos_ref, bf16[32,80,128]{2,1,0:T(8,128)(2,1)S(1)} %all-to-all-done.gathered, s32[31,128]{1,0:T(8,128)S(1)} %copy-done.13, f32[16,1]{1,0:T(8,128)S(1)} %copy.11.ridge, f32[16,16384]{1,0:T(8,128)S(1)} %bitcast.16, f32[16,16128]{1,0:T(8,128)S(1)} %copy-done.10, ...), custom_call_target="tpu_custom_call" | custom-call | tf_op jit(solution)/shard_map/downward/pallas_call | solution.py:340
  115.1 16.1 %near_low.1 = f32[16,16384]{1,0:T(8,128)S(1)} custom-call(s32[11,64]{1,0:T(8,128)S(1)} %stack.7.lst, bf16[64,128,256]{2,1,0:T(8,128)(2,1)S(1)} %copy-done.1, bf16[64,16384]{1,0:T(8,128)(2,1)S(1)} %collective-permute-done.xlow, bf16[16,16384]{1,0:T(8,128)(2,1)S(1)} %slice.336.w, f32[16,16384]{1,0:T(8,128)S(1)} %copy-done.6, f32[16,16384]{1,0:T(8,128)S(1)} %downward.1.add2), custom_call_target="tpu_custom_call" | custom-call | tf_op jit(solution)/shard_map/near_low/pallas_call | solution.py:248
  131.2 2.1 %add_bitcast_fusion = f32[16384,16]{0,1:T(8,128)} fusion(f32[16,16384]{1,0:T(8,128)S(1)} %near_low.1, bf16[16,16384]{1,0:T(8,128)(2,1)} %collective-permute-done.2), kind=kLoop, calls=%fused_computation.2 | loop fusion | flops 524288 | bytes 2621440 | tf_op jit(solution)/shard_map/transpose | solution.py:420
  (48 shorter events, 0.6 us)
Async XLA Ops:
  0.0 5.7 %copy-start.12 = (s32[63,128]{1,0:T(8,128)S(1)}, s32[63,128]{1,0:T(8,128)}, u32[]{:S(2)}) copy-start(s32[63,128]{1,0:T(8,128)} %local_pick.1) | copy-start | bytes 96772
  0.0 5.7 %copy-start.11 = (s32[64,128]{1,0:T(8,128)S(1)}, s32[64,128]{1,0:T(8,128)}, u32[]{:S(2)}) copy-start(s32[64,128]{1,0:T(8,128)} %leaf_pick.1) | copy-start | bytes 98308
  3.1 37.2 %collective-permute-start.1 = (bf16[16,16512]{1,0:T(8,128)(2,1)}, bf16[16,16512]{1,0:T(8,128)(2,1)}, u32[]{:S(2)}, u32[]{:S(2)}) collective-permute-start(bf16[16,16512]{1,0:T(8,128)(2,1)} %fusion.1), channel_id=1, source_target_pairs={{0,1},{1,2},{2,3},{3,4},{4,5},{5,6},{6,7},{7,8},{8,9},{9,10},{10,1... | collective-permute-start | bytes 1585160 | tf_op jit(solution)/shard_map/ppermute | solution.py:396
  4.4 36.6 %collective-permute-start = (bf16[64,16384]{1,0:T(8,128)(2,1)}, bf16[64,16384]{1,0:T(8,128)(2,1)S(1)}, u32[]{:S(2)}, u32[]{:S(2)}) collective-permute-start(bf16[64,16384]{1,0:T(8,128)(2,1)} %bitcast.17), channel_id=1, source_target_pairs={{0,1},{1,2},{2,3},{3,4},{4,5},{5,6},{6,7},{7,8},{8,9},{9,10},{10,1... | collective-permute-start | bytes 6291464 | tf_op jit(solution)/shard_map/ppermute | solution.py:392
  5.7 1.6 %copy-start.7 = (bf16[16384,64]{0,1:T(8,128)(2,1)S(1)}, bf16[16384,64]{0,1:T(8,128)(2,1)}, u32[]{:S(2)}) copy-start(bf16[16384,64]{0,1:T(8,128)(2,1)} %param.10) | copy-start | bytes 6291460
  30.0 1.0 copy-start.9
  31.9 63.5 %all-to-all-start = ((bf16[32,80,128]{2,1,0:T(8,128)(2,1)}), bf16[32,80,128]{2,1,0:T(8,128)(2,1)S(1)}, u32[]{:S(2)}, u32[]{:S(2)}) async-start(bf16[32,80,128]{2,1,0:T(8,128)(2,1)} %broadcast_in_dim.182), calls=%async_computation | async-start | bytes 1310720 | tf_op jit(solution)/shard_map/all_to_all | solution.py:402
  41.0 2.2 %copy-start.2 = (bf16[64,256,128]{2,1,0:T(8,128)(2,1)S(1)}, bf16[64,256,128]{2,1,0:T(8,128)(2,1)}, u32[]{:S(2)}) copy-start(bf16[64,256,128]{2,1,0:T(8,128)(2,1)} %get-tuple-element.10.b) | copy-start | bytes 12582916
  43.2 19.2 %copy-start.14 = (f32[16]{0:T(128)S(1)}, f32[16]{0:T(128)}, u32[]{:S(2)}) copy-start(f32[16]{0:T(128)} %param.12) | copy-start | bytes 196
  58.5 72.7 %collective-permute-start.2 = (bf16[16,16384]{1,0:T(8,128)(2,1)}, bf16[16,16384]{1,0:T(8,128)(2,1)}, u32[]{:S(2)}, u32[]{:S(2)}) collective-permute-start(bf16[16,16384]{1,0:T(8,128)(2,1)} %near_back.1), channel_id=1, source_target_pairs={{1,0},{2,1},{3,2},{4,3},{5,4},{6,5},{7,6},{8,7},{9,8},{10,9},{11,1... | collective-permute-start | bytes 1572872 | tf_op jit(solution)/shard_map/ppermute | solution.py:412
  62.5 2.2 %copy-start = (bf16[64,128,256]{2,1,0:T(8,128)(2,1)S(1)}, bf16[64,128,256]{2,1,0:T(8,128)(2,1)}, u32[]{:S(2)}) copy-start(bf16[64,128,256]{2,1,0:T(8,128)(2,1)} %get-tuple-element.9.at) | copy-start | bytes 12582916
  64.7 2.2 %copy-start.3 = (bf16[64,256,128]{2,1,0:T(8,128)(2,1)S(1)}, bf16[64,256,128]{2,1,0:T(8,128)(2,1)}, u32[]{:S(2)}) copy-start(bf16[64,256,128]{2,1,0:T(8,128)(2,1)} %get-tuple-element.10.b) | copy-start | bytes 12582916
  66.9 28.6 %copy-start.13 = (s32[31,128]{1,0:T(8,128)S(1)}, s32[31,128]{1,0:T(8,128)}, u32[]{:S(2)}) copy-start(s32[31,128]{1,0:T(8,128)} %top_pick.1) | copy-start | bytes 47620
  93.3 1.0 copy-start.5
  95.5 1.2 copy-start.4
  96.7 1.6 %copy-start.8 = (bf16[31,256,128]{2,1,0:T(8,128)(2,1)S(1)}, bf16[31,256,128]{2,1,0:T(8,128)(2,1)}, u32[]{:S(2)}) copy-start(bf16[31,256,128]{2,1,0:T(8,128)(2,1)} %top_hbm.1) | copy-start | bytes 6094852
  98.3 1.2 copy-start.10
  99.5 15.6 %copy-start.1 = (bf16[64,128,256]{2,1,0:T(8,128)(2,1)S(1)}, bf16[64,128,256]{2,1,0:T(8,128)(2,1)}, u32[]{:S(2)}) copy-start(bf16[64,128,256]{2,1,0:T(8,128)(2,1)} %get-tuple-element.9.at) | copy-start | bytes 12582916
  99.5 15.6 %copy-start.6 = (f32[16,16384]{1,0:T(8,128)S(1)}, f32[16,16384]{1,0:T(8,128)}, u32[]{:S(2)}) copy-start(f32[16,16384]{1,0:T(8,128)} %copy-done.5) | copy-start | bytes 3145732

commit v2 on v1

--- a/solution.py
+++ b/solution.py
@@ -58,12 +58,13 @@
     return jnp.exp2(s * SCALE).astype(bf16)
 
 
-def grouped(count, group, fn):
+def grouped(count, group, compute, store):
     group = min(group, count)
 
     def body(t, carry):
+        got = [compute(t * group + u) for u in range(group)]
         for u in range(group):
-            fn(t * group + u)
+            store(t * group + u, got[u])
         return carry
 
     if count == group:
@@ -72,10 +73,10 @@
         lax.fori_loop(0, count // group, body, 0)
 
 
-def lanes(start, width):
+def lanes(start, width, number=1):
     if isinstance(start, int):
-        return pl.ds(start * width, width)
-    return pl.ds(pl.multiple_of(start * width, width), width)
+        return pl.ds(start * width, number * width)
+    return pl.ds(pl.multiple_of(start * width, width), number * width)
 
 
 def up_kernel(dims, xt, wt, leaf_pick, local_pick, leaf_hbm, local_hbm, at, b, terms, root, lb, nb, coeff, skel, sems):
@@ -87,20 +88,24 @@
 
     def prepare(l):
         left, right = feature_pair(xt[:, lanes(l, leaf)])
-        at[l] = left
-        b[l] = right.T
-
-    grouped(count, 4, prepare)
+        return left, right.T
+
+    def keep(l, got):
+        at[l], b[l] = got
+
+    grouped(count, 4, prepare, keep)
     get_leaf.wait()
     base = count - 1
 
     def leaf_step(l):
         c = dot(wt[:, lanes(l, leaf)], lb[l])
-        coeff[:, lanes(base + l, rank)] = c.astype(bf16)
         sel = selector(leaf_pick[pl.ds(l, 1), :], leaf)
-        skel[:, lanes(base + l, rank)] = dot(at[l], sel).astype(bf16)
-
-    grouped(count, 4, leaf_step)
+        return c.astype(bf16), dot(at[l], sel).astype(bf16)
+
+    def leaf_keep(l, got):
+        coeff[:, lanes(base + l, rank)], skel[:, lanes(base + l, rank)] = got
+
+    grouped(count, 8, leaf_step, leaf_keep)
     get_local.wait()
     depth = count.bit_length() - 1
     for d in range(depth, 0, -1):
@@ -108,24 +113,25 @@
         up = 2 ** (d - 1) - 1
 
         def pair_step(m):
-            both = pl.ds((off + 2 * m) * rank, 2 * rank)
-            if not isinstance(m, int):
-                both = pl.ds(pl.multiple_of((off + 2 * m) * rank, rank), 2 * rank)
+            both = lanes(off + 2 * m, rank, 2)
             c2 = coeff[:, both]
             s2 = skel[:, both]
             left, right = s2[:, :rank], s2[:, rank:]
             c = dot(c2, nb[up + m])
             sel = selector(local_pick[pl.ds(up + m, 1), :], 2 * rank)
             s = dot(s2, sel)
-            coeff[:, lanes(up + m, rank)] = c.astype(bf16)
-            skel[:, lanes(up + m, rank)] = s.astype(bf16)
             g = gauss(swap_form(right, dim).T, left)
             term_left = dot(c2[:, rank:], g)
             term_right = dot(c2[:, :rank], g, 1, 1)
-            terms[:, lanes(2**d - 2 + 2 * m, rank)] = term_left
-            terms[:, lanes(2**d - 1 + 2 * m, rank)] = term_right
-
-        grouped(2 ** (d - 1), 4, pair_step)
+            return c.astype(bf16), s.astype(bf16), term_left, term_right
+
+        def pair_keep(m, got):
+            coeff[:, lanes(up + m, rank)] = got[0]
+            skel[:, lanes(up + m, rank)] = got[1]
+            terms[:, lanes(2**d - 2 + 2 * m, rank)] = got[2]
+            terms[:, lanes(2**d - 1 + 2 * m, rank)] = got[3]
+
+        grouped(2 ** (d - 1), 8, pair_step, pair_keep)
     root[:cols, :] = coeff[:, :rank]
     root[cols:, :] = skel[:dim, :rank]
 
@@ -152,7 +158,7 @@
             pltpu.VMEM((FEAT, (2 * count - 1) * rank), bf16),
             pltpu.SemaphoreType.DMA((2,)),
         ],
-        compiler_params=pltpu.CompilerParams(vmem_limit_bytes=48 << 20),
+        compiler_params=pltpu.CompilerParams(vmem_limit_bytes=32 << 20),
         name="upward",
     )(xt, wt, leaf_pick, local_pick, leaf_basis, local_basis)
 
@@ -210,37 +216,42 @@
     ]
 
 
+def write_out(out, acc, count, leaf, *more):
+    def compute(l):
+        return functools.reduce(lambda x, y: x + y[:, lanes(l, leaf)], more, acc[l])
+
+    def store(l, got):
+        out[:, lanes(l, leaf)] = got.astype(out.dtype)
+
+    grouped(count, 4, compute, store)
+
+
 def near_own_kernel(count, entries, lst, at, b, w, out, pair, acc, tiles):
     near_pairs(count, entries, lst, pair, at, b, w, acc, tiles)
     leaf = b.shape[1]
-    grouped(count, 4, lambda l: out.__setitem__((slice(None), lanes(l, leaf)), acc[l]))
+    write_out(out, acc, count, leaf)
 
 
 def near_back_kernel(count, entries, lst, xlow, b, w, out, pair, acc, tiles, at):
     leaf = b.shape[1]
 
-    def prepare(l):
-        at[l] = feature_pair(xlow[:, lanes(l, leaf)])[0]
-
-    grouped(count, 4, prepare)
+    def keep(l, got):
+        at[l] = got
+
+    grouped(count, 4, lambda l: feature_pair(xlow[:, lanes(l, leaf)])[0], keep)
     near_pairs(count, entries, lst, pair, at, b, w, acc, tiles)
-    grouped(count, 4, lambda l: out.__setitem__((slice(None), lanes(l, leaf)), acc[l].astype(bf16)))
+    write_out(out, acc, count, leaf)
 
 
 def near_low_kernel(count, entries, lst, at, xlow, w, add1, add2, out, pair, acc, tiles, b):
     leaf = at.shape[2]
 
-    def prepare(l):
-        b[l] = feature_pair(xlow[:, lanes(l, leaf)])[1].T
-
-    grouped(count, 4, prepare)
+    def keep(l, got):
+        b[l] = got
+
+    grouped(count, 4, lambda l: feature_pair(xlow[:, lanes(l, leaf)])[1].T, keep)
     near_pairs(count, entries, lst, pair, at, b, w, acc, tiles)
-
-    def finish(l):
-        s = lanes(l, leaf)
-        out[:, s] = acc[l] + add1[:, s] + add2[:, s]
-
-    grouped(count, 4, finish)
+    write_out(out, acc, count, leaf, add1, add2)
 
 
 def near_call(kernel, lst, operands, count, entries, leaf, cols, dtype, extra, name):
@@ -255,7 +266,7 @@
             scratch_shapes=near_scratch(count, entries, leaf, cols) + extra,
         ),
         out_shape=jax.ShapeDtypeStruct((cols, count * leaf), dtype),
-        compiler_params=pltpu.CompilerParams(vmem_limit_bytes=40 << 20),
+        compiler_params=pltpu.CompilerParams(vmem_limit_bytes=24 << 20),
         name=name,
     )(lst, *operands)
 
@@ -280,17 +291,16 @@
         up = 2**d - 1
 
         def climb(m):
-            start = (off + 2 * m) * rank
-            if not isinstance(m, int):
-                start = pl.multiple_of(start, rank)
-            both = pl.ds(start, 2 * rank)
+            both = lanes(off + 2 * m, rank, 2)
             c = dot(tcoeff[:, both], tb[up + m])
             sel = selector(top_pick[pl.ds(up + m, 1), :], 2 * rank)
             s = dot(tskel[:, both], sel)
-            tcoeff[:, lanes(up + m, rank)] = c.astype(bf16)
-            tskel[:, lanes(up + m, rank)] = s.astype(bf16)
-
-        grouped(2**d, 4, climb)
+            return c.astype(bf16), s.astype(bf16)
+
+        def climb_keep(m, got):
+            tcoeff[:, lanes(up + m, rank)], tskel[:, lanes(up + m, rank)] = got
+
+        grouped(2**d, 8, climb, climb_keep)
     top_terms = {}
     for d in range(depth, 0, -1):
         mine = pos >> (depth - d)
@@ -314,21 +324,23 @@
 
         def descend(m):
             down = dot(value[:, lanes(up + m, rank)], nb[up + m], 1, 1)
-            start_t, start_v = (2**d - 2 + 2 * m) * rank, (2**d - 1 + 2 * m) * rank
-            if not isinstance(m, int):
-                start_t, start_v = pl.multiple_of(start_t, rank), pl.multiple_of(start_v, rank)
-            value[:, pl.ds(start_v, 2 * rank)] = (terms[:, pl.ds(start_t, 2 * rank)] + down).astype(bf16)
-
-        grouped(2 ** (d - 1), 4, descend)
+            return (terms[:, lanes(2**d - 2 + 2 * m, rank, 2)] + down).astype(bf16)
+
+        def descend_keep(m, got):
+            value[:, lanes(2**d - 1 + 2 * m, rank, 2)] = got
+
+        grouped(2 ** (d - 1), 8, descend, descend_keep)
     get_leaf.wait()
     scale = ridge[...]
 
     def finish(l):
-        s = lanes(l, leaf)
         far = dot(value[:, lanes(count - 1 + l, rank)], lb[l], 1, 1)
-        out[:, s] = scale * dt[:, s] + far
-
-    grouped(count, 4, finish)
+        return scale * dt[:, lanes(l, leaf)] + far
+
+    def finish_keep(l, got):
+        out[:, lanes(l, leaf)] = got
+
+    grouped(count, 8, finish, finish_keep)
 
 
 def downward(pos, gathered, top_pick, ridge, dt, terms, top_basis, local_basis, leaf_basis, dim):
@@ -355,7 +367,7 @@
             ],
         ),
         out_shape=jax.ShapeDtypeStruct(dt.shape, f32),
-        compiler_params=pltpu.CompilerParams(vmem_limit_bytes=48 << 20),
+        compiler_params=pltpu.CompilerParams(vmem_limit_bytes=24 << 20),
         name="downward",
     )(pos, gathered, top_pick, ridge, dt, terms, top_basis, local_basis, leaf_basis)
 

time: 134 us -> 135 us (level)
  Pallas kernels: 96 us -> 83.2 us
  local copies, waits for them, and re-layouts: 16.4 us -> 29.1 us
    unnamed x30 -> x42, local copies, waits for them, and re-layouts: 14.2 us -> 26.8 us
    pallas_call x1, Pallas kernels: 15.6 us -> 7.5 us  [downward(): pl.pallas_call(functools.partial(down_kernel, (count, leaf, rank, dim, co...]
    pallas_call x1, Pallas kernels: 22.6 us -> 18.8 us  [upward(): pl.pallas_call(functools.partial(up_kernel, (count, leaf, rank, dim, cols...]
  transfers between devices with their start and end apart: 4 -> 4, of which waited for: 0 -> 0; matrix products, arithmetic and copies ran while one was open for 2% -> 2% of each run, Pallas kernels for 72% -> 62%
where the time goes in v2:
time: 135 us; the launch traced here: 134 us
  Pallas kernels  83.2 us (62%)
  local copies, waits for them, and re-layouts  29.1 us (22%)
  starting transfers between devices  15.4 us (11%)
  other arithmetic  6.06 us (4%)
    pallas_call x3, Pallas kernels, near_call(): pl.pallas_call(functools.partial(kernel, count, entries), grid_spec=pltpu...  56.9 us
    unnamed x42, local copies, waits for them, and re-layouts  26.8 us
    pallas_call x1, Pallas kernels, upward(): pl.pallas_call(functools.partial(up_kernel, (count, leaf, rank, dim, cols...  18.8 us
    all_to_all x1, starting transfers between devices, shards(): gathered = lax.all_to_all(spread, AXES, 0, 0)  8.07 us
    pallas_call x1, Pallas kernels, downward(): pl.pallas_call(functools.partial(down_kernel, (count, leaf, rank, dim, co...  7.5 us
    ppermute x1, starting transfers between devices, shards(): returned = lax.ppermute(back, AXES, lower)  4.76 us
  transfers between devices with their start and end apart: 4, of which 0 were waited for; matrix products, arithmetic and copies ran while one was open for 2% of the time, Pallas kernels for 62%

profile of v2, /device:TPU:31, one launch (start us, length us, event | category | flops | bytes accessed | tf_op | source)
XLA Modules:
  0.0 134.0 jit_solution(14924891018315634439)
XLA Ops:
  0.0 0.7 fusion.148
  0.9 1.3 bitcast_convert_fusion.wt.w
  2.3 0.8 fusion.1
  3.1 1.3 collective-permute-start.1
  4.4 1.3 collective-permute-start
  5.7 2.2 %copy-done.6 = bf16[64,256,128]{2,1,0:T(8,128)(2,1)S(1)} copy-done((bf16[64,256,128]{2,1,0:T(8,128)(2,1)S(1)}, bf16[64,256,128]{2,1,0:T(8,128)(2,1)}, u32[]{:S(2)}) %copy-start.6) | copy-done | bytes 4194328
  7.9 2.2 %copy-done.8 = bf16[63,256,128]{2,1,0:T(8,128)(2,1)S(1)} copy-done((bf16[63,256,128]{2,1,0:T(8,128)(2,1)S(1)}, bf16[63,256,128]{2,1,0:T(8,128)(2,1)}, u32[]{:S(2)}) %copy-start.8) | copy-done | bytes 4128792
  10.1 1.6 %copy-done.13 = bf16[16384,64]{0,1:T(8,128)(2,1)S(1)} copy-done((bf16[16384,64]{0,1:T(8,128)(2,1)S(1)}, bf16[16384,64]{0,1:T(8,128)(2,1)}, u32[]{:S(2)}) %copy-start.13) | copy-done | bytes 2097176
  11.7 18.8 %upward.1 = (bf16[64,128,256]{2,1,0:T(8,128)(2,1)S(1)}, bf16[64,256,128]{2,1,0:T(8,128)(2,1)S(1)}, f32[16,16128]{1,0:T(8,128)S(1)}, bf16[80,128]{1,0:T(8,128)(2,1)S(1)}) custom-call(bf16[64,16384]{1,0:T(8,128)(2,1)S(1)} %bitcast.18, bf16[16,16384]{1,0:T(8,128)(2,1)S(1)} %bitcast_convert_fusion.wt.w, s32[64,128]{1,0:T(8,128)S(1)} %copy-done.17, ...), custom_call_target="tpu_custom_call" | custom-call | tf_op jit(solution)/shard_map/upward/pallas_call | solution.py:144
  30.5 2.0 %copy-done = bf16[64,128,256]{2,1,0:T(8,128)(2,1)} copy-done((bf16[64,128,256]{2,1,0:T(8,128)(2,1)}, bf16[64,128,256]{2,1,0:T(8,128)(2,1)S(1)}, u32[]{:S(2)}) %copy-start) | copy-done | bytes 4194328
  32.4 2.0 %copy-done.3 = bf16[64,256,128]{2,1,0:T(8,128)(2,1)} copy-done((bf16[64,256,128]{2,1,0:T(8,128)(2,1)}, bf16[64,256,128]{2,1,0:T(8,128)(2,1)S(1)}, u32[]{:S(2)}) %copy-start.3) | copy-done | bytes 4194328
  34.4 1.0 copy-done.15
  35.5 0.9 broadcast_in_dim.182
  36.4 8.1 %all-to-all-start = ((bf16[32,80,128]{2,1,0:T(8,128)(2,1)}), bf16[32,80,128]{2,1,0:T(8,128)(2,1)S(1)}, u32[]{:S(2)}, u32[]{:S(2)}) async-start(bf16[32,80,128]{2,1,0:T(8,128)(2,1)} %broadcast_in_dim.182), calls=%async_computation | async-start | bytes 1310720 | tf_op jit(solution)/shard_map/all_to_all | solution.py:414
  44.8 0.7 slice_convert_fusion.lst
  45.5 2.2 %copy-done.4 = bf16[64,256,128]{2,1,0:T(8,128)(2,1)S(1)} copy-done((bf16[64,256,128]{2,1,0:T(8,128)(2,1)S(1)}, bf16[64,256,128]{2,1,0:T(8,128)(2,1)}, u32[]{:S(2)}) %copy-start.4) | copy-done | bytes 4194328
  47.6 14.4 %near_back.1 = bf16[16,16384]{1,0:T(8,128)(2,1)} custom-call(s32[11,64]{1,0:T(8,128)S(1)} %slice_convert_fusion.lst, bf16[64,16384]{1,0:T(8,128)(2,1)S(1)} %collective-permute-done.xlow, bf16[64,256,128]{2,1,0:T(8,128)(2,1)S(1)} %copy-done.4, bf16[16,16384]{1,0:T(8,128)(2,1)S(1)} %bitcast_convert_fusion.wt.w), custom_call_target="tpu_custom_call" | custom-call | tf_op jit(solution)/shard_map/near_back/pallas_call | solution.py:259
  62.1 4.8 %collective-permute-start.2 = (bf16[16,16384]{1,0:T(8,128)(2,1)}, bf16[16,16384]{1,0:T(8,128)(2,1)}, u32[]{:S(2)}, u32[]{:S(2)}) collective-permute-start(bf16[16,16384]{1,0:T(8,128)(2,1)} %near_back.1), channel_id=1, source_target_pairs={{1,0},{2,1},{3,2},{4,3},{5,4},{6,5},{7,6},{8,7},{9,8},{10,9},{11,1... | collective-permute-start | bytes 1572872 | tf_op jit(solution)/shard_map/ppermute | solution.py:424
  66.8 0.1 copy.11.ridge
  67.0 2.2 %copy-done.1 = bf16[64,128,256]{2,1,0:T(8,128)(2,1)S(1)} copy-done((bf16[64,128,256]{2,1,0:T(8,128)(2,1)S(1)}, bf16[64,128,256]{2,1,0:T(8,128)(2,1)}, u32[]{:S(2)}) %copy-start.1) | copy-done | bytes 4194328
  69.2 2.2 %copy-done.5 = bf16[64,256,128]{2,1,0:T(8,128)(2,1)S(1)} copy-done((bf16[64,256,128]{2,1,0:T(8,128)(2,1)S(1)}, bf16[64,256,128]{2,1,0:T(8,128)(2,1)}, u32[]{:S(2)}) %copy-start.5) | copy-done | bytes 4194328
  71.3 27.3 %near_own.1.add1 = f32[16,16384]{1,0:T(8,128)S(1)} custom-call(s32[11,64]{1,0:T(8,128)S(1)} %stack.9.lst, bf16[64,128,256]{2,1,0:T(8,128)(2,1)S(1)} %copy-done.1, bf16[64,256,128]{2,1,0:T(8,128)(2,1)S(1)} %copy-done.5, bf16[16,16384]{1,0:T(8,128)(2,1)S(1)} %bitcast_convert_fusion.wt.w), custom_call_target="tpu_custom_call" | custom-call | tf_op jit(solution)/shard_map/near_own/pallas_call | solution.py:259
  98.6 1.0 copy-done.11
  99.7 1.1 slice.336.w
  100.8 2.2 %copy-done.7 = bf16[64,256,128]{2,1,0:T(8,128)(2,1)S(1)} copy-done((bf16[64,256,128]{2,1,0:T(8,128)(2,1)S(1)}, bf16[64,256,128]{2,1,0:T(8,128)(2,1)}, u32[]{:S(2)}) %copy-start.7) | copy-done | bytes 4194328
  103.0 2.2 %copy-done.9 = bf16[63,256,128]{2,1,0:T(8,128)(2,1)S(1)} copy-done((bf16[63,256,128]{2,1,0:T(8,128)(2,1)S(1)}, bf16[63,256,128]{2,1,0:T(8,128)(2,1)}, u32[]{:S(2)}) %copy-start.9) | copy-done | bytes 4128792
  105.2 1.2 copy-done.10
  106.4 1.6 %copy-done.14 = bf16[31,256,128]{2,1,0:T(8,128)(2,1)S(1)} copy-done((bf16[31,256,128]{2,1,0:T(8,128)(2,1)S(1)}, bf16[31,256,128]{2,1,0:T(8,128)(2,1)}, u32[]{:S(2)}) %copy-start.14) | copy-done | bytes 2031640
  108.0 1.2 copy-done.16
  109.2 7.5 %downward.1.add2 = f32[16,16384]{1,0:T(8,128)S(1)} custom-call(s32[1]{0:T(128)} %bitcast.5.pos_ref, bf16[32,80,128]{2,1,0:T(8,128)(2,1)S(1)} %all-to-all-done.gathered, s32[31,128]{1,0:T(8,128)S(1)} %copy-done.19, f32[16,1]{1,0:T(8,128)S(1)} %copy.11.ridge, f32[16,16384]{1,0:T(8,128)S(1)} %bitcast.16, f32[16,16128]{1,0:T(8,128)S(1)} %copy-done.16, ...), custom_call_target="tpu_custom_call" | custom-call | tf_op jit(solution)/shard_map/downward/pallas_call | solution.py:352
  116.7 15.2 %near_low.1 = f32[16,16384]{1,0:T(8,128)S(1)} custom-call(s32[11,64]{1,0:T(8,128)S(1)} %stack.7.lst, bf16[64,128,256]{2,1,0:T(8,128)(2,1)S(1)} %copy-done.2, bf16[64,16384]{1,0:T(8,128)(2,1)S(1)} %collective-permute-done.xlow, bf16[16,16384]{1,0:T(8,128)(2,1)S(1)} %slice.336.w, f32[16,16384]{1,0:T(8,128)S(1)} %copy-done.12, f32[16,16384]{1,0:T(8,128)S(1)} %downward.1.add2), custom_call_target="tpu_custom_call" | custom-call | tf_op jit(solution)/shard_map/near_low/pallas_call | solution.py:259
  131.9 2.1 %add_bitcast_fusion = f32[16384,16]{0,1:T(8,128)} fusion(f32[16,16384]{1,0:T(8,128)S(1)} %near_low.1, bf16[16,16384]{1,0:T(8,128)(2,1)} %collective-permute-done.2), kind=kLoop, calls=%fused_computation.2 | loop fusion | flops 524288 | bytes 2621440 | tf_op jit(solution)/shard_map/transpose | solution.py:432
  (60 shorter events, 0.7 us)
Async XLA Ops:
  0.0 5.7 %copy-start.18 = (s32[63,128]{1,0:T(8,128)S(1)}, s32[63,128]{1,0:T(8,128)}, u32[]{:S(2)}) copy-start(s32[63,128]{1,0:T(8,128)} %local_pick.1) | copy-start | bytes 96772
  0.0 5.7 %copy-start.17 = (s32[64,128]{1,0:T(8,128)S(1)}, s32[64,128]{1,0:T(8,128)}, u32[]{:S(2)}) copy-start(s32[64,128]{1,0:T(8,128)} %leaf_pick.1) | copy-start | bytes 98308
  3.1 41.6 %collective-permute-start.1 = (bf16[16,16512]{1,0:T(8,128)(2,1)}, bf16[16,16512]{1,0:T(8,128)(2,1)}, u32[]{:S(2)}, u32[]{:S(2)}) collective-permute-start(bf16[16,16512]{1,0:T(8,128)(2,1)} %fusion.1), channel_id=1, source_target_pairs={{0,1},{1,2},{2,3},{3,4},{4,5},{5,6},{6,7},{7,8},{8,9},{9,10},{10,1... | collective-permute-start | bytes 1585160 | tf_op jit(solution)/shard_map/ppermute | solution.py:408
  4.4 41.0 %collective-permute-start = (bf16[64,16384]{1,0:T(8,128)(2,1)}, bf16[64,16384]{1,0:T(8,128)(2,1)S(1)}, u32[]{:S(2)}, u32[]{:S(2)}) collective-permute-start(bf16[64,16384]{1,0:T(8,128)(2,1)} %bitcast.17), channel_id=1, source_target_pairs={{0,1},{1,2},{2,3},{3,4},{4,5},{5,6},{6,7},{7,8},{8,9},{9,10},{10,1... | collective-permute-start | bytes 6291464 | tf_op jit(solution)/shard_map/ppermute | solution.py:404
  5.7 2.2 %copy-start.6 = (bf16[64,256,128]{2,1,0:T(8,128)(2,1)S(1)}, bf16[64,256,128]{2,1,0:T(8,128)(2,1)}, u32[]{:S(2)}) copy-start(bf16[64,256,128]{2,1,0:T(8,128)(2,1)} %leaf_hbm.3) | copy-start | bytes 12582916
  7.9 2.2 %copy-start.8 = (bf16[63,256,128]{2,1,0:T(8,128)(2,1)S(1)}, bf16[63,256,128]{2,1,0:T(8,128)(2,1)}, u32[]{:S(2)}) copy-start(bf16[63,256,128]{2,1,0:T(8,128)(2,1)} %local_hbm.3) | copy-start | bytes 12386308
  10.1 1.6 %copy-start.13 = (bf16[16384,64]{0,1:T(8,128)(2,1)S(1)}, bf16[16384,64]{0,1:T(8,128)(2,1)}, u32[]{:S(2)}) copy-start(bf16[16384,64]{0,1:T(8,128)(2,1)} %param.10) | copy-start | bytes 6291460
  30.5 2.0 %copy-start = (bf16[64,128,256]{2,1,0:T(8,128)(2,1)}, bf16[64,128,256]{2,1,0:T(8,128)(2,1)S(1)}, u32[]{:S(2)}) copy-start(bf16[64,128,256]{2,1,0:T(8,128)(2,1)S(1)} %get-tuple-element.9.at) | copy-start | bytes 12582916
  32.4 2.0 %copy-start.3 = (bf16[64,256,128]{2,1,0:T(8,128)(2,1)}, bf16[64,256,128]{2,1,0:T(8,128)(2,1)S(1)}, u32[]{:S(2)}) copy-start(bf16[64,256,128]{2,1,0:T(8,128)(2,1)S(1)} %get-tuple-element.10.b) | copy-start | bytes 12582916
  34.4 1.0 copy-start.15
  36.4 64.4 %all-to-all-start = ((bf16[32,80,128]{2,1,0:T(8,128)(2,1)}), bf16[32,80,128]{2,1,0:T(8,128)(2,1)S(1)}, u32[]{:S(2)}, u32[]{:S(2)}) async-start(bf16[32,80,128]{2,1,0:T(8,128)(2,1)} %broadcast_in_dim.182), calls=%async_computation | async-start | bytes 1310720 | tf_op jit(solution)/shard_map/all_to_all | solution.py:414
  45.5 2.2 %copy-start.4 = (bf16[64,256,128]{2,1,0:T(8,128)(2,1)S(1)}, bf16[64,256,128]{2,1,0:T(8,128)(2,1)}, u32[]{:S(2)}) copy-start(bf16[64,256,128]{2,1,0:T(8,128)(2,1)} %copy-done.3) | copy-start | bytes 12582916
  47.6 19.2 %copy-start.20 = (f32[16]{0:T(128)S(1)}, f32[16]{0:T(128)}, u32[]{:S(2)}) copy-start(f32[16]{0:T(128)} %param.12) | copy-start | bytes 196
  62.1 69.9 %collective-permute-start.2 = (bf16[16,16384]{1,0:T(8,128)(2,1)}, bf16[16,16384]{1,0:T(8,128)(2,1)}, u32[]{:S(2)}, u32[]{:S(2)}) collective-permute-start(bf16[16,16384]{1,0:T(8,128)(2,1)} %near_back.1), channel_id=1, source_target_pairs={{1,0},{2,1},{3,2},{4,3},{5,4},{6,5},{7,6},{8,7},{9,8},{10,9},{11,1... | collective-permute-start | bytes 1572872 | tf_op jit(solution)/shard_map/ppermute | solution.py:424
  67.0 2.2 %copy-start.1 = (bf16[64,128,256]{2,1,0:T(8,128)(2,1)S(1)}, bf16[64,128,256]{2,1,0:T(8,128)(2,1)}, u32[]{:S(2)}) copy-start(bf16[64,128,256]{2,1,0:T(8,128)(2,1)} %copy-done) | copy-start | bytes 12582916
  69.2 2.2 %copy-start.5 = (bf16[64,256,128]{2,1,0:T(8,128)(2,1)S(1)}, bf16[64,256,128]{2,1,0:T(8,128)(2,1)}, u32[]{:S(2)}) copy-start(bf16[64,256,128]{2,1,0:T(8,128)(2,1)} %copy-done.3) | copy-start | bytes 12582916
  71.3 29.4 %copy-start.19 = (s32[31,128]{1,0:T(8,128)S(1)}, s32[31,128]{1,0:T(8,128)}, u32[]{:S(2)}) copy-start(s32[31,128]{1,0:T(8,128)} %top_pick.1) | copy-start | bytes 47620
  98.6 1.0 copy-start.11
  100.8 2.2 %copy-start.7 = (bf16[64,256,128]{2,1,0:T(8,128)(2,1)S(1)}, bf16[64,256,128]{2,1,0:T(8,128)(2,1)}, u32[]{:S(2)}) copy-start(bf16[64,256,128]{2,1,0:T(8,128)(2,1)} %leaf_hbm.3) | copy-start | bytes 12582916
  103.0 2.2 %copy-start.9 = (bf16[63,256,128]{2,1,0:T(8,128)(2,1)S(1)}, bf16[63,256,128]{2,1,0:T(8,128)(2,1)}, u32[]{:S(2)}) copy-start(bf16[63,256,128]{2,1,0:T(8,128)(2,1)} %local_hbm.3) | copy-start | bytes 12386308
  105.2 1.2 copy-start.10
  106.4 1.6 %copy-start.14 = (bf16[31,256,128]{2,1,0:T(8,128)(2,1)S(1)}, bf16[31,256,128]{2,1,0:T(8,128)(2,1)}, u32[]{:S(2)}) copy-start(bf16[31,256,128]{2,1,0:T(8,128)(2,1)} %top_hbm.1) | copy-start | bytes 6094852
  108.0 1.2 copy-start.16
  109.2 7.5 %copy-start.2 = (bf16[64,128,256]{2,1,0:T(8,128)(2,1)S(1)}, bf16[64,128,256]{2,1,0:T(8,128)(2,1)}, u32[]{:S(2)}) copy-start(bf16[64,128,256]{2,1,0:T(8,128)(2,1)} %copy-done) | copy-start | bytes 12582916
  109.2 7.5 %copy-start.12 = (f32[16,16384]{1,0:T(8,128)S(1)}, f32[16,16384]{1,0:T(8,128)}, u32[]{:S(2)}) copy-start(f32[16,16384]{1,0:T(8,128)} %copy-done.11) | copy-start | bytes 3145732

commit v3 on v2

v3 whole, which is shorter than its diff:
```python
import functools
import math

import jax
import jax.numpy as jnp
from jax import lax
from jax.experimental import pallas as pl
from jax.experimental.pallas import tpu as pltpu
from jax.sharding import PartitionSpec as P

f32 = jnp.float32
bf16 = jnp.bfloat16
AXES = ("leaf", "chip")
SCALE = math.log2(math.e) / 32.0
FEAT = 128
GROUP = 16


def dot(a, b, ca=1, cb=0):
    return lax.dot_general(a, b, (((ca,), (cb,)), ((), ())), preferred_element_type=f32)


def copy(src, dst, sem):
    c = pltpu.make_async_copy(src, dst, sem)
    c.start()
    return c


VM = pl.BlockSpec(memory_space=pltpu.VMEM)
HBM = pl.BlockSpec(memory_space=pltpu.HBM)
ANY = pl.BlockSpec(memory_space=pl.ANY)


def square_rows(xf):
    n = jnp.sum(xf * xf, axis=0, keepdims=True)
    hi = n.astype(bf16).astype(f32)
    rest = n - hi
    mid = rest.astype(bf16).astype(f32)
    low = rest - mid
    row = lax.broadcasted_iota(jnp.int32, (16, xf.shape[1]), 0)
    zero = jnp.zeros((), f32)
    neg = jnp.where(row == 0, -hi, jnp.where(row == 1, -mid, jnp.where(row == 2, -low, zero)))
    ones = jnp.where(row < 3, jnp.ones((), f32), zero)
    return neg.astype(bf16), ones.astype(bf16)


def feature_pair(x):
    dim, width = x.shape
    xf = x.astype(f32)
    neg, ones = square_rows(xf)
    pad = jnp.zeros((FEAT - dim - 32, width), bf16)
    left = jnp.concatenate([(xf + xf).astype(bf16), ones, neg, pad], 0)
    right = jnp.concatenate([x, neg, ones, pad], 0)
    return left, right


def swap_form(left, dim):
    half = (left[:dim].astype(f32) * 0.5).astype(bf16)
    return jnp.concatenate([half, left[dim + 16 : dim + 32], left[dim : dim + 16], left[dim + 32 :]], 0)


def selector(pick_row, width):
    rows = lax.broadcasted_iota(jnp.int32, (width, pick_row.shape[1]), 0)
    return jnp.where(rows == pick_row, jnp.ones((), f32), jnp.zeros((), f32)).astype(bf16)


def gauss(right_rows, left_cols):
    s = dot(right_rows, left_cols)
    return jnp.exp2(s * SCALE).astype(bf16)


def grouped(count, group, compute, store, start=0):
    group = min(group, count)

    def body(t, carry):
        got = [compute(start + t * group + u) for u in range(group)]
        for u in range(group):
            store(start + t * group + u, got[u])
        return carry

    if count == group:
        body(0, 0)
    else:
        lax.fori_loop(0, count // group, body, 0)


def lanes(start, width, number=1):
    if isinstance(start, int):
        return pl.ds(start * width, number * width)
    return pl.ds(pl.multiple_of(start * width, width), number * width)


CHUNKS = 4
PAIRS = 8


def up_kernel(dims, x_hbm, d_hbm, ext, leaf_pick, local_pick, leaf_hbm, local_hbm,
              at_hbm, b_hbm, w_hbm, terms_hbm, spread,
              xt, dt, at, b, wt, terms, lb, nb, coeff, skel, tiles, xs, ls, ms, os):
    count, leaf, rank, dim, cols = dims
    part = count // CHUNKS
    seg = lambda c: pl.ds(c * part * leaf, part * leaf)
    own = lambda c: pl.ds(c * part, part)
    get_x = [copy(x_hbm.at[:, seg(c)], xt.at[:, seg(c)], xs.at[c]) for c in range(CHUNKS)]
    get_d = copy(d_hbm, dt, ms.at[0])
    get_leaf = [copy(leaf_hbm.at[own(c)], lb.at[own(c)], ls.at[c]) for c in range(CHUNKS)]
    get_local = copy(local_hbm, nb, ms.at[1])

    def prepare(l):
        left, right = feature_pair(xt[:, lanes(l, leaf)])
        return left, right.T

    def keep(l, got):
        at[l], b[l] = got

    puts = []
    for c in range(CHUNKS):
        get_x[c].wait()
        grouped(part, 8, prepare, keep, c * part)
        puts.append(copy(at.at[own(c)], at_hbm.at[own(c)], os.at[0, c]))
        puts.append(copy(b.at[own(c)], b_hbm.at[own(c)], os.at[1, c]))
    get_d.wait()
    for c in range(CHUNKS):
        wt[:, seg(c)] = dt[:, seg(c)].astype(bf16)
    wt[:, pl.ds(count * leaf, 128)] = ext[...]
    puts.append(copy(wt, w_hbm, ms.at[2]))
    base = count - 1

    def leaf_step(l):
        c = dot(wt[:, lanes(l, leaf)], lb[l])
        sel = selector(leaf_pick[pl.ds(l, 1), :], leaf)
        return c.astype(bf16), dot(at[l], sel).astype(bf16)

    def leaf_keep(l, got):
        coeff[:, lanes(base + l, rank)], skel[:, lanes(base + l, rank)] = got

    for c in range(CHUNKS):
        get_leaf[c].wait()
        grouped(part, 8, leaf_step, leaf_keep, c * part)
    get_local.wait()
    depth = count.bit_length() - 1
    for d in range(depth, 0, -1):
        up = 2 ** (d - 1) - 1

        def climb(j):
            both = lanes(2 * j + 1, rank, 2)
            sel = selector(local_pick[pl.ds(j, 1), :], 2 * rank)
            return dot(coeff[:, both], nb[j]).astype(bf16), dot(skel[:, both], sel).astype(bf16)

        def climb_keep(j, got):
            coeff[:, lanes(j, rank)], skel[:, lanes(j, rank)] = got

        grouped(2 ** (d - 1), 8, climb, climb_keep, up)
    root_c, root_s = coeff[:, :rank], skel[:dim, :rank]
    for s in range(spread.shape[0]):
        spread[s, :cols, :] = root_c
        spread[s, cols:, :] = root_s

    last = count - 2

    def index(j):
        return min(j, last) if isinstance(j, int) else jnp.minimum(j, last)

    def first(j, slot):
        both = skel[:, lanes(2 * index(j) + 1, rank, 2)]
        tiles[slot] = gauss(swap_form(both[:, rank:], dim).T, both[:, :rank])

    def second(j, slot):
        c2 = coeff[:, lanes(2 * index(j) + 1, rank, 2)]
        g = tiles[slot]
        return jnp.concatenate([dot(c2[:, rank:], g), dot(c2[:, :rank], g, 1, 1)], 1)

    for u in range(PAIRS):
        first(u, u)

    def body(t, carry):
        for phase in range(2):
            k = (2 * t + phase) * PAIRS
            got = []
            for u in range(PAIRS):
                first(k + PAIRS + u, (1 - phase) * PAIRS + u)
                got.append(second(k + u, phase * PAIRS + u))
            for u in range(PAIRS):
                terms[:, lanes(2 * index(k + u), rank, 2)] = got[u]
        return carry

    lax.fori_loop(0, count // (2 * PAIRS), body, 0)
    puts.append(copy(terms, terms_hbm, ms.at[3]))
    for p in puts:
        p.wait()


def upward(xt, dt, ext, leaf_pick, local_pick, leaf_basis, local_basis, subtrees):
    count, leaf, rank = leaf_basis.shape
    dim, cols = xt.shape[0], dt.shape[0]
    width = count * leaf + 128
    return pl.pallas_call(
        functools.partial(up_kernel, (count, leaf, rank, dim, cols)),
        in_specs=[HBM, HBM, VM, VM, VM, HBM, HBM],
        out_specs=[HBM] * 4 + [VM],
        out_shape=[
            jax.ShapeDtypeStruct((count, FEAT, leaf), bf16),
            jax.ShapeDtypeStruct((count, leaf, FEAT), bf16),
            jax.ShapeDtypeStruct((cols, width), bf16),
            jax.ShapeDtypeStruct((cols, (2 * count - 2) * rank), f32),
            jax.ShapeDtypeStruct((subtrees, cols + dim, rank), bf16),
        ],
        scratch_shapes=[
            pltpu.VMEM(xt.shape, bf16),
            pltpu.VMEM(dt.shape, f32),
            pltpu.VMEM((count, FEAT, leaf), bf16),
            pltpu.VMEM((count, leaf, FEAT), bf16),
            pltpu.VMEM((cols, width), bf16),
            pltpu.VMEM((cols, (2 * count - 2) * rank), f32),
            pltpu.VMEM(leaf_basis.shape, bf16),
            pltpu.VMEM(local_basis.shape, bf16),
            pltpu.VMEM((cols, (2 * count - 1) * rank), bf16),
            pltpu.VMEM((FEAT, (2 * count - 1) * rank), bf16),
            pltpu.VMEM((2 * PAIRS, rank, rank), bf16),
            pltpu.SemaphoreType.DMA((CHUNKS,)),
            pltpu.SemaphoreType.DMA((CHUNKS,)),
            pltpu.SemaphoreType.DMA((4,)),
            pltpu.SemaphoreType.DMA((2, CHUNKS)),
        ],
        compiler_params=pltpu.CompilerParams(vmem_limit_bytes=60 << 20),
        name="upward",
    )(xt, dt, ext, leaf_pick, local_pick, leaf_basis, local_basis)


def scan_list(count, entries, lst, pair):
    def scan(i, pos):
        for e in range(entries):
            pair[pos + e] = i * count + lst[e, i]
        return pos + lst[entries, i]

    total = lax.fori_loop(0, count, scan, 0)
    for u in range(3 * GROUP):
        pair[total + u] = count * count
    return total


def near_pairs(count, total, pair, at, b, w, acc, tiles):
    h = GROUP
    leaf = b.shape[1]

    def first(k, slot):
        code = pair[k]
        i = code // count
        v = code - i * count
        tiles[slot] = gauss(b[v], at[jnp.where(i < count, i, 0)])

    def second(k, slot):
        code = pair[k]
        i = code // count
        v = code - i * count
        return i, dot(w[:, lanes(v, leaf)], tiles[slot])

    for u in range(h):
        first(u, u)

    def body(t, carry):
        for phase in range(2):
            k = (2 * t + phase) * h
            got = []
            for u in range(h):
                first(k + h + u, (1 - phase) * h + u)
                got.append(second(k + u, phase * h + u))
            for i, o in got:
                acc[i] += o
        return carry

    blocks = (total + h - 1) // h
    lax.fori_loop(0, (blocks + 1) // 2, body, 0)


def write_out(out, acc, count, leaf):
    def store(l, got):
        out[:, lanes(l, leaf)] = got.astype(out.dtype)

    grouped(count, 8, lambda l: acc[l], store)


def near_own_kernel(count, entries, lst, at_hbm, b_hbm, w_hbm, out, pair, acc, tiles, at, b, w, sems):
    gets = [copy(at_hbm, at, sems.at[0]), copy(b_hbm, b, sems.at[1]), copy(w_hbm, w, sems.at[2])]
    total = scan_list(count, entries, lst, pair)
    acc[...] = jnp.zeros_like(acc)
    for g in gets:
        g.wait()
    near_pairs(count, total, pair, at, b, w, acc, tiles)
    write_out(out, acc, count, b.shape[1])


def near_back_kernel(count, entries, lst, x_hbm, b_hbm, w_hbm, after, out, pair, acc, tiles, at, b, w, x, sems):
    leaf = b.shape[1]
    get_x = copy(x_hbm, x, sems.at[0])
    gets = [copy(b_hbm, b, sems.at[1]), copy(w_hbm, w, sems.at[2])]
    total = scan_list(count, entries, lst, pair)
    acc[...] = jnp.zeros_like(acc)

    def keep(l, got):
        at[l] = got

    get_x.wait()
    grouped(count, 8, lambda l: feature_pair(x[:, lanes(l, leaf)])[0], keep)
    for g in gets:
        g.wait()
    near_pairs(count, total, pair, at, b, w, acc, tiles)
    write_out(out, acc, count, leaf)


def near_low_kernel(count, entries, lst, x_hbm, at_hbm, w_hbm, after, out, pair, acc, tiles, at, b, w, x, sems):
    leaf = b.shape[1]
    get_x = copy(x_hbm, x, sems.at[0])
    gets = [copy(at_hbm, at, sems.at[1]), copy(w_hbm, w, sems.at[2])]
    total = scan_list(count, entries, lst, pair)
    acc[...] = jnp.zeros_like(acc)

    def keep(l, got):
        b[l] = got

    get_x.wait()
    grouped(count, 8, lambda l: feature_pair(x[:, lanes(l, leaf)])[1].T, keep)
    for g in gets:
        g.wait()
    near_pairs(count, total, pair, at, b, w, acc, tiles)
    write_out(out, acc, count, leaf)


def near_call(kernel, lst, operands, count, entries, leaf, dim, cols, dtype, own, name):
    return pl.pallas_call(
        functools.partial(kernel, count, entries),
        grid_spec=pltpu.PrefetchScalarGridSpec(
            num_scalar_prefetch=1,
            grid=(1,),
            in_specs=[HBM] * 3 if own else [ANY, HBM, ANY, HBM],
            out_specs=VM,
            scratch_shapes=[
                pltpu.SMEM((count * entries + entries + 4 * GROUP,), jnp.int32),
                pltpu.VMEM((count + 1, cols, leaf), f32),
                pltpu.VMEM((2 * GROUP, leaf, leaf), bf16),
                pltpu.VMEM((count, FEAT, leaf), bf16),
                pltpu.VMEM((count, leaf, FEAT), bf16),
                pltpu.VMEM((cols, count * leaf + 128), bf16),
            ]
            + ([] if own else [pltpu.VMEM((dim, count * leaf), bf16)])
            + [pltpu.SemaphoreType.DMA((3,))],
        ),
        out_shape=jax.ShapeDtypeStruct((cols, count * leaf), dtype),
        compiler_params=pltpu.CompilerParams(vmem_limit_bytes=60 << 20),
        name=name,
    )(lst, *operands)


def down_kernel(dims, pos_ref, gathered, top_pick, ridge, top_hbm, terms_hbm, local_hbm, leaf_hbm, d_hbm, n1_hbm,
                n2_hbm, n3_hbm, out, tb, terms, nb, lb, dt, n1, n2, n3, tcoeff, tskel, value, sems):
    count, leaf, rank, dim, cols, subtrees = dims
    pairs = ((top_hbm, tb), (terms_hbm, terms), (local_hbm, nb), (leaf_hbm, lb), (d_hbm, dt), (n1_hbm, n1),
             (n2_hbm, n2), (n3_hbm, n3))
    gets = [copy(src, dst, sems.at[k]) for k, (src, dst) in enumerate(pairs)]
    pos = pos_ref[0]
    depth = subtrees.bit_length() - 1
    for s in range(subtrees):
        tcoeff[:, lanes(subtrees - 1 + s, rank)] = gathered[s, :cols]
        tskel[:, lanes(subtrees - 1 + s, rank)] = gathered[s, cols:]
    gets[0].wait()
    for d in range(depth - 1, 0, -1):

        def climb(j):
            both = lanes(2 * j + 1, rank, 2)
            sel = selector(top_pick[pl.ds(j, 1), :], 2 * rank)
            return dot(tcoeff[:, both], tb[j]).astype(bf16), dot(tskel[:, both], sel).astype(bf16)

        def climb_keep(j, got):
            tcoeff[:, lanes(j, rank)], tskel[:, lanes(j, rank)] = got

        grouped(2**d, 8, climb, climb_keep, 2**d - 1)

    def half(v):
        return (v.astype(f32) * 0.5).astype(bf16)

    top_terms = {}
    for d in range(depth, 0, -1):
        mine = pos >> (depth - d)
        other = mine ^ 1
        own_left = feature_pair(half(tskel[:, lanes(2**d - 1 + mine, rank)]))[0]
        sib_right = feature_pair(half(tskel[:, lanes(2**d - 1 + other, rank)]))[1]
        g = gauss(sib_right.T, own_left)
        top_terms[d] = dot(tcoeff[:, lanes(2**d - 1 + other, rank)], g)
    v = jnp.zeros((cols, rank), bf16)
    for d in range(1, depth + 1):
        parent = pos >> (depth - d + 1)
        down = dot(v, tb[2 ** (d - 1) - 1 + parent], 1, 1)
        right = ((pos >> (depth - d)) & 1) == 1
        v = (top_terms[d] + jnp.where(right, down[:, rank:], down[:, :rank])).astype(bf16)
    value[:, lanes(0, rank)] = v
    gets[1].wait()
    gets[2].wait()
    local_depth = count.bit_length() - 1
    for d in range(1, local_depth + 1):

        def descend(j):
            down = dot(value[:, lanes(j, rank)], nb[j], 1, 1)
            return (terms[:, lanes(2 * j, rank, 2)] + down).astype(bf16)

        def descend_keep(j, got):
            value[:, lanes(2 * j + 1, rank, 2)] = got

        grouped(2 ** (d - 1), 8, descend, descend_keep, 2 ** (d - 1) - 1)
    for g in gets[3:]:
        g.wait()
    scale = ridge[...]

    def finish(l):
        far = dot(value[:, lanes(count - 1 + l, rank)], lb[l], 1, 1)
        s = lanes(l, leaf)
        return scale * dt[:, s] + far + (n1[:, s] + n2[:, s] + n3[:, s].astype(f32))

    def finish_keep(l, got):
        out[:, lanes(l, leaf)] = got

    grouped(count, 8, finish, finish_keep)


def downward(pos, gathered, top_pick, ridge, top_basis, terms, local_basis, leaf_basis, dt, n1, n2, n3, dim):
    count, leaf, rank = leaf_basis.shape
    cols = dt.shape[0]
    subtrees = gathered.shape[0]
    big = (top_basis, terms, local_basis, leaf_basis, dt, n1, n2, n3)
    return pl.pallas_call(
        functools.partial(down_kernel, (count, leaf, rank, dim, cols, subtrees)),
        grid_spec=pltpu.PrefetchScalarGridSpec(
            num_scalar_prefetch=1,
            grid=(1,),
            in_specs=[VM] * 3 + [HBM] * 7 + [ANY],
            out_specs=VM,
            scratch_shapes=[pltpu.VMEM(a.shape, a.dtype) for a in big]
            + [
                pltpu.VMEM((cols, (2 * subtrees - 1) * rank), bf16),
                pltpu.VMEM((dim, (2 * subtrees - 1) * rank), bf16),
                pltpu.VMEM((cols, (2 * count - 1) * rank), bf16),
                pltpu.SemaphoreType.DMA((8,)),
            ],
        ),
        out_shape=jax.ShapeDtypeStruct(dt.shape, f32),
        compiler_params=pltpu.CompilerParams(vmem_limit_bytes=60 << 20),
        name="downward",
    )(pos, gathered, top_pick, ridge, *big)


def class_list(ids, low, count):
    entries = ids.shape[0]
    local = ids - low
    inside = (local >= 0) & (local < count)
    ones = inside.astype(jnp.int32)
    row = [jnp.zeros_like(ones[0])]
    for e in range(entries):
        row.append(row[-1] + ones[e])
    out = []
    for k in range(entries):
        acc = jnp.zeros_like(ones[0])
        for e in range(k, entries):
            acc = acc + jnp.where(inside[e] & (row[e] == k), local[e], 0)
        out.append(acc)
    out.append(row[-1])
    return jnp.stack(out, 0)


def shards(points, direction, ridge, leaf_basis, local_basis, top_basis, leaf_pick, local_pick, top_pick, near_list):
    count, leaf, rank = leaf_basis.shape
    dim, cols = points.shape[1], direction.shape[1]
    entries = near_list.shape[1]
    chips = lax.axis_size("chip")
    subtrees = lax.axis_size("leaf") * chips
    pos = lax.axis_index("leaf") * chips + lax.axis_index("chip")
    upper = [(i, i + 1) for i in range(subtrees - 1)]
    lower = [(i + 1, i) for i in range(subtrees - 1)]

    xt, dt, ids = points.T, direction.T, near_list.T
    x_low = lax.ppermute(xt, AXES, upper)
    list_up = class_list(ids, (pos + 1) * count, count)
    ext = jnp.pad(list_up.astype(bf16), ((0, cols - entries - 1), (0, 128 - count)))
    list_own = class_list(ids, pos * count, count)
    list_low = class_list(ids, (pos - 1) * count, count)

    at, b, w, terms, spread = upward(xt, dt, ext, leaf_pick, local_pick, leaf_basis, local_basis, subtrees)
    w_low = lax.ppermute(w, AXES, upper)
    gathered = lax.all_to_all(spread, AXES, 0, 0)
    call = functools.partial(near_call, count=count, entries=entries, leaf=leaf, dim=dim, cols=cols)
    n_own = call(near_own_kernel, list_own, (at, b, w), dtype=f32, own=True, name="near_own")
    list_back = w_low[: entries + 1, count * leaf : count * leaf + count].astype(jnp.int32)
    back = call(near_back_kernel, list_back, (x_low, b, w, n_own), dtype=bf16, own=False, name="near_back")
    returned = lax.ppermute(back, AXES, lower)
    n_low = call(near_low_kernel, list_low, (x_low, at, w_low, back), dtype=f32, own=False, name="near_low")
    out = downward(
        pos[None], gathered, top_pick, ridge[:, None], top_basis, terms, local_basis, leaf_basis, dt,
        n_own, n_low, returned, dim,
    )
    return out.T


def solution(mesh):
    split = P(AXES, None)
    split3 = P(AXES, None, None)
    return jax.shard_map(
        shards,
        mesh=mesh,
        in_specs=(split, split, P(), split3, split3, P(), split, split, P(), split),
        out_specs=split,
        check_vma=False,
    )
```

time: 135 us -> 107 us (0.79)
  local copies, waits for them, and re-layouts: 29.1 us -> 6.17 us
  starting transfers between devices: 15.4 us -> 10.9 us
  other arithmetic: 6.06 us -> 1.81 us
  Pallas kernels: 83.2 us -> 86.5 us
    unnamed x42 -> x10, local copies, waits for them, and re-layouts: 26.8 us -> 2.41 us
    ppermute x1, starting transfers between devices: 4.76 us -> 1.32 us  [shards(): returned = lax.ppermute(back, AXES, lower)]
    pallas_call x1, Pallas kernels: 7.5 us -> 9.91 us  [downward(): pl.pallas_call(functools.partial(down_kernel, (count, leaf, rank, dim, co...]
    pallas_call x3, Pallas kernels: 56.9 us -> 59.3 us  [near_call(): pl.pallas_call(functools.partial(kernel, count, entries), grid_spec=pltpu...]
    another operation x3, local copies, waits for them, and re-layouts: 0.16 us -> 2.49 us  [class_list(): return jnp.stack(out, 0)]
    transpose x1 -> x0, other arithmetic: 2.1 us -> none  [shards(): return (out + returned.astype(f32)).T]
    pallas_call x1, Pallas kernels: 18.8 us -> 17.3 us  [upward(): pl.pallas_call(functools.partial(up_kernel, (count, leaf, rank, dim, cols...]
  transfers between devices with their start and end apart: 4 -> 4, of which waited for: 0 -> 0; matrix products, arithmetic and copies ran while one was open for 2% -> 5% of each run, Pallas kernels for 62% -> 72%
where the time goes in v3:
time: 107 us; the launch traced here: 106 us
  Pallas kernels  86.5 us (81%)
  starting transfers between devices  10.9 us (10%)
  local copies, waits for them, and re-layouts  6.17 us (6%)
  other arithmetic  1.81 us (2%)
    pallas_call x3, Pallas kernels, near_call(): pl.pallas_call(functools.partial(kernel, count, entries), grid_spec=pltpu...  59.3 us
    pallas_call x1, Pallas kernels, upward(): pl.pallas_call(functools.partial(up_kernel, (count, leaf, rank, dim, cols...  17.3 us
    pallas_call x1, Pallas kernels, downward(): pl.pallas_call(functools.partial(down_kernel, (count, leaf, rank, dim, co...  9.91 us
    all_to_all x1, starting transfers between devices, shards(): gathered = lax.all_to_all(spread, AXES, 0, 0)  7.05 us
    another operation x3, local copies, waits for them, and re-layouts, class_list(): return jnp.stack(out, 0)  2.49 us
    unnamed x10, local copies, waits for them, and re-layouts  2.41 us
  transfers between devices with their start and end apart: 4, of which 0 were waited for; matrix products, arithmetic and copies ran while one was open for 5% of the time, Pallas kernels for 72%

profile of v3, /device:TPU:31, one launch (start us, length us, event | category | flops | bytes accessed | tf_op | source)
XLA Modules:
  0.0 105.8 jit_solution(830951845734965530)
XLA Ops:
  0.0 1.3 %collective-permute-start = (bf16[64,16384]{1,0:T(8,128)(2,1)}, bf16[64,16384]{1,0:T(8,128)(2,1)S(1)}, u32[]{:S(2)}, u32[]{:S(2)}) collective-permute-start(bf16[64,16384]{1,0:T(8,128)(2,1)} %bitcast.16), channel_id=1, source_target_pairs={{0,1},{1,2},{2,3},{3,4},{4,5},{5,6},{6,7},{7,8},{8,9},{9,10},{10,1... | collective-permute-start | bytes 6291464 | tf_op jit(solution)/shard_map/ppermute | solution.py:479
  1.3 0.7 fusion.146
  2.2 0.1 stack.7
  2.3 0.6 pad.4.ext
  2.9 17.3 %upward.1 = (bf16[64,128,256]{2,1,0:T(8,128)(2,1)}, bf16[64,256,128]{2,1,0:T(8,128)(2,1)}, bf16[16,16512]{1,0:T(8,128)(2,1)}, f32[16,16128]{1,0:T(8,128)}, bf16[32,80,128]{2,1,0:T(8,128)(2,1)}) custom-call(bf16[64,16384]{1,0:T(8,128)(2,1)} %bitcast.17, f32[16,16384]{1,0:T(8,128)} %bitcast.14, bf16[16,128]{1,0:T(8,128)(2,1)} %pad.4.ext, s32[64,128]{1,0:T(8,128)} %leaf_pick.1, ...), custom_call_target="tpu_custom_call" | custom-call | tf_op jit(solution)/shard_map/upward/pallas_call | solution.py:197
  20.2 7.1 %all-to-all-start = ((bf16[32,80,128]{2,1,0:T(8,128)(2,1)}), bf16[32,80,128]{2,1,0:T(8,128)(2,1)S(1)}, u32[]{:S(2)}, u32[]{:S(2)}) async-start(bf16[32,80,128]{2,1,0:T(8,128)(2,1)} %get-tuple-element.10), calls=%async_computation | async-start | bytes 1310720 | tf_op jit(solution)/shard_map/all_to_all | solution.py:487
  27.2 1.3 %collective-permute-start.1 = (bf16[16,16512]{1,0:T(8,128)(2,1)}, bf16[16,16512]{1,0:T(8,128)(2,1)S(1)}, u32[]{:S(2)}, u32[]{:S(2)}) collective-permute-start(bf16[16,16512]{1,0:T(8,128)(2,1)} %get-tuple-element.14.w_hbm), channel_id=1, source_target_pairs={{0,1},{1,2},{2,3},{3,4},{4,5},{5,6},{6,7},{7,8},{8,9},{9,10},{10,1... | collective-permute-start | bytes 1585160 | tf_op jit(solution)/shard_map/ppermute | solution.py:486
  28.8 1.2 %stack.8.lst = s32[11,64]{1,0:T(8,128)} concatenate(s32[1,64]{1,0:T(1,128)S(1)} %fusion.51, s32[1,64]{1,0:T(1,128)S(1)} %fusion.59, s32[1,64]{1,0:T(1,128)S(1)} %fusion.66, s32[1,64]{1,0:T(1,128)S(1)} %fusion.72, s32[1,64]{1,0:T(1,128)S(1)} %fusion.77, s32[1,64]{1,0:T(1,128)S(1)} %get-tuple-element.60, s32[1,64]{1,0:T(1,128)S(1)} %get-tuple-element.54, ...), dimensions={0} | concatenate | bytes 5632 | tf_op jit(solution)/shard_map/stack | solution.py:465
  30.0 27.7 %near_own.1.after.n1_hbm = f32[16,16384]{1,0:T(8,128)} custom-call(s32[11,64]{1,0:T(8,128)} %stack.8.lst, bf16[64,128,256]{2,1,0:T(8,128)(2,1)} %get-tuple-element.12.at_hbm, bf16[64,256,128]{2,1,0:T(8,128)(2,1)} %get-tuple-element.13.b_hbm, bf16[16,16512]{1,0:T(8,128)(2,1)} %get-tuple-element.14.w_hbm), custom_call_target="tpu_custom_call" | custom-call | tf_op jit(solution)/shard_map/near_own/pallas_call | solution.py:330
  57.8 0.0 collective-permute-done.1.w_hbm
  57.8 0.0 copy-start.2
  57.8 0.6 slice_convert_fusion.lst
  58.4 0.0 copy-start.4
  58.4 0.0 collective-permute-done.x_hbm
  58.5 0.0 copy-start
  58.5 1.4 %copy-done = bf16[64,16384]{1,0:T(8,128)(2,1)} copy-done((bf16[64,16384]{1,0:T(8,128)(2,1)}, bf16[64,16384]{1,0:T(8,128)(2,1)S(1)}, u32[]{:S(2)}) %copy-start) | copy-done | bytes 2097176
  59.8 14.6 %near_back.1.after = bf16[16,16384]{1,0:T(8,128)(2,1)} custom-call(s32[11,64]{1,0:T(8,128)} %slice_convert_fusion.lst, bf16[64,16384]{1,0:T(8,128)(2,1)} %copy-done, bf16[64,256,128]{2,1,0:T(8,128)(2,1)} %get-tuple-element.13.b_hbm, bf16[16,16512]{1,0:T(8,128)(2,1)} %get-tuple-element.14.w_hbm, f32[16,16384]{1,0:T(8,128)} %near_own.1.after.n1_hbm), custom_call_target="tpu_custom_call" | custom-call | tf_op jit(solution)/shard_map/near_back/pallas_call | solution.py:330
  74.4 1.3 %collective-permute-start.2 = (bf16[16,16384]{1,0:T(8,128)(2,1)}, bf16[16,16384]{1,0:T(8,128)(2,1)S(1)}, u32[]{:S(2)}, u32[]{:S(2)}) collective-permute-start(bf16[16,16384]{1,0:T(8,128)(2,1)} %near_back.1.after), channel_id=1, source_target_pairs={{1,0},{2,1},{3,2},{4,3},{5,4},{6,5},{7,6},{8,7},{9,8},{10,9},{11,1... | collective-permute-start | bytes 1572872 | tf_op jit(solution)/shard_map/ppermute | solution.py:492
  75.8 0.0 copy-done.4
  75.8 0.7 copy.11.ridge
  76.5 1.2 %stack.9.lst = s32[11,64]{1,0:T(8,128)} concatenate(s32[1,64]{1,0:T(1,128)S(1)} %fusion.95, s32[1,64]{1,0:T(1,128)S(1)} %fusion.103, s32[1,64]{1,0:T(1,128)S(1)} %fusion.110, s32[1,64]{1,0:T(1,128)S(1)} %fusion.116, s32[1,64]{1,0:T(1,128)S(1)} %fusion.121, s32[1,64]{1,0:T(1,128)S(1)} %get-tuple-element.58, s32[1,64]{1,0:T(1,128)S(1)} %get-tuple-element.52, ...), dimensions={0} | concatenate | bytes 5632 | tf_op jit(solution)/shard_map/stack | solution.py:465
  77.7 0.0 copy-done.2
  77.7 17.0 %near_low.1.n2_hbm = f32[16,16384]{1,0:T(8,128)} custom-call(s32[11,64]{1,0:T(8,128)} %stack.9.lst, bf16[64,16384]{1,0:T(8,128)(2,1)} %copy-done, bf16[64,128,256]{2,1,0:T(8,128)(2,1)} %get-tuple-element.12.at_hbm, bf16[16,16512]{1,0:T(8,128)(2,1)} %copy-done.2, bf16[16,16384]{1,0:T(8,128)(2,1)} %near_back.1.after), custom_call_target="tpu_custom_call" | custom-call | tf_op jit(solution)/shard_map/near_low/pallas_call | solution.py:330
  94.7 0.0 all-to-all-done.gathered
  94.7 0.0 copy-start.1
  94.7 0.0 collective-permute-done.2.n3_hbm
  94.7 0.0 copy-start.3
  94.8 0.8 copy-done.1
  95.6 0.2 copy-done.3
  95.8 9.9 %downward.1 = f32[16,16384]{1,0:T(8,128)} custom-call(s32[1]{0:T(128)} %bitcast.pos_ref, bf16[32,80,128]{2,1,0:T(8,128)(2,1)} %copy-done.1, s32[31,128]{1,0:T(8,128)} %top_pick.1, f32[16,1]{1,0:T(8,128)} %copy.11.ridge, bf16[31,256,128]{2,1,0:T(8,128)(2,1)} %top_hbm.1, f32[16,16128]{1,0:T(8,128)} %get-tuple-element.11.terms_hbm, ...), custom_call_target="tpu_custom_call" | custom-call | tf_op jit(solution)/shard_map/downward/pallas_call | solution.py:429
  (26 shorter events, 0.5 us)
Async XLA Ops:
  0.0 58.5 %collective-permute-start = (bf16[64,16384]{1,0:T(8,128)(2,1)}, bf16[64,16384]{1,0:T(8,128)(2,1)S(1)}, u32[]{:S(2)}, u32[]{:S(2)}) collective-permute-start(bf16[64,16384]{1,0:T(8,128)(2,1)} %bitcast.16), channel_id=1, source_target_pairs={{0,1},{1,2},{2,3},{3,4},{4,5},{5,6},{6,7},{7,8},{8,9},{9,10},{10,1... | collective-permute-start | bytes 6291464 | tf_op jit(solution)/shard_map/ppermute | solution.py:479
  20.2 74.6 %all-to-all-start = ((bf16[32,80,128]{2,1,0:T(8,128)(2,1)}), bf16[32,80,128]{2,1,0:T(8,128)(2,1)S(1)}, u32[]{:S(2)}, u32[]{:S(2)}) async-start(bf16[32,80,128]{2,1,0:T(8,128)(2,1)} %get-tuple-element.10), calls=%async_computation | async-start | bytes 1310720 | tf_op jit(solution)/shard_map/all_to_all | solution.py:487
  27.2 30.6 %collective-permute-start.1 = (bf16[16,16512]{1,0:T(8,128)(2,1)}, bf16[16,16512]{1,0:T(8,128)(2,1)S(1)}, u32[]{:S(2)}, u32[]{:S(2)}) collective-permute-start(bf16[16,16512]{1,0:T(8,128)(2,1)} %get-tuple-element.14.w_hbm), channel_id=1, source_target_pairs={{0,1},{1,2},{2,3},{3,4},{4,5},{5,6},{6,7},{7,8},{8,9},{9,10},{10,1... | collective-permute-start | bytes 1585160 | tf_op jit(solution)/shard_map/ppermute | solution.py:486
  57.8 19.9 %copy-start.2 = (bf16[16,16512]{1,0:T(8,128)(2,1)}, bf16[16,16512]{1,0:T(8,128)(2,1)S(1)}, u32[]{:S(2)}) copy-start(bf16[16,16512]{1,0:T(8,128)(2,1)S(1)} %collective-permute-done.1.w_hbm) | copy-start | bytes 1585156
  58.4 17.3 %copy-start.4 = (f32[16]{0:T(128)S(1)}, f32[16]{0:T(128)}, u32[]{:S(2)}) copy-start(f32[16]{0:T(128)} %param.12) | copy-start | bytes 196
  58.5 1.4 %copy-start = (bf16[64,16384]{1,0:T(8,128)(2,1)}, bf16[64,16384]{1,0:T(8,128)(2,1)S(1)}, u32[]{:S(2)}) copy-start(bf16[64,16384]{1,0:T(8,128)(2,1)S(1)} %collective-permute-done.x_hbm) | copy-start | bytes 6291460
  74.4 20.3 %collective-permute-start.2 = (bf16[16,16384]{1,0:T(8,128)(2,1)}, bf16[16,16384]{1,0:T(8,128)(2,1)S(1)}, u32[]{:S(2)}, u32[]{:S(2)}) collective-permute-start(bf16[16,16384]{1,0:T(8,128)(2,1)} %near_back.1.after), channel_id=1, source_target_pairs={{1,0},{2,1},{3,2},{4,3},{5,4},{6,5},{7,6},{8,7},{9,8},{10,9},{11,1... | collective-permute-start | bytes 1572872 | tf_op jit(solution)/shard_map/ppermute | solution.py:492
  94.7 0.8 copy-start.1
  94.7 1.0 copy-start.3

commit v4 on v3

v4 whole, which is shorter than its diff:
```python
import functools
import math

import jax
import jax.numpy as jnp
from jax import lax
from jax.experimental import pallas as pl
from jax.experimental.pallas import tpu as pltpu
from jax.sharding import PartitionSpec as P

f32 = jnp.float32
bf16 = jnp.bfloat16
AXES = ("leaf", "chip")
SCALE = math.log2(math.e) / 32.0
FEAT = 128
GROUP = 16


def dot(a, b, ca=1, cb=0):
    return lax.dot_general(a, b, (((ca,), (cb,)), ((), ())), preferred_element_type=f32)


def copy(src, dst, sem):
    c = pltpu.make_async_copy(src, dst, sem)
    c.start()
    return c


VM = pl.BlockSpec(memory_space=pltpu.VMEM)
HBM = pl.BlockSpec(memory_space=pltpu.HBM)
ANY = pl.BlockSpec(memory_space=pl.ANY)


def square_rows(xf):
    n = jnp.sum(xf * xf, axis=0, keepdims=True)
    hi = n.astype(bf16).astype(f32)
    rest = n - hi
    mid = rest.astype(bf16).astype(f32)
    low = rest - mid
    row = lax.broadcasted_iota(jnp.int32, (16, xf.shape[1]), 0)
    zero = jnp.zeros((), f32)
    neg = jnp.where(row == 0, -hi, jnp.where(row == 1, -mid, jnp.where(row == 2, -low, zero)))
    ones = jnp.where(row < 3, jnp.ones((), f32), zero)
    return neg.astype(bf16), ones.astype(bf16)


def feature_pair(x):
    dim, width = x.shape
    xf = x.astype(f32)
    neg, ones = square_rows(xf)
    pad = jnp.zeros((FEAT - dim - 32, width), bf16)
    left = jnp.concatenate([(xf + xf).astype(bf16), ones, neg, pad], 0)
    right = jnp.concatenate([x, neg, ones, pad], 0)
    return left, right


def swap_form(left, dim):
    half = (left[:dim].astype(f32) * 0.5).astype(bf16)
    return jnp.concatenate([half, left[dim + 16 : dim + 32], left[dim : dim + 16], left[dim + 32 :]], 0)


def selector(pick_row, width):
    rows = lax.broadcasted_iota(jnp.int32, (width, pick_row.shape[1]), 0)
    return jnp.where(rows == pick_row, jnp.ones((), f32), jnp.zeros((), f32)).astype(bf16)


def gauss(right_rows, left_cols):
    s = dot(right_rows, left_cols)
    return jnp.exp2(s * SCALE).astype(bf16)


def grouped(count, group, compute, store, start=0):
    group = min(group, count)

    def body(t, carry):
        got = [compute(start + t * group + u) for u in range(group)]
        for u in range(group):
            store(start + t * group + u, got[u])
        return carry

    if count == group:
        body(0, 0)
    else:
        lax.fori_loop(0, count // group, body, 0)


def lanes(start, width, number=1):
    if isinstance(start, int):
        return pl.ds(start * width, number * width)
    return pl.ds(pl.multiple_of(start * width, width), number * width)


CHUNKS = 4
PAIRS = 8


def class_list(ids, low, count):
    entries = ids.shape[0]
    local = ids - low
    inside = (local >= 0) & (local < count)
    ones = inside.astype(jnp.int32)
    rank = [jnp.zeros_like(ones[0:1])]
    for e in range(entries):
        rank.append(rank[-1] + ones[e : e + 1])
    row = lax.broadcasted_iota(jnp.int32, (16, ids.shape[1]), 0)
    out = jnp.where(row == entries, rank[-1], 0)
    for e in range(entries):
        here = (row == rank[e]) & (ones[e : e + 1] == 1)
        out = out + jnp.where(here, local[e : e + 1], 0)
    return out


def up_kernel(dims, pos_ref, x_hbm, d_hbm, ids, leaf_pick, local_pick, leaf_hbm, local_hbm,
              w_hbm, terms_hbm, spread, list_own, list_low,
              xt, dt, at, wt, terms, lb, nb, coeff, skel, tiles, xs, ls, ms):
    count, leaf, rank, dim, cols = dims
    part = count // CHUNKS
    seg = lambda c: pl.ds(c * part * leaf, part * leaf)
    own = lambda c: pl.ds(c * part, part)
    get_x = [copy(x_hbm.at[:, seg(c)], xt.at[:, seg(c)], xs.at[c]) for c in range(CHUNKS)]
    get_d = copy(d_hbm, dt, ms.at[0])
    get_leaf = [copy(leaf_hbm.at[own(c)], lb.at[own(c)], ls.at[c]) for c in range(CHUNKS)]
    get_local = copy(local_hbm, nb, ms.at[1])
    pos = pos_ref[0]
    table = ids[...]
    list_own[...] = class_list(table, pos * count, count)
    list_low[...] = class_list(table, (pos - 1) * count, count)
    wt[:, pl.ds(count * leaf, 128)] = jnp.zeros((cols, 128), bf16)
    wt[:, pl.ds(count * leaf, count)] = class_list(table, (pos + 1) * count, count).astype(f32).astype(bf16)

    def keep(l, got):
        at[l] = got

    for c in range(CHUNKS):
        get_x[c].wait()
        grouped(part, 8, lambda l: feature_pair(xt[:, lanes(l, leaf)])[0], keep, c * part)
    get_d.wait()
    for c in range(CHUNKS):
        wt[:, seg(c)] = dt[:, seg(c)].astype(bf16)
    puts = [copy(wt, w_hbm, ms.at[2])]
    base = count - 1

    def leaf_step(l):
        c = dot(wt[:, lanes(l, leaf)], lb[l])
        sel = selector(leaf_pick[pl.ds(l, 1), :], leaf)
        return c.astype(bf16), dot(at[l], sel).astype(bf16)

    def leaf_keep(l, got):
        coeff[:, lanes(base + l, rank)], skel[:, lanes(base + l, rank)] = got

    for c in range(CHUNKS):
        get_leaf[c].wait()
        grouped(part, 8, leaf_step, leaf_keep, c * part)
    get_local.wait()
    depth = count.bit_length() - 1
    for d in range(depth, 0, -1):
        up = 2 ** (d - 1) - 1

        def climb(j):
            both = lanes(2 * j + 1, rank, 2)
            sel = selector(local_pick[pl.ds(j, 1), :], 2 * rank)
            return dot(coeff[:, both], nb[j]).astype(bf16), dot(skel[:, both], sel).astype(bf16)

        def climb_keep(j, got):
            coeff[:, lanes(j, rank)], skel[:, lanes(j, rank)] = got

        grouped(2 ** (d - 1), 8, climb, climb_keep, up)
    root_c, root_s = coeff[:, :rank], skel[:dim, :rank]
    for s in range(spread.shape[0]):
        spread[s, :cols, :] = root_c
        spread[s, cols:, :] = root_s

    last = count - 2

    def index(j):
        return min(j, last) if isinstance(j, int) else jnp.minimum(j, last)

    def first(j, slot):
        both = skel[:, lanes(2 * index(j) + 1, rank, 2)]
        tiles[slot] = gauss(swap_form(both[:, rank:], dim).T, both[:, :rank])

    def second(j, slot):
        c2 = coeff[:, lanes(2 * index(j) + 1, rank, 2)]
        g = tiles[slot]
        return jnp.concatenate([dot(c2[:, rank:], g), dot(c2[:, :rank], g, 1, 1)], 1)

    for u in range(PAIRS):
        first(u, u)

    def body(t, carry):
        for phase in range(2):
            k = (2 * t + phase) * PAIRS
            got = []
            for u in range(PAIRS):
                first(k + PAIRS + u, (1 - phase) * PAIRS + u)
                got.append(second(k + u, phase * PAIRS + u))
            for u in range(PAIRS):
                terms[:, lanes(2 * index(k + u), rank, 2)] = got[u]
        return carry

    lax.fori_loop(0, count // (2 * PAIRS), body, 0)
    puts.append(copy(terms, terms_hbm, ms.at[3]))
    for p in puts:
        p.wait()


def upward(pos, xt, dt, ids, leaf_pick, local_pick, leaf_basis, local_basis, subtrees):
    count, leaf, rank = leaf_basis.shape
    dim, cols = xt.shape[0], dt.shape[0]
    width = count * leaf + 128
    return pl.pallas_call(
        functools.partial(up_kernel, (count, leaf, rank, dim, cols)),
        grid_spec=pltpu.PrefetchScalarGridSpec(
            num_scalar_prefetch=1,
            grid=(1,),
            in_specs=[HBM, HBM, VM, VM, VM, HBM, HBM],
            out_specs=[HBM, HBM, VM, VM, VM],
            scratch_shapes=[
                pltpu.VMEM(xt.shape, bf16),
                pltpu.VMEM(dt.shape, f32),
                pltpu.VMEM((count, FEAT, leaf), bf16),
                pltpu.VMEM((cols, width), bf16),
                pltpu.VMEM((cols, (2 * count - 2) * rank), f32),
                pltpu.VMEM(leaf_basis.shape, bf16),
                pltpu.VMEM(local_basis.shape, bf16),
                pltpu.VMEM((cols, (2 * count - 1) * rank), bf16),
                pltpu.VMEM((FEAT, (2 * count - 1) * rank), bf16),
                pltpu.VMEM((2 * PAIRS, rank, rank), bf16),
                pltpu.SemaphoreType.DMA((CHUNKS,)),
                pltpu.SemaphoreType.DMA((CHUNKS,)),
                pltpu.SemaphoreType.DMA((4,)),
            ],
        ),
        out_shape=[
            jax.ShapeDtypeStruct((cols, width), bf16),
            jax.ShapeDtypeStruct((cols, (2 * count - 2) * rank), f32),
            jax.ShapeDtypeStruct((subtrees, cols + dim, rank), bf16),
            jax.ShapeDtypeStruct((16, count), jnp.int32),
            jax.ShapeDtypeStruct((16, count), jnp.int32),
        ],
        compiler_params=pltpu.CompilerParams(vmem_limit_bytes=60 << 20),
        name="upward",
    )(pos, xt, dt, ids, leaf_pick, local_pick, leaf_basis, local_basis)


def scan_list(count, entries, lst, pair):
    def scan(i, pos):
        for e in range(entries):
            pair[pos + e] = i * count + lst[e, i]
        return pos + lst[entries, i]

    total = lax.fori_loop(0, count, scan, 0)
    for u in range(3 * GROUP):
        pair[total + u] = count * count
    return total


def near_pairs(count, total, pair, at, b, w, acc, tiles):
    h = GROUP
    leaf = b.shape[1]
    shift = count.bit_length() - 1

    def first(k, slot):
        code = pair[k]
        tiles[slot] = gauss(b[code & (count - 1)], at[(code >> shift) & (count - 1)])

    def second(k, slot):
        code = pair[k]
        return code >> shift, dot(w[:, lanes(code & (count - 1), leaf)], tiles[slot])

    for u in range(h):
        first(u, u)

    def body(t, carry):
        for phase in range(2):
            k = (2 * t + phase) * h
            got = []
            for u in range(h):
                first(k + h + u, (1 - phase) * h + u)
                got.append(second(k + u, phase * h + u))
            for i, o in got:
                acc[i] += o
        return carry

    blocks = (total + h - 1) // h
    lax.fori_loop(0, (blocks + 1) // 2, body, 0)


def near_scratch(count, entries, leaf, dim, cols):
    return [
        pltpu.SMEM((count * entries + entries + 4 * GROUP,), jnp.int32),
        pltpu.VMEM((2 * GROUP, leaf, leaf), bf16),
        pltpu.VMEM((count, FEAT, leaf), bf16),
        pltpu.VMEM((count, leaf, FEAT), bf16),
        pltpu.VMEM((cols, count * leaf + 128), bf16),
        pltpu.VMEM((dim, count * leaf), bf16),
    ]


def near_own_kernel(entries, lst, x_hbm, w_hbm, acc, pair, tiles, at, b, w, x, xs, sems):
    count, _, leaf = at.shape
    part = count // CHUNKS
    seg = lambda c: pl.ds(c * part * leaf, part * leaf)
    get_x = [copy(x_hbm.at[:, seg(c)], x.at[:, seg(c)], xs.at[c]) for c in range(CHUNKS)]
    get_w = copy(w_hbm, w, sems.at[0])
    total = scan_list(count, entries, lst, pair)
    acc[...] = jnp.zeros_like(acc)

    def prepare(l):
        left, right = feature_pair(x[:, lanes(l, leaf)])
        return left, right.T

    def keep(l, got):
        at[l], b[l] = got

    for c in range(CHUNKS):
        get_x[c].wait()
        grouped(part, 8, prepare, keep, c * part)
    get_w.wait()
    near_pairs(count, total, pair, at, b, w, acc, tiles)


def near_own(lst, x, w, count, entries, leaf):
    dim, cols = x.shape[0], w.shape[0]
    return pl.pallas_call(
        functools.partial(near_own_kernel, entries),
        grid_spec=pltpu.PrefetchScalarGridSpec(
            num_scalar_prefetch=1,
            grid=(1,),
            in_specs=[HBM] * 2,
            out_specs=VM,
            scratch_shapes=near_scratch(count, entries, leaf, dim, cols)
            + [pltpu.SemaphoreType.DMA((CHUNKS,)), pltpu.SemaphoreType.DMA((1,))],
        ),
        out_shape=jax.ShapeDtypeStruct((count + 1, cols, leaf), f32),
        compiler_params=pltpu.CompilerParams(vmem_limit_bytes=60 << 20),
        name="near_own",
    )(lst, x, w)


def two_sided(count, leaf, target_hbm, source_hbm, x, y, at, b, xs):
    part = count // CHUNKS
    seg = lambda c: pl.ds(c * part * leaf, part * leaf)
    gets = []
    for c in range(CHUNKS):
        gets.append(copy(source_hbm.at[:, seg(c)], y.at[:, seg(c)], xs.at[1, c]))
        gets.append(copy(target_hbm.at[:, seg(c)], x.at[:, seg(c)], xs.at[0, c]))

    def finish():
        def prepare(l):
            return feature_pair(x[:, lanes(l, leaf)])[0], feature_pair(y[:, lanes(l, leaf)])[1].T

        def keep(l, got):
            at[l], b[l] = got

        for c in range(CHUNKS):
            gets[2 * c].wait()
            gets[2 * c + 1].wait()
            grouped(part, 8, prepare, keep, c * part)

    return finish


def near_back_kernel(entries, low_hbm, x_hbm, wlow_hbm, w_hbm, after, out,
                     pair, tiles, at, b, w, x, y, acc, lf, lv, lst, xs, sems):
    count, _, leaf = at.shape
    get_list = copy(wlow_hbm.at[:, pl.ds(count * leaf, 128)], lf, sems.at[0])
    finish = two_sided(count, leaf, low_hbm, x_hbm, x, y, at, b, xs)
    get_w = copy(w_hbm, w, sems.at[1])
    get_list.wait()
    lv[...] = lf[...].astype(f32).astype(jnp.int32)
    put_list = copy(lv, lst, sems.at[2])
    acc[...] = jnp.zeros_like(acc)
    put_list.wait()
    total = scan_list(count, entries, lst, pair)
    finish()
    get_w.wait()
    near_pairs(count, total, pair, at, b, w, acc, tiles)

    def store(l, got):
        out[:, lanes(l, leaf)] = got.astype(out.dtype)

    grouped(count, 8, lambda l: acc[l], store)


def near_back(x_low, x, w_low, w, after, count, entries, leaf):
    dim, cols = x.shape[0], w.shape[0]
    return pl.pallas_call(
        functools.partial(near_back_kernel, entries),
        grid=(1,),
        in_specs=[ANY, HBM, ANY, HBM, HBM],
        out_specs=VM,
        scratch_shapes=near_scratch(count, entries, leaf, dim, cols)
        + [
            pltpu.VMEM((dim, count * leaf), bf16),
            pltpu.VMEM((count + 1, cols, leaf), f32),
            pltpu.VMEM((cols, 128), bf16),
            pltpu.VMEM((cols, 128), jnp.int32),
            pltpu.SMEM((cols, 128), jnp.int32),
            pltpu.SemaphoreType.DMA((2, CHUNKS)),
            pltpu.SemaphoreType.DMA((3,)),
        ],
        out_shape=jax.ShapeDtypeStruct((cols, count * leaf), bf16),
        compiler_params=pltpu.CompilerParams(vmem_limit_bytes=57 << 20),
        name="near_back",
    )(x_low, x, w_low, w, after)


def down_kernel(dims, pos_ref, lst, ridge, gathered, top_pick, low_hbm, x_hbm, wlow_hbm, own_hbm,
                top_hbm, terms_hbm, local_hbm, leaf_hbm, d_hbm, after, out,
                pair, tiles, at, b, w, x, y, acc, tb, terms, nb, lb, dt, tcoeff, tskel, value, xs, sems):
    count, leaf, rank, dim, cols, subtrees, entries = dims
    finish_features = two_sided(count, leaf, x_hbm, low_hbm, x, y, at, b, xs)
    get_w = copy(wlow_hbm, w, sems.at[0])
    get_acc = copy(own_hbm, acc, sems.at[1])
    pairs = ((top_hbm, tb), (terms_hbm, terms), (local_hbm, nb), (leaf_hbm, lb), (d_hbm, dt))
    gets = [copy(src, dst, sems.at[k + 2]) for k, (src, dst) in enumerate(pairs)]
    total = scan_list(count, entries, lst, pair)
    finish_features()
    get_w.wait()
    get_acc.wait()
    near_pairs(count, total, pair, at, b, w, acc, tiles)

    pos = pos_ref[0]
    depth = subtrees.bit_length() - 1
    for s in range(subtrees):
        tcoeff[:, lanes(subtrees - 1 + s, rank)] = gathered[s, :cols]
        tskel[:, lanes(subtrees - 1 + s, rank)] = gathered[s, cols:]
    for g in gets:
        g.wait()
    for d in range(depth - 1, 0, -1):

        def climb(j):
            both = lanes(2 * j + 1, rank, 2)
            sel = selector(top_pick[pl.ds(j, 1), :], 2 * rank)
            return dot(tcoeff[:, both], tb[j]).astype(bf16), dot(tskel[:, both], sel).astype(bf16)

        def climb_keep(j, got):
            tcoeff[:, lanes(j, rank)], tskel[:, lanes(j, rank)] = got

        grouped(2**d, 8, climb, climb_keep, 2**d - 1)

    def half(v):
        return (v.astype(f32) * 0.5).astype(bf16)

    top_terms = {}
    for d in range(depth, 0, -1):
        mine = pos >> (depth - d)
        other = mine ^ 1
        own_left = feature_pair(half(tskel[:, lanes(2**d - 1 + mine, rank)]))[0]
        sib_right = feature_pair(half(tskel[:, lanes(2**d - 1 + other, rank)]))[1]
        g = gauss(sib_right.T, own_left)
        top_terms[d] = dot(tcoeff[:, lanes(2**d - 1 + other, rank)], g)
    v = jnp.zeros((cols, rank), bf16)
    for d in range(1, depth + 1):
        parent = pos >> (depth - d + 1)
        down = dot(v, tb[2 ** (d - 1) - 1 + parent], 1, 1)
        right = ((pos >> (depth - d)) & 1) == 1
        v = (top_terms[d] + jnp.where(right, down[:, rank:], down[:, :rank])).astype(bf16)
    value[:, lanes(0, rank)] = v
    local_depth = count.bit_length() - 1
    for d in range(1, local_depth + 1):

        def descend(j):
            down = dot(value[:, lanes(j, rank)], nb[j], 1, 1)
            return (terms[:, lanes(2 * j, rank, 2)] + down).astype(bf16)

        def descend_keep(j, got):
            value[:, lanes(2 * j + 1, rank, 2)] = got

        grouped(2 ** (d - 1), 8, descend, descend_keep, 2 ** (d - 1) - 1)
    row = lax.broadcasted_iota(jnp.int32, (cols, leaf), 0)
    scale = jnp.zeros((cols, leaf), f32)
    for r in range(cols):
        scale = jnp.where(row == r, ridge[r], scale)

    def finish(l):
        far = dot(value[:, lanes(count - 1 + l, rank)], lb[l], 1, 1)
        return scale * dt[:, lanes(l, leaf)] + far + acc[l]

    def finish_keep(l, got):
        out[:, lanes(l, leaf)] = got

    grouped(count, 8, finish, finish_keep)


def downward(pos, lst, ridge, gathered, top_pick, x_low, x, w_low, n_own, top_basis, terms, local_basis, leaf_basis,
             dt, after, entries):
    count, leaf, rank = leaf_basis.shape
    dim, cols = x.shape[0], dt.shape[0]
    subtrees = gathered.shape[0]
    big = (top_basis, terms, local_basis, leaf_basis, dt)
    return pl.pallas_call(
        functools.partial(down_kernel, (count, leaf, rank, dim, cols, subtrees, entries)),
        grid_spec=pltpu.PrefetchScalarGridSpec(
            num_scalar_prefetch=3,
            grid=(1,),
            in_specs=[VM] * 2 + [ANY, HBM, ANY] + [HBM] * 7,
            out_specs=VM,
            scratch_shapes=near_scratch(count, entries, leaf, dim, cols)
            + [pltpu.VMEM((dim, count * leaf), bf16), pltpu.VMEM((count + 1, cols, leaf), f32)]
            + [pltpu.VMEM(a.shape, a.dtype) for a in big]
            + [
                pltpu.VMEM((cols, (2 * subtrees - 1) * rank), bf16),
                pltpu.VMEM((dim, (2 * subtrees - 1) * rank), bf16),
                pltpu.VMEM((cols, (2 * count - 1) * rank), bf16),
                pltpu.SemaphoreType.DMA((2, CHUNKS)),
                pltpu.SemaphoreType.DMA((7,)),
            ],
        ),
        out_shape=jax.ShapeDtypeStruct(dt.shape, f32),
        compiler_params=pltpu.CompilerParams(vmem_limit_bytes=57 << 20),
        name="downward",
    )(pos, lst, ridge, gathered, top_pick, x_low, x, w_low, n_own, *big, after)


def shards(points, direction, ridge, leaf_basis, local_basis, top_basis, leaf_pick, local_pick, top_pick, near_list):
    count, leaf, rank = leaf_basis.shape
    entries = near_list.shape[1]
    chips = lax.axis_size("chip")
    subtrees = lax.axis_size("leaf") * chips
    pos = (lax.axis_index("leaf") * chips + lax.axis_index("chip"))[None]
    upper = [(i, i + 1) for i in range(subtrees - 1)]
    lower = [(i + 1, i) for i in range(subtrees - 1)]

    xt, dt, ids = points.T, direction.T, near_list.T
    x_low = lax.ppermute(xt, AXES, upper)
    w, terms, spread, list_own, list_low = upward(
        pos, xt, dt, ids, leaf_pick, local_pick, leaf_basis, local_basis, subtrees
    )
    gathered = lax.all_to_all(spread, AXES, 0, 0)
    w_low = lax.ppermute(w, AXES, upper)
    n_own = near_own(list_own, xt, w, count, entries, leaf)
    back = near_back(x_low, xt, w_low, w, n_own, count, entries, leaf)
    returned = lax.ppermute(back, AXES, lower)
    out = downward(
        pos, list_low, ridge, gathered, top_pick, x_low, xt, w_low, n_own, top_basis, terms, local_basis, leaf_basis,
        dt, back, entries,
    )
    return (out + returned.astype(f32)).T


def solution(mesh):
    split = P(AXES, None)
    split3 = P(AXES, None, None)
    return jax.shard_map(
        shards,
        mesh=mesh,
        in_specs=(split, split, P(), split3, split3, P(), split, split, P(), split),
        out_specs=split,
        check_vma=False,
    )
```

time: 107 us -> 105 us (0.981)
  local copies, waits for them, and re-layouts: 6.17 us -> 2.98 us
  Pallas kernels: 86.5 us -> 87.8 us
    pallas_call x1, Pallas kernels: 9.91 us -> 27.3 us  [downward(): pl.pallas_call(functools.partial(down_kernel, (count, leaf, rank, dim, co...]
    pallas_call x3 -> x2, Pallas kernels: 59.3 us -> 44.6 us  [the longest x1 27.7 us: near_own(): pl.pallas_call(functools.partial(near_own_kernel, entries), grid_spec=plt...]
    another operation x3 -> x0, local copies, waits for them, and re-layouts: 2.49 us -> none  [class_list(): return jnp.stack(out, 0)]
    transpose x0 -> x1, other arithmetic: none -> 2.28 us  [shards(): return (out + returned.astype(f32)).T]
    pallas_call x1, Pallas kernels: 17.3 us -> 15.9 us  [upward(): pl.pallas_call(functools.partial(up_kernel, (count, leaf, rank, dim, cols...]
    convert_element_type x2 -> x0, other arithmetic: 1.36 us -> none  [the longest x1 0.71 us: class_list(): ones = inside.astype(jnp.int32)]
    unnamed x10 -> x6, local copies, waits for them, and re-layouts: 2.41 us -> 2.98 us
  transfers between devices with their start and end apart: 4 -> 4, of which waited for: 0 -> 0; matrix products, arithmetic and copies ran while one was open for 5% -> 0% of each run, Pallas kernels for 72% -> 84%
where the time goes in v4:
time: 105 us; the launch traced here: 104 us
  Pallas kernels  87.8 us (84%)
  starting transfers between devices  11.1 us (11%)
  local copies, waits for them, and re-layouts  2.98 us (3%)
  other arithmetic  2.28 us (2%)
    pallas_call x1, Pallas kernels, near_own(): pl.pallas_call(functools.partial(near_own_kernel, entries), grid_spec=plt...  27.7 us
    pallas_call x1, Pallas kernels, downward(): pl.pallas_call(functools.partial(down_kernel, (count, leaf, rank, dim, co...  27.3 us
    pallas_call x1, Pallas kernels, near_back(): pl.pallas_call(functools.partial(near_back_kernel, entries), grid=(1,), i...  16.9 us
    pallas_call x1, Pallas kernels, upward(): pl.pallas_call(functools.partial(up_kernel, (count, leaf, rank, dim, cols...  15.9 us
    all_to_all x1, starting transfers between devices, shards(): gathered = lax.all_to_all(spread, AXES, 0, 0)  7.05 us
    unnamed x6, local copies, waits for them, and re-layouts  2.98 us
    transpose x1, other arithmetic, shards(): return (out + returned.astype(f32)).T  2.28 us
  transfers between devices with their start and end apart: 4, of which 0 were waited for; matrix products, arithmetic and copies ran while one was open for 0% of the time, Pallas kernels for 84%

profile of v4, /device:TPU:31, one launch (start us, length us, event | category | flops | bytes accessed | tf_op | source)
XLA Modules:
  0.0 104.3 jit_solution(4448187087052047079)
XLA Ops:
  0.0 1.3 %collective-permute-start = (bf16[64,16384]{1,0:T(8,128)(2,1)}, bf16[64,16384]{1,0:T(8,128)(2,1)S(1)}, u32[]{:S(2)}, u32[]{:S(2)}) collective-permute-start(bf16[64,16384]{1,0:T(8,128)(2,1)} %bitcast.6), channel_id=1, source_target_pairs={{0,1},{1,2},{2,3},{3,4},{4,5},{5,6},{6,7},{7,8},{8,9},{9,10},{10,1... | collective-permute-start | bytes 6291464 | tf_op jit(solution)/shard_map/ppermute | solution.py:527
  1.3 15.9 %upward.1 = (bf16[16,16512]{1,0:T(8,128)(2,1)}, f32[16,16128]{1,0:T(8,128)}, bf16[32,80,128]{2,1,0:T(8,128)(2,1)}, s32[16,64]{1,0:T(8,128)}, s32[16,64]{1,0:T(8,128)}) custom-call(s32[1]{0:T(128)} %bitcast.pos_ref, bf16[64,16384]{1,0:T(8,128)(2,1)} %bitcast.7, f32[16,16384]{1,0:T(8,128)} %bitcast.11, s32[10,64]{1,0:T(8,128)} %bitcast.13, ...), custom_call_target="tpu_custom_call" | custom-call | tf_op jit(solution)/shard_map/upward/pallas_call | solution.py:211
  17.2 7.1 %all-to-all-start = ((bf16[32,80,128]{2,1,0:T(8,128)(2,1)}), bf16[32,80,128]{2,1,0:T(8,128)(2,1)S(1)}, u32[]{:S(2)}, u32[]{:S(2)}) async-start(bf16[32,80,128]{2,1,0:T(8,128)(2,1)} %get-tuple-element.11), calls=%async_computation | async-start | bytes 1310720 | tf_op jit(solution)/shard_map/all_to_all | solution.py:531
  24.3 1.3 %collective-permute-start.1 = (bf16[16,16512]{1,0:T(8,128)(2,1)}, bf16[16,16512]{1,0:T(8,128)(2,1)S(1)}, u32[]{:S(2)}, u32[]{:S(2)}) collective-permute-start(bf16[16,16512]{1,0:T(8,128)(2,1)} %get-tuple-element.12.w_hbm), channel_id=1, source_target_pairs={{0,1},{1,2},{2,3},{3,4},{4,5},{5,6},{6,7},{7,8},{8,9},{9,10},{10,1... | collective-permute-start | bytes 1585160 | tf_op jit(solution)/shard_map/ppermute | solution.py:532
  25.6 27.7 %near_own.1.after.own_hbm = f32[65,16,256]{2,1,0:T(8,128)} custom-call(s32[16,64]{1,0:T(8,128)} %get-tuple-element.13.lst, bf16[64,16384]{1,0:T(8,128)(2,1)} %bitcast.8, bf16[16,16512]{1,0:T(8,128)(2,1)} %get-tuple-element.12.w_hbm), custom_call_target="tpu_custom_call" | custom-call | tf_op jit(solution)/shard_map/near_own/pallas_call | solution.py:325
  53.3 0.0 collective-permute-done.1.wlow_hbm
  53.3 0.0 copy-start.2
  53.3 0.0 collective-permute-done.low_hbm
  53.3 0.8 copy-done.2
  54.1 0.0 copy-start
  54.1 1.3 %copy-done = bf16[64,16384]{1,0:T(8,128)(2,1)} copy-done((bf16[64,16384]{1,0:T(8,128)(2,1)}, bf16[64,16384]{1,0:T(8,128)(2,1)S(1)}, u32[]{:S(2)}) %copy-start) | copy-done | bytes 2097176
  55.4 16.9 %near_back.1.after = bf16[16,16384]{1,0:T(8,128)(2,1)} custom-call(bf16[64,16384]{1,0:T(8,128)(2,1)} %copy-done, bf16[64,16384]{1,0:T(8,128)(2,1)} %bitcast.9, bf16[16,16512]{1,0:T(8,128)(2,1)} %copy-done.2, bf16[16,16512]{1,0:T(8,128)(2,1)} %get-tuple-element.12.w_hbm, f32[65,16,256]{2,1,0:T(8,128)} %near_own.1.after.own_hbm), custom_call_target="tpu_custom_call" | custom-call | tf_op jit(solution)/shard_map/near_back/pallas_call | solution.py:388
  72.4 1.5 %collective-permute-start.2 = (bf16[16,16384]{1,0:T(8,128)(2,1)}, bf16[16,16384]{1,0:T(8,128)(2,1)S(1)}, u32[]{:S(2)}, u32[]{:S(2)}) collective-permute-start(bf16[16,16384]{1,0:T(8,128)(2,1)} %near_back.1.after), channel_id=1, source_target_pairs={{1,0},{2,1},{3,2},{4,3},{5,4},{6,5},{7,6},{8,7},{9,8},{10,9},{11,1... | collective-permute-start | bytes 1572872 | tf_op jit(solution)/shard_map/ppermute | solution.py:535
  73.9 0.0 all-to-all-done.gathered
  73.9 0.0 copy-start.1
  73.9 0.8 copy-done.1
  74.8 27.3 %downward.1 = f32[16,16384]{1,0:T(8,128)} custom-call(s32[1]{0:T(128)} %bitcast.pos_ref, s32[16,64]{1,0:T(8,128)} %get-tuple-element.10.lst, f32[16]{0:T(128)} %ridge.1, bf16[32,80,128]{2,1,0:T(8,128)(2,1)} %copy-done.1, s32[31,128]{1,0:T(8,128)} %top_pick.1, bf16[64,16384]{1,0:T(8,128)(2,1)} %copy-done, bf16[64,16384]{1,0:T(8,128)(2,1)} %bitcast.10, ...), custom_call_target="tpu_custom_call" | custom-call | tf_op jit(solution)/shard_map/downward/pallas_call | solution.py:493
  102.0 0.0 collective-permute-done.2
  102.0 2.3 %add_bitcast_fusion = f32[16384,16]{0,1:T(8,128)} fusion(f32[16,16384]{1,0:T(8,128)} %downward.1, bf16[16,16384]{1,0:T(8,128)(2,1)S(1)} %collective-permute-done.2), kind=kLoop, calls=%fused_computation | loop fusion | flops 524288 | bytes 2621440 | tf_op jit(solution)/shard_map/transpose | solution.py:540
Async XLA Ops:
  0.0 53.3 %collective-permute-start = (bf16[64,16384]{1,0:T(8,128)(2,1)}, bf16[64,16384]{1,0:T(8,128)(2,1)S(1)}, u32[]{:S(2)}, u32[]{:S(2)}) collective-permute-start(bf16[64,16384]{1,0:T(8,128)(2,1)} %bitcast.6), channel_id=1, source_target_pairs={{0,1},{1,2},{2,3},{3,4},{4,5},{5,6},{6,7},{7,8},{8,9},{9,10},{10,1... | collective-permute-start | bytes 6291464 | tf_op jit(solution)/shard_map/ppermute | solution.py:527
  17.2 56.7 %all-to-all-start = ((bf16[32,80,128]{2,1,0:T(8,128)(2,1)}), bf16[32,80,128]{2,1,0:T(8,128)(2,1)S(1)}, u32[]{:S(2)}, u32[]{:S(2)}) async-start(bf16[32,80,128]{2,1,0:T(8,128)(2,1)} %get-tuple-element.11), calls=%async_computation | async-start | bytes 1310720 | tf_op jit(solution)/shard_map/all_to_all | solution.py:531
  24.3 29.0 %collective-permute-start.1 = (bf16[16,16512]{1,0:T(8,128)(2,1)}, bf16[16,16512]{1,0:T(8,128)(2,1)S(1)}, u32[]{:S(2)}, u32[]{:S(2)}) collective-permute-start(bf16[16,16512]{1,0:T(8,128)(2,1)} %get-tuple-element.12.w_hbm), channel_id=1, source_target_pairs={{0,1},{1,2},{2,3},{3,4},{4,5},{5,6},{6,7},{7,8},{8,9},{9,10},{10,1... | collective-permute-start | bytes 1585160 | tf_op jit(solution)/shard_map/ppermute | solution.py:532
  53.3 0.8 copy-start.2
  54.1 1.3 %copy-start = (bf16[64,16384]{1,0:T(8,128)(2,1)}, bf16[64,16384]{1,0:T(8,128)(2,1)S(1)}, u32[]{:S(2)}) copy-start(bf16[64,16384]{1,0:T(8,128)(2,1)S(1)} %collective-permute-done.low_hbm) | copy-start | bytes 6291460
  72.4 29.6 %collective-permute-start.2 = (bf16[16,16384]{1,0:T(8,128)(2,1)}, bf16[16,16384]{1,0:T(8,128)(2,1)S(1)}, u32[]{:S(2)}, u32[]{:S(2)}) collective-permute-start(bf16[16,16384]{1,0:T(8,128)(2,1)} %near_back.1.after), channel_id=1, source_target_pairs={{1,0},{2,1},{3,2},{4,3},{5,4},{6,5},{7,6},{8,7},{9,8},{10,9},{11,1... | collective-permute-start | bytes 1572872 | tf_op jit(solution)/shard_map/ppermute | solution.py:535
  73.9 0.8 copy-start.1

commit v5 on v4

--- a/solution.py
+++ b/solution.py
@@ -69,19 +69,20 @@
     return jnp.exp2(s * SCALE).astype(bf16)
 
 
-def grouped(count, group, compute, store, start=0):
+def grouped(count, group, compute, store, start=0, also=None, carry=0):
     group = min(group, count)
 
     def body(t, carry):
         got = [compute(start + t * group + u) for u in range(group)]
         for u in range(group):
             store(start + t * group + u, got[u])
+            if also is not None:
+                carry = also(start + t * group + u, carry)
         return carry
 
     if count == group:
-        body(0, 0)
-    else:
-        lax.fori_loop(0, count // group, body, 0)
+        return body(0, carry)
+    return lax.fori_loop(0, count // group, body, carry)
 
 
 def lanes(start, width, number=1):
@@ -91,7 +92,7 @@
 
 
 CHUNKS = 4
-PAIRS = 8
+PAIRS = 16
 
 
 def class_list(ids, low, count):
@@ -111,29 +112,38 @@
 
 
 def up_kernel(dims, pos_ref, x_hbm, d_hbm, ids, leaf_pick, local_pick, leaf_hbm, local_hbm,
-              w_hbm, terms_hbm, spread, list_own, list_low,
-              xt, dt, at, wt, terms, lb, nb, coeff, skel, tiles, xs, ls, ms):
+              w_hbm, terms_hbm, spread, list_low, acc,
+              pair, big, at, b, wt, xt, dt, terms, lb, nb, coeff, skel, tiles, lv, lst, xs, ls, ms):
     count, leaf, rank, dim, cols = dims
+    entries = ids.shape[0]
     part = count // CHUNKS
     seg = lambda c: pl.ds(c * part * leaf, part * leaf)
     own = lambda c: pl.ds(c * part, part)
     get_x = [copy(x_hbm.at[:, seg(c)], xt.at[:, seg(c)], xs.at[c]) for c in range(CHUNKS)]
     get_d = copy(d_hbm, dt, ms.at[0])
-    get_leaf = [copy(leaf_hbm.at[own(c)], lb.at[own(c)], ls.at[c]) for c in range(CHUNKS)]
-    get_local = copy(local_hbm, nb, ms.at[1])
     pos = pos_ref[0]
     table = ids[...]
-    list_own[...] = class_list(table, pos * count, count)
+    put_list = put_class(table, pos * count, count, lv, lst, ms.at[4])
     list_low[...] = class_list(table, (pos - 1) * count, count)
-    wt[:, pl.ds(count * leaf, 128)] = jnp.zeros((cols, 128), bf16)
-    wt[:, pl.ds(count * leaf, count)] = class_list(table, (pos + 1) * count, count).astype(f32).astype(bf16)
+    acc[...] = jnp.zeros_like(acc)
+
+    def prepare(l):
+        left, right = feature_pair(xt[:, lanes(l, leaf)])
+        return left, right.T
 
     def keep(l, got):
-        at[l] = got
-
+        at[l], b[l] = got
+
+    total = 0
     for c in range(CHUNKS):
         get_x[c].wait()
-        grouped(part, 8, lambda l: feature_pair(xt[:, lanes(l, leaf)])[0], keep, c * part)
+        if c == 0:
+            put_list.wait()
+        if c == 1:
+            get_leaf = [copy(leaf_hbm.at[own(k)], lb.at[own(k)], ls.at[k]) for k in range(CHUNKS)]
+            get_local = copy(local_hbm, nb, ms.at[1])
+        total = grouped(part, 8, prepare, keep, c * part, scan_leaf(count, entries, lst, pair), total)
+    end_list(count, pair, total)
     get_d.wait()
     for c in range(CHUNKS):
         wt[:, seg(c)] = dt[:, seg(c)].astype(bf16)
@@ -164,7 +174,7 @@
         def climb_keep(j, got):
             coeff[:, lanes(j, rank)], skel[:, lanes(j, rank)] = got
 
-        grouped(2 ** (d - 1), 8, climb, climb_keep, up)
+        grouped(2 ** (d - 1), 16, climb, climb_keep, up)
     root_c, root_s = coeff[:, :rank], skel[:dim, :rank]
     for s in range(spread.shape[0]):
         spread[s, :cols, :] = root_c
@@ -200,14 +210,21 @@
 
     lax.fori_loop(0, count // (2 * PAIRS), body, 0)
     puts.append(copy(terms, terms_hbm, ms.at[3]))
+    near_pairs(count, total, pair, at, b, wt, acc, big)
     for p in puts:
         p.wait()
+
+
+def put_class(table, low, count, lv, lst, sem):
+    lv[...] = jnp.zeros_like(lv)
+    lv[:, :count] = class_list(table, low, count)
+    return copy(lv, lst, sem)
 
 
 def upward(pos, xt, dt, ids, leaf_pick, local_pick, leaf_basis, local_basis, subtrees):
     count, leaf, rank = leaf_basis.shape
     dim, cols = xt.shape[0], dt.shape[0]
-    width = count * leaf + 128
+    entries = ids.shape[0]
     return pl.pallas_call(
         functools.partial(up_kernel, (count, leaf, rank, dim, cols)),
         grid_spec=pltpu.PrefetchScalarGridSpec(
@@ -215,44 +232,46 @@
             grid=(1,),
             in_specs=[HBM, HBM, VM, VM, VM, HBM, HBM],
             out_specs=[HBM, HBM, VM, VM, VM],
-            scratch_shapes=[
-                pltpu.VMEM(xt.shape, bf16),
+            scratch_shapes=near_scratch(count, entries, leaf, dim, cols)
+            + [
                 pltpu.VMEM(dt.shape, f32),
-                pltpu.VMEM((count, FEAT, leaf), bf16),
-                pltpu.VMEM((cols, width), bf16),
                 pltpu.VMEM((cols, (2 * count - 2) * rank), f32),
                 pltpu.VMEM(leaf_basis.shape, bf16),
                 pltpu.VMEM(local_basis.shape, bf16),
                 pltpu.VMEM((cols, (2 * count - 1) * rank), bf16),
                 pltpu.VMEM((FEAT, (2 * count - 1) * rank), bf16),
                 pltpu.VMEM((2 * PAIRS, rank, rank), bf16),
+                pltpu.VMEM((16, 128), jnp.int32),
+                pltpu.SMEM((16, 128), jnp.int32),
                 pltpu.SemaphoreType.DMA((CHUNKS,)),
                 pltpu.SemaphoreType.DMA((CHUNKS,)),
-                pltpu.SemaphoreType.DMA((4,)),
+                pltpu.SemaphoreType.DMA((5,)),
             ],
         ),
         out_shape=[
-            jax.ShapeDtypeStruct((cols, width), bf16),
+            jax.ShapeDtypeStruct((cols, count * leaf), bf16),
             jax.ShapeDtypeStruct((cols, (2 * count - 2) * rank), f32),
             jax.ShapeDtypeStruct((subtrees, cols + dim, rank), bf16),
             jax.ShapeDtypeStruct((16, count), jnp.int32),
-            jax.ShapeDtypeStruct((16, count), jnp.int32),
+            jax.ShapeDtypeStruct((count + 1, cols, leaf), f32),
         ],
         compiler_params=pltpu.CompilerParams(vmem_limit_bytes=60 << 20),
         name="upward",
     )(pos, xt, dt, ids, leaf_pick, local_pick, leaf_basis, local_basis)
 
 
-def scan_list(count, entries, lst, pair):
+def scan_leaf(count, entries, lst, pair):
     def scan(i, pos):
         for e in range(entries):
             pair[pos + e] = i * count + lst[e, i]
         return pos + lst[entries, i]
 
-    total = lax.fori_loop(0, count, scan, 0)
+    return scan
+
+
+def end_list(count, pair, total):
     for u in range(3 * GROUP):
         pair[total + u] = count * count
-    return total
 
 
 def near_pairs(count, total, pair, at, b, w, acc, tiles):
@@ -292,50 +311,9 @@
         pltpu.VMEM((2 * GROUP, leaf, leaf), bf16),
         pltpu.VMEM((count, FEAT, leaf), bf16),
         pltpu.VMEM((count, leaf, FEAT), bf16),
-        pltpu.VMEM((cols, count * leaf + 128), bf16),
+        pltpu.VMEM((cols, count * leaf), bf16),
         pltpu.VMEM((dim, count * leaf), bf16),
     ]
-
-
-def near_own_kernel(entries, lst, x_hbm, w_hbm, acc, pair, tiles, at, b, w, x, xs, sems):
-    count, _, leaf = at.shape
-    part = count // CHUNKS
-    seg = lambda c: pl.ds(c * part * leaf, part * leaf)
-    get_x = [copy(x_hbm.at[:, seg(c)], x.at[:, seg(c)], xs.at[c]) for c in range(CHUNKS)]
-    get_w = copy(w_hbm, w, sems.at[0])
-    total = scan_list(count, entries, lst, pair)
-    acc[...] = jnp.zeros_like(acc)
-
-    def prepare(l):
-        left, right = feature_pair(x[:, lanes(l, leaf)])
-        return left, right.T
-
-    def keep(l, got):
-        at[l], b[l] = got
-
-    for c in range(CHUNKS):
-        get_x[c].wait()
-        grouped(part, 8, prepare, keep, c * part)
-    get_w.wait()
-    near_pairs(count, total, pair, at, b, w, acc, tiles)
-
-
-def near_own(lst, x, w, count, entries, leaf):
-    dim, cols = x.shape[0], w.shape[0]
-    return pl.pallas_call(
-        functools.partial(near_own_kernel, entries),
-        grid_spec=pltpu.PrefetchScalarGridSpec(
-            num_scalar_prefetch=1,
-            grid=(1,),
-            in_specs=[HBM] * 2,
-            out_specs=VM,
-            scratch_shapes=near_scratch(count, entries, leaf, dim, cols)
-            + [pltpu.SemaphoreType.DMA((CHUNKS,)), pltpu.SemaphoreType.DMA((1,))],
-        ),
-        out_shape=jax.ShapeDtypeStruct((count + 1, cols, leaf), f32),
-        compiler_params=pltpu.CompilerParams(vmem_limit_bytes=60 << 20),
-        name="near_own",
-    )(lst, x, w)
 
 
 def two_sided(count, leaf, target_hbm, source_hbm, x, y, at, b, xs):
@@ -346,34 +324,36 @@
         gets.append(copy(source_hbm.at[:, seg(c)], y.at[:, seg(c)], xs.at[1, c]))
         gets.append(copy(target_hbm.at[:, seg(c)], x.at[:, seg(c)], xs.at[0, c]))
 
-    def finish():
+    def finish(also):
         def prepare(l):
             return feature_pair(x[:, lanes(l, leaf)])[0], feature_pair(y[:, lanes(l, leaf)])[1].T
 
         def keep(l, got):
             at[l], b[l] = got
 
+        total = 0
         for c in range(CHUNKS):
             gets[2 * c].wait()
             gets[2 * c + 1].wait()
-            grouped(part, 8, prepare, keep, c * part)
+            total = grouped(part, 8, prepare, keep, c * part, also, total)
+        return total
 
     return finish
 
 
-def near_back_kernel(entries, low_hbm, x_hbm, wlow_hbm, w_hbm, after, out,
-                     pair, tiles, at, b, w, x, y, acc, lf, lv, lst, xs, sems):
+def near_back_kernel(pos_ref, ids, low_hbm, x_hbm, w_hbm, out,
+                     pair, tiles, at, b, w, x, y, acc, lv, lst, xs, sems):
     count, _, leaf = at.shape
-    get_list = copy(wlow_hbm.at[:, pl.ds(count * leaf, 128)], lf, sems.at[0])
+    entries = ids.shape[0]
     finish = two_sided(count, leaf, low_hbm, x_hbm, x, y, at, b, xs)
-    get_w = copy(w_hbm, w, sems.at[1])
-    get_list.wait()
-    lv[...] = lf[...].astype(f32).astype(jnp.int32)
-    put_list = copy(lv, lst, sems.at[2])
+    get_w = copy(w_hbm, w, sems.at[0])
+    pos = pos_ref[0]
+    low = jnp.where(pos == 0, -(1 << 24), pos * count)
+    put_list = put_class(ids[...], low, count, lv, lst, sems.at[1])
     acc[...] = jnp.zeros_like(acc)
     put_list.wait()
-    total = scan_list(count, entries, lst, pair)
-    finish()
+    total = finish(scan_leaf(count, entries, lst, pair))
+    end_list(count, pair, total)
     get_w.wait()
     near_pairs(count, total, pair, at, b, w, acc, tiles)
 
@@ -383,27 +363,30 @@
     grouped(count, 8, lambda l: acc[l], store)
 
 
-def near_back(x_low, x, w_low, w, after, count, entries, leaf):
+def near_back(pos, ids_low, x_low, x, w, count, leaf):
     dim, cols = x.shape[0], w.shape[0]
+    entries = ids_low.shape[0]
     return pl.pallas_call(
-        functools.partial(near_back_kernel, entries),
-        grid=(1,),
-        in_specs=[ANY, HBM, ANY, HBM, HBM],
-        out_specs=VM,
-        scratch_shapes=near_scratch(count, entries, leaf, dim, cols)
-        + [
-            pltpu.VMEM((dim, count * leaf), bf16),
-            pltpu.VMEM((count + 1, cols, leaf), f32),
-            pltpu.VMEM((cols, 128), bf16),
-            pltpu.VMEM((cols, 128), jnp.int32),
-            pltpu.SMEM((cols, 128), jnp.int32),
-            pltpu.SemaphoreType.DMA((2, CHUNKS)),
-            pltpu.SemaphoreType.DMA((3,)),
-        ],
+        near_back_kernel,
+        grid_spec=pltpu.PrefetchScalarGridSpec(
+            num_scalar_prefetch=1,
+            grid=(1,),
+            in_specs=[VM, ANY, HBM, HBM],
+            out_specs=VM,
+            scratch_shapes=near_scratch(count, entries, leaf, dim, cols)
+            + [
+                pltpu.VMEM((dim, count * leaf), bf16),
+                pltpu.VMEM((count + 1, cols, leaf), f32),
+                pltpu.VMEM((16, 128), jnp.int32),
+                pltpu.SMEM((16, 128), jnp.int32),
+                pltpu.SemaphoreType.DMA((2, CHUNKS)),
+                pltpu.SemaphoreType.DMA((2,)),
+            ],
+        ),
         out_shape=jax.ShapeDtypeStruct((cols, count * leaf), bf16),
-        compiler_params=pltpu.CompilerParams(vmem_limit_bytes=57 << 20),
+        compiler_params=pltpu.CompilerParams(vmem_limit_bytes=52 << 20),
         name="near_back",
-    )(x_low, x, w_low, w, after)
+    )(pos, ids_low, x_low, x, w)
 
 
 def down_kernel(dims, pos_ref, lst, ridge, gathered, top_pick, low_hbm, x_hbm, wlow_hbm, own_hbm,
@@ -414,9 +397,9 @@
     get_w = copy(wlow_hbm, w, sems.at[0])
     get_acc = copy(own_hbm, acc, sems.at[1])
     pairs = ((top_hbm, tb), (terms_hbm, terms), (local_hbm, nb), (leaf_hbm, lb), (d_hbm, dt))
+    total = finish_features(scan_leaf(count, entries, lst, pair))
+    end_list(count, pair, total)
     gets = [copy(src, dst, sems.at[k + 2]) for k, (src, dst) in enumerate(pairs)]
-    total = scan_list(count, entries, lst, pair)
-    finish_features()
     get_w.wait()
     get_acc.wait()
     near_pairs(count, total, pair, at, b, w, acc, tiles)
@@ -509,7 +492,7 @@
             ],
         ),
         out_shape=jax.ShapeDtypeStruct(dt.shape, f32),
-        compiler_params=pltpu.CompilerParams(vmem_limit_bytes=57 << 20),
+        compiler_params=pltpu.CompilerParams(vmem_limit_bytes=52 << 20),
         name="downward",
     )(pos, lst, ridge, gathered, top_pick, x_low, x, w_low, n_own, *big, after)
 
@@ -525,13 +508,13 @@
 
     xt, dt, ids = points.T, direction.T, near_list.T
     x_low = lax.ppermute(xt, AXES, upper)
-    w, terms, spread, list_own, list_low = upward(
+    ids_low = lax.ppermute(ids, AXES, upper)
+    w, terms, spread, list_low, n_own = upward(
         pos, xt, dt, ids, leaf_pick, local_pick, leaf_basis, local_basis, subtrees
     )
     gathered = lax.all_to_all(spread, AXES, 0, 0)
     w_low = lax.ppermute(w, AXES, upper)
-    n_own = near_own(list_own, xt, w, count, entries, leaf)
-    back = near_back(x_low, xt, w_low, w, n_own, count, entries, leaf)
+    back = near_back(pos, ids_low, x_low, xt, w, count, leaf)
     returned = lax.ppermute(back, AXES, lower)
     out = downward(
         pos, list_low, ridge, gathered, top_pick, x_low, xt, w_low, n_own, top_basis, terms, local_basis, leaf_basis,

time: 105 us -> 110 us (1.048)
  the two profiles are of different devices: /device:TPU:31 before, /device:TPU:17 now
where the time goes in v5:
time: 110 us; the launch traced here: 111 us
  Pallas kernels  71.2 us (65%)
  starting transfers between devices  36.4 us (33%)
  other arithmetic  2.32 us (2%)
    pallas_call x1, Pallas kernels, upward(): pl.pallas_call(functools.partial(up_kernel, (count, leaf, rank, dim, cols...  30.5 us
    pallas_call x1, Pallas kernels, downward(): pl.pallas_call(functools.partial(down_kernel, (count, leaf, rank, dim, co...  24.2 us
    pallas_call x1, Pallas kernels, near_back(): pl.pallas_call(near_back_kernel, grid_spec=pltpu.PrefetchScalarGridSpec(n...  16.5 us
    ppermute x1, starting transfers between devices, shards(): returned = lax.ppermute(back, AXES, lower)  14.4 us
    all_to_all x1, starting transfers between devices, shards(): gathered = lax.all_to_all(spread, AXES, 0, 0)  13 us
    ppermute x1, starting transfers between devices, shards(): x_low = lax.ppermute(xt, AXES, upper)  3.67 us
    ppermute x1, starting transfers between devices, shards(): ids_low = lax.ppermute(ids, AXES, upper)  3.34 us
    transpose x1, other arithmetic, shards(): return (out + returned.astype(f32)).T  2.32 us
  transfers between devices with their start and end apart: 5, of which 0 were waited for; matrix products, arithmetic and copies ran while one was open for 0% of the time, Pallas kernels for 64%

profile of v5, /device:TPU:17, one launch (start us, length us, event | category | flops | bytes accessed | tf_op | source)
XLA Modules:
  0.0 111.2 jit_solution(12482336978242046738)
XLA Ops:
  0.0 3.7 %collective-permute-start = (bf16[64,16384]{1,0:T(8,128)(2,1)}, bf16[64,16384]{1,0:T(8,128)(2,1)}, u32[]{:S(2)}, u32[]{:S(2)}) collective-permute-start(bf16[64,16384]{1,0:T(8,128)(2,1)} %bitcast.6), channel_id=1, source_target_pairs={{0,1},{1,2},{2,3},{3,4},{4,5},{5,6},{6,7},{7,8},{8,9},{9,10},{10,1... | collective-permute-start | bytes 6291464 | tf_op jit(solution)/shard_map/ppermute | solution.py:510
  3.7 0.0 copy-start.4
  3.7 30.5 %upward.1 = (bf16[16,16384]{1,0:T(8,128)(2,1)}, f32[16,16128]{1,0:T(8,128)}, bf16[32,80,128]{2,1,0:T(8,128)(2,1)}, s32[16,64]{1,0:T(8,128)}, f32[65,16,256]{2,1,0:T(8,128)}) custom-call(s32[1]{0:T(128)} %bitcast.pos_ref, bf16[64,16384]{1,0:T(8,128)(2,1)} %bitcast.7, f32[16,16384]{1,0:T(8,128)} %bitcast.10, s32[10,64]{1,0:T(8,128)} %bitcast.12, ...), custom_call_target="tpu_custom_call" | custom-call | tf_op jit(solution)/shard_map/upward/pallas_call | solution.py:228
  34.2 13.0 %all-to-all-start = ((bf16[32,80,128]{2,1,0:T(8,128)(2,1)}), bf16[32,80,128]{2,1,0:T(8,128)(2,1)S(1)}, u32[]{:S(2)}, u32[]{:S(2)}) async-start(bf16[32,80,128]{2,1,0:T(8,128)(2,1)} %get-tuple-element.11), calls=%async_computation | async-start | bytes 1310720 | tf_op jit(solution)/shard_map/all_to_all | solution.py:515
  47.2 0.0 copy-done.4
  47.2 3.3 %collective-permute-start.2 = (s32[10,64]{1,0:T(8,128)S(1)}, s32[10,64]{1,0:T(8,128)S(1)}, u32[]{:S(2)}, u32[]{:S(2)}) collective-permute-start(s32[10,64]{1,0:T(8,128)S(1)} %bitcast.13), channel_id=1, source_target_pairs={{0,1},{1,2},{2,3},{3,4},{4,5},{5,6},{6,7},{7,8},{8,9},{9,10},{10,1... | collective-permute-start | bytes 7688 | tf_op jit(solution)/shard_map/ppermute | solution.py:511
  50.6 0.0 copy-start.3
  50.6 2.1 %collective-permute-start.1 = (bf16[16,16384]{1,0:T(8,128)(2,1)}, bf16[16,16384]{1,0:T(8,128)(2,1)S(1)}, u32[]{:S(2)}, u32[]{:S(2)}) collective-permute-start(bf16[16,16384]{1,0:T(8,128)(2,1)} %get-tuple-element.12.w_hbm), channel_id=1, source_target_pairs={{0,1},{1,2},{2,3},{3,4},{4,5},{5,6},{6,7},{7,8},{8,9},{9,10},{10,1... | collective-permute-start | bytes 1572872 | tf_op jit(solution)/shard_map/ppermute | solution.py:516
  52.6 0.0 collective-permute-done.2.ids
  52.6 0.0 collective-permute-done.low_hbm
  52.7 0.0 copy-start
  52.7 1.1 copy-done
  53.7 0.0 copy-start.1
  53.7 0.0 copy-start.2
  53.7 16.5 %near_back.1.after = bf16[16,16384]{1,0:T(8,128)(2,1)S(1)} custom-call(s32[1]{0:T(128)} %bitcast.pos_ref, s32[10,64]{1,0:T(8,128)S(1)} %collective-permute-done.2.ids, bf16[64,16384]{1,0:T(8,128)(2,1)} %collective-permute-done.low_hbm, bf16[64,16384]{1,0:T(8,128)(2,1)} %bitcast.8, bf16[16,16384]{1,0:T(8,128)(2,1)S(1)} %copy-done), custom_call_target="tpu_custom_call" | custom-call | tf_op jit(solution)/shard_map/near_back/pallas_call | solution.py:369
  70.2 14.4 %collective-permute-start.3 = (bf16[16,16384]{1,0:T(8,128)(2,1)S(1)}, bf16[16,16384]{1,0:T(8,128)(2,1)S(1)}, u32[]{:S(2)}, u32[]{:S(2)}) collective-permute-start(bf16[16,16384]{1,0:T(8,128)(2,1)S(1)} %near_back.1.after), channel_id=1, source_target_pairs={{1,0},{2,1},{3,2},{4,3},{5,4},{6,5},{7,6},{8,7},{9,8},{10,9},{11,1... | collective-permute-start | bytes 1572872 | tf_op jit(solution)/shard_map/ppermute | solution.py:518
  84.6 0.0 collective-permute-done.1.wlow_hbm
  84.6 0.0 all-to-all-done.gathered
  84.6 0.0 copy-done.3
  84.6 0.0 copy-done.1
  84.6 0.0 copy-done.2
  84.6 24.2 %downward.1 = f32[16,16384]{1,0:T(8,128)} custom-call(s32[1]{0:T(128)} %bitcast.pos_ref, s32[16,64]{1,0:T(8,128)S(1)} %copy-done.2, f32[16]{0:T(128)S(1)} %copy-done.3, bf16[32,80,128]{2,1,0:T(8,128)(2,1)S(1)} %all-to-all-done.gathered, s32[31,128]{1,0:T(8,128)S(1)} %copy-done.1, bf16[64,16384]{1,0:T(8,128)(2,1)} %collective-permute-done.low_hbm, ...), custom_call_target="tpu_custom_call" | custom-call | tf_op jit(solution)/shard_map/downward/pallas_call | solution.py:476
  108.9 0.0 collective-permute-done.3
  108.9 2.3 %add_bitcast_fusion = f32[16384,16]{0,1:T(8,128)} fusion(f32[16,16384]{1,0:T(8,128)} %downward.1, bf16[16,16384]{1,0:T(8,128)(2,1)S(1)} %collective-permute-done.3), kind=kLoop, calls=%fused_computation | loop fusion | flops 524288 | bytes 2621440 | tf_op jit(solution)/shard_map/transpose | solution.py:523
Async XLA Ops:
  0.0 52.6 %collective-permute-start = (bf16[64,16384]{1,0:T(8,128)(2,1)}, bf16[64,16384]{1,0:T(8,128)(2,1)}, u32[]{:S(2)}, u32[]{:S(2)}) collective-permute-start(bf16[64,16384]{1,0:T(8,128)(2,1)} %bitcast.6), channel_id=1, source_target_pairs={{0,1},{1,2},{2,3},{3,4},{4,5},{5,6},{6,7},{7,8},{8,9},{9,10},{10,1... | collective-permute-start | bytes 6291464 | tf_op jit(solution)/shard_map/ppermute | solution.py:510
  3.7 43.5 %copy-start.4 = (s32[64,10]{0,1:T(8,128)S(1)}, s32[64,10]{0,1:T(8,128)}, u32[]{:S(2)}) copy-start(s32[64,10]{0,1:T(8,128)} %param.19) | copy-start | bytes 7684
  34.2 50.4 %all-to-all-start = ((bf16[32,80,128]{2,1,0:T(8,128)(2,1)}), bf16[32,80,128]{2,1,0:T(8,128)(2,1)S(1)}, u32[]{:S(2)}, u32[]{:S(2)}) async-start(bf16[32,80,128]{2,1,0:T(8,128)(2,1)} %get-tuple-element.11), calls=%async_computation | async-start | bytes 1310720 | tf_op jit(solution)/shard_map/all_to_all | solution.py:515
  47.2 5.4 %collective-permute-start.2 = (s32[10,64]{1,0:T(8,128)S(1)}, s32[10,64]{1,0:T(8,128)S(1)}, u32[]{:S(2)}, u32[]{:S(2)}) collective-permute-start(s32[10,64]{1,0:T(8,128)S(1)} %bitcast.13), channel_id=1, source_target_pairs={{0,1},{1,2},{2,3},{3,4},{4,5},{5,6},{6,7},{7,8},{8,9},{9,10},{10,1... | collective-permute-start | bytes 7688 | tf_op jit(solution)/shard_map/ppermute | solution.py:511
  50.6 34.0 %copy-start.3 = (f32[16]{0:T(128)S(1)}, f32[16]{0:T(128)}, u32[]{:S(2)}) copy-start(f32[16]{0:T(128)} %ridge.1) | copy-start | bytes 196
  50.6 34.0 %collective-permute-start.1 = (bf16[16,16384]{1,0:T(8,128)(2,1)}, bf16[16,16384]{1,0:T(8,128)(2,1)S(1)}, u32[]{:S(2)}, u32[]{:S(2)}) collective-permute-start(bf16[16,16384]{1,0:T(8,128)(2,1)} %get-tuple-element.12.w_hbm), channel_id=1, source_target_pairs={{0,1},{1,2},{2,3},{3,4},{4,5},{5,6},{6,7},{7,8},{8,9},{9,10},{10,1... | collective-permute-start | bytes 1572872 | tf_op jit(solution)/shard_map/ppermute | solution.py:516
  52.7 1.1 copy-start
  53.7 30.9 %copy-start.1 = (s32[31,128]{1,0:T(8,128)S(1)}, s32[31,128]{1,0:T(8,128)}, u32[]{:S(2)}) copy-start(s32[31,128]{1,0:T(8,128)} %top_pick.1) | copy-start | bytes 47620
  53.7 30.9 %copy-start.2 = (s32[16,64]{1,0:T(8,128)S(1)}, s32[16,64]{1,0:T(8,128)}, u32[]{:S(2)}) copy-start(s32[16,64]{1,0:T(8,128)} %get-tuple-element.10.lst) | copy-start | bytes 12292
  70.2 38.7 %collective-permute-start.3 = (bf16[16,16384]{1,0:T(8,128)(2,1)S(1)}, bf16[16,16384]{1,0:T(8,128)(2,1)S(1)}, u32[]{:S(2)}, u32[]{:S(2)}) collective-permute-start(bf16[16,16384]{1,0:T(8,128)(2,1)S(1)} %near_back.1.after), channel_id=1, source_target_pairs={{1,0},{2,1},{3,2},{4,3},{5,4},{6,5},{7,6},{8,7},{9,8},{10,9},{11,1... | collective-permute-start | bytes 1572872 | tf_op jit(solution)/shard_map/ppermute | solution.py:518

commit v6 on v5

--- a/solution.py
+++ b/solution.py
@@ -507,8 +507,9 @@
     lower = [(i + 1, i) for i in range(subtrees - 1)]
 
     xt, dt, ids = points.T, direction.T, near_list.T
-    x_low = lax.ppermute(xt, AXES, upper)
     ids_low = lax.ppermute(ids, AXES, upper)
+    x_sent, ids_low = lax.optimization_barrier((xt, ids_low))
+    x_low = lax.ppermute(x_sent, AXES, upper)
     w, terms, spread, list_low, n_own = upward(
         pos, xt, dt, ids, leaf_pick, local_pick, leaf_basis, local_basis, subtrees
     )

time: 110 us -> 101 us (0.918)
  the two profiles are of different devices: /device:TPU:17 before, /device:TPU:8 now
where the time goes in v6:
time: 101 us
  Pallas kernels  68.8 us (68%)
  starting transfers between devices  23.4 us (23%)
  waiting for transfers between devices  5.06 us (5%)
  other arithmetic  2.3 us (2%)
  local copies, waits for them, and re-layouts  1.05 us (1%)
    pallas_call x1, Pallas kernels, upward(): pl.pallas_call(functools.partial(up_kernel, (count, leaf, rank, dim, cols...  30 us
    pallas_call x1, Pallas kernels, downward(): pl.pallas_call(functools.partial(down_kernel, (count, leaf, rank, dim, co...  24 us
    pallas_call x1, Pallas kernels, near_back(): pl.pallas_call(near_back_kernel, grid_spec=pltpu.PrefetchScalarGridSpec(n...  14.7 us
    all_to_all x1, starting transfers between devices, shards(): gathered = lax.all_to_all(spread, AXES, 0, 0)  10.7 us
    ppermute x1, starting transfers between devices, shards(): returned = lax.ppermute(back, AXES, lower)  6.85 us
    ppermute x1, waiting for transfers between devices, shards(): ids_low = lax.ppermute(ids, AXES, upper)  5.05 us
    transpose x1, other arithmetic, shards(): return (out + returned.astype(f32)).T  2.3 us
    ppermute x1, starting transfers between devices, shards(): w_low = lax.ppermute(w, AXES, upper)  2.06 us
  transfers between devices with their start and end apart: 5, of which 1 were waited for; matrix products, arithmetic and copies ran while one was open for 0% of the time, Pallas kernels for 68%

profile of v6, /device:TPU:8, one launch (start us, length us, event | category | flops | bytes accessed | tf_op | source)
XLA Modules:
  0.0 100.8 jit_solution(7363904137633162699)
XLA Ops:
  0.0 1.9 %collective-permute-start = (s32[10,64]{1,0:T(8,128)}, s32[10,64]{1,0:T(8,128)S(1)}, u32[]{:S(2)}, u32[]{:S(2)}) collective-permute-start(s32[10,64]{1,0:T(8,128)} %bitcast.12), channel_id=1, source_target_pairs={{0,1},{1,2},{2,3},{3,4},{4,5},{5,6},{6,7},{7,8},{8,9},{9,10},{10,1... | collective-permute-start | bytes 7688 | tf_op jit(solution)/shard_map/ppermute | solution.py:510
  1.9 5.0 %collective-permute-done.ids = s32[10,64]{1,0:T(8,128)S(1)} collective-permute-done((s32[10,64]{1,0:T(8,128)}, s32[10,64]{1,0:T(8,128)S(1)}, u32[]{:S(2)}, u32[]{:S(2)}) %collective-permute-start) | collective-permute-done | bytes 2592 | tf_op jit(solution)/shard_map/ppermute | solution.py:510
  7.0 1.9 %collective-permute-start.1 = (bf16[64,16384]{1,0:T(8,128)(2,1)}, bf16[64,16384]{1,0:T(8,128)(2,1)}, u32[]{:S(2)}, u32[]{:S(2)}) collective-permute-start(bf16[64,16384]{1,0:T(8,128)(2,1)} %bitcast.6), channel_id=1, source_target_pairs={{0,1},{1,2},{2,3},{3,4},{4,5},{5,6},{6,7},{7,8},{8,9},{9,10},{10,1... | collective-permute-start | bytes 6291464 | tf_op jit(solution)/shard_map/ppermute | solution.py:512
  8.9 30.0 %upward.1 = (bf16[16,16384]{1,0:T(8,128)(2,1)}, f32[16,16128]{1,0:T(8,128)}, bf16[32,80,128]{2,1,0:T(8,128)(2,1)}, s32[16,64]{1,0:T(8,128)}, f32[65,16,256]{2,1,0:T(8,128)}) custom-call(s32[1]{0:T(128)} %bitcast.pos_ref, bf16[64,16384]{1,0:T(8,128)(2,1)} %bitcast.7, f32[16,16384]{1,0:T(8,128)} %bitcast.10, s32[10,64]{1,0:T(8,128)} %bitcast.13, ...), custom_call_target="tpu_custom_call" | custom-call | tf_op jit(solution)/shard_map/upward/pallas_call | solution.py:228
  38.9 10.7 %all-to-all-start = ((bf16[32,80,128]{2,1,0:T(8,128)(2,1)}), bf16[32,80,128]{2,1,0:T(8,128)(2,1)S(1)}, u32[]{:S(2)}, u32[]{:S(2)}) async-start(bf16[32,80,128]{2,1,0:T(8,128)(2,1)} %get-tuple-element.13), calls=%async_computation | async-start | bytes 1310720 | tf_op jit(solution)/shard_map/all_to_all | solution.py:516
  49.7 0.0 copy-start.3
  49.7 2.1 %collective-permute-start.2 = (bf16[16,16384]{1,0:T(8,128)(2,1)}, bf16[16,16384]{1,0:T(8,128)(2,1)S(1)}, u32[]{:S(2)}, u32[]{:S(2)}) collective-permute-start(bf16[16,16384]{1,0:T(8,128)(2,1)} %get-tuple-element.15.w_hbm), channel_id=1, source_target_pairs={{0,1},{1,2},{2,3},{3,4},{4,5},{5,6},{6,7},{7,8},{8,9},{9,10},{10,1... | collective-permute-start | bytes 1572872 | tf_op jit(solution)/shard_map/ppermute | solution.py:517
  51.7 0.0 collective-permute-done.1.low_hbm
  51.7 0.0 copy-start
  51.8 1.0 %copy-done = bf16[16,16384]{1,0:T(8,128)(2,1)S(1)} copy-done((bf16[16,16384]{1,0:T(8,128)(2,1)S(1)}, bf16[16,16384]{1,0:T(8,128)(2,1)}, u32[]{:S(2)}) %copy-start) | copy-done | bytes 524312
  52.8 0.0 copy-start.1
  52.8 0.0 copy-start.2
  52.8 14.7 %near_back.1.after = bf16[16,16384]{1,0:T(8,128)(2,1)S(1)} custom-call(s32[1]{0:T(128)} %bitcast.pos_ref, s32[10,64]{1,0:T(8,128)S(1)} %collective-permute-done.ids, bf16[64,16384]{1,0:T(8,128)(2,1)} %collective-permute-done.1.low_hbm, bf16[64,16384]{1,0:T(8,128)(2,1)} %bitcast.8, bf16[16,16384]{1,0:T(8,128)(2,1)S(1)} %copy-done), custom_call_target="tpu_custom_call" | custom-call | tf_op jit(solution)/shard_map/near_back/pallas_call | solution.py:369
  67.5 6.9 %collective-permute-start.3 = (bf16[16,16384]{1,0:T(8,128)(2,1)S(1)}, bf16[16,16384]{1,0:T(8,128)(2,1)S(1)}, u32[]{:S(2)}, u32[]{:S(2)}) collective-permute-start(bf16[16,16384]{1,0:T(8,128)(2,1)S(1)} %near_back.1.after), channel_id=1, source_target_pairs={{1,0},{2,1},{3,2},{4,3},{5,4},{6,5},{7,6},{8,7},{9,8},{10,9},{11,1... | collective-permute-start | bytes 1572872 | tf_op jit(solution)/shard_map/ppermute | solution.py:519
  74.4 0.0 collective-permute-done.2.wlow_hbm
  74.4 0.0 all-to-all-done.gathered
  74.4 0.0 copy-done.3
  74.4 0.0 copy-done.1
  74.4 0.0 copy-done.2
  74.4 24.0 %downward.1 = f32[16,16384]{1,0:T(8,128)} custom-call(s32[1]{0:T(128)} %bitcast.pos_ref, s32[16,64]{1,0:T(8,128)S(1)} %copy-done.2, f32[16]{0:T(128)S(1)} %copy-done.3, bf16[32,80,128]{2,1,0:T(8,128)(2,1)S(1)} %all-to-all-done.gathered, s32[31,128]{1,0:T(8,128)S(1)} %copy-done.1, bf16[64,16384]{1,0:T(8,128)(2,1)} %collective-permute-done.1.low_hbm, ...), custom_call_target="tpu_custom_call" | custom-call | tf_op jit(solution)/shard_map/downward/pallas_call | solution.py:476
  98.4 0.0 collective-permute-done.3
  98.5 2.3 %add_bitcast_fusion = f32[16384,16]{0,1:T(8,128)} fusion(f32[16,16384]{1,0:T(8,128)} %downward.1, bf16[16,16384]{1,0:T(8,128)(2,1)S(1)} %collective-permute-done.3), kind=kLoop, calls=%fused_computation | loop fusion | flops 524288 | bytes 2621440 | tf_op jit(solution)/shard_map/transpose | solution.py:524
Async XLA Ops:
  0.0 7.0 %collective-permute-start = (s32[10,64]{1,0:T(8,128)}, s32[10,64]{1,0:T(8,128)S(1)}, u32[]{:S(2)}, u32[]{:S(2)}) collective-permute-start(s32[10,64]{1,0:T(8,128)} %bitcast.12), channel_id=1, source_target_pairs={{0,1},{1,2},{2,3},{3,4},{4,5},{5,6},{6,7},{7,8},{8,9},{9,10},{10,1... | collective-permute-start | bytes 7688 | tf_op jit(solution)/shard_map/ppermute | solution.py:510
  7.0 44.8 %collective-permute-start.1 = (bf16[64,16384]{1,0:T(8,128)(2,1)}, bf16[64,16384]{1,0:T(8,128)(2,1)}, u32[]{:S(2)}, u32[]{:S(2)}) collective-permute-start(bf16[64,16384]{1,0:T(8,128)(2,1)} %bitcast.6), channel_id=1, source_target_pairs={{0,1},{1,2},{2,3},{3,4},{4,5},{5,6},{6,7},{7,8},{8,9},{9,10},{10,1... | collective-permute-start | bytes 6291464 | tf_op jit(solution)/shard_map/ppermute | solution.py:512
  38.9 35.5 %all-to-all-start = ((bf16[32,80,128]{2,1,0:T(8,128)(2,1)}), bf16[32,80,128]{2,1,0:T(8,128)(2,1)S(1)}, u32[]{:S(2)}, u32[]{:S(2)}) async-start(bf16[32,80,128]{2,1,0:T(8,128)(2,1)} %get-tuple-element.13), calls=%async_computation | async-start | bytes 1310720 | tf_op jit(solution)/shard_map/all_to_all | solution.py:516
  49.7 24.8 %copy-start.3 = (f32[16]{0:T(128)S(1)}, f32[16]{0:T(128)}, u32[]{:S(2)}) copy-start(f32[16]{0:T(128)} %ridge.1) | copy-start | bytes 196
  49.7 24.7 %collective-permute-start.2 = (bf16[16,16384]{1,0:T(8,128)(2,1)}, bf16[16,16384]{1,0:T(8,128)(2,1)S(1)}, u32[]{:S(2)}, u32[]{:S(2)}) collective-permute-start(bf16[16,16384]{1,0:T(8,128)(2,1)} %get-tuple-element.15.w_hbm), channel_id=1, source_target_pairs={{0,1},{1,2},{2,3},{3,4},{4,5},{5,6},{6,7},{7,8},{8,9},{9,10},{10,1... | collective-permute-start | bytes 1572872 | tf_op jit(solution)/shard_map/ppermute | solution.py:517
  51.7 1.0 %copy-start = (bf16[16,16384]{1,0:T(8,128)(2,1)S(1)}, bf16[16,16384]{1,0:T(8,128)(2,1)}, u32[]{:S(2)}) copy-start(bf16[16,16384]{1,0:T(8,128)(2,1)} %get-tuple-element.15.w_hbm) | copy-start | bytes 1572868
  52.8 21.6 %copy-start.1 = (s32[31,128]{1,0:T(8,128)S(1)}, s32[31,128]{1,0:T(8,128)}, u32[]{:S(2)}) copy-start(s32[31,128]{1,0:T(8,128)} %top_pick.1) | copy-start | bytes 47620
  52.8 21.6 %copy-start.2 = (s32[16,64]{1,0:T(8,128)S(1)}, s32[16,64]{1,0:T(8,128)}, u32[]{:S(2)}) copy-start(s32[16,64]{1,0:T(8,128)} %get-tuple-element.12.lst) | copy-start | bytes 12292
  67.5 30.9 %collective-permute-start.3 = (bf16[16,16384]{1,0:T(8,128)(2,1)S(1)}, bf16[16,16384]{1,0:T(8,128)(2,1)S(1)}, u32[]{:S(2)}, u32[]{:S(2)}) collective-permute-start(bf16[16,16384]{1,0:T(8,128)(2,1)S(1)} %near_back.1.after), channel_id=1, source_target_pairs={{1,0},{2,1},{3,2},{4,3},{5,4},{6,5},{7,6},{8,7},{9,8},{10,9},{11,1... | collective-permute-start | bytes 1572872 | tf_op jit(solution)/shard_map/ppermute | solution.py:519

commit v7 on v5

--- a/solution.py
+++ b/solution.py
@@ -24,6 +24,12 @@
     c = pltpu.make_async_copy(src, dst, sem)
     c.start()
     return c
+
+
+def near_cost(pairs, leaf, cols, data):
+    return pl.CostEstimate(
+        flops=pairs * 2 * leaf * leaf * (2 * FEAT + leaf), transcendentals=pairs * leaf * leaf, bytes_accessed=data
+    )
 
 
 VM = pl.BlockSpec(memory_space=pltpu.VMEM)
@@ -111,19 +117,49 @@
     return out
 
 
-def up_kernel(dims, pos_ref, x_hbm, d_hbm, ids, leaf_pick, local_pick, leaf_hbm, local_hbm,
-              w_hbm, terms_hbm, spread, list_low, acc,
-              pair, big, at, b, wt, xt, dt, terms, lb, nb, coeff, skel, tiles, lv, lst, xs, ls, ms):
+def pack_kernel(pos_ref, d_hbm, ids, out, dt, sems):
+    cols, width = dt.shape
+    count = ids.shape[1]
+    part = width // CHUNKS
+    gets = [copy(d_hbm.at[:, pl.ds(c * part, part)], dt.at[:, pl.ds(c * part, part)], sems.at[c]) for c in range(CHUNKS)]
+    out[:, pl.ds(width, 128)] = jnp.zeros((cols, 128), bf16)
+    out[:, pl.ds(width, count)] = class_list(ids[...], (pos_ref[0] + 1) * count, count).astype(f32).astype(bf16)
+    for c in range(CHUNKS):
+        gets[c].wait()
+        s = pl.ds(c * part, part)
+        out[:, s] = dt[:, s].astype(bf16)
+
+
+def pack(pos, dt, ids):
+    cols, width = dt.shape
+    return pl.pallas_call(
+        pack_kernel,
+        grid_spec=pltpu.PrefetchScalarGridSpec(
+            num_scalar_prefetch=1,
+            grid=(1,),
+            in_specs=[HBM, VM],
+            out_specs=VM,
+            scratch_shapes=[pltpu.VMEM(dt.shape, f32), pltpu.SemaphoreType.DMA((CHUNKS,))],
+        ),
+        out_shape=jax.ShapeDtypeStruct((cols, width + 128), bf16),
+        compiler_params=pltpu.CompilerParams(vmem_limit_bytes=60 << 20),
+        name="pack",
+    )(pos, dt, ids)
+
+
+def up_kernel(dims, pos_ref, x_hbm, w_hbm, ids, leaf_pick, local_pick, leaf_hbm, local_hbm,
+              terms_hbm, spread, list_low, acc,
+              pair, big, at, b, wt, xt, terms, lb, nb, coeff, skel, tiles, lv, lst, xs, ls, ms):
     count, leaf, rank, dim, cols = dims
     entries = ids.shape[0]
     part = count // CHUNKS
     seg = lambda c: pl.ds(c * part * leaf, part * leaf)
     own = lambda c: pl.ds(c * part, part)
     get_x = [copy(x_hbm.at[:, seg(c)], xt.at[:, seg(c)], xs.at[c]) for c in range(CHUNKS)]
-    get_d = copy(d_hbm, dt, ms.at[0])
+    get_w = copy(w_hbm, wt, ms.at[0])
     pos = pos_ref[0]
     table = ids[...]
-    put_list = put_class(table, pos * count, count, lv, lst, ms.at[4])
+    put_list = put_class(table, pos * count, count, lv, lst, ms.at[3])
     list_low[...] = class_list(table, (pos - 1) * count, count)
     acc[...] = jnp.zeros_like(acc)
 
@@ -142,12 +178,9 @@
         if c == 1:
             get_leaf = [copy(leaf_hbm.at[own(k)], lb.at[own(k)], ls.at[k]) for k in range(CHUNKS)]
             get_local = copy(local_hbm, nb, ms.at[1])
-        total = grouped(part, 8, prepare, keep, c * part, scan_leaf(count, entries, lst, pair), total)
+        total = grouped(part, 16, prepare, keep, c * part, scan_leaf(count, entries, lst, pair), total)
     end_list(count, pair, total)
-    get_d.wait()
-    for c in range(CHUNKS):
-        wt[:, seg(c)] = dt[:, seg(c)].astype(bf16)
-    puts = [copy(wt, w_hbm, ms.at[2])]
+    get_w.wait()
     base = count - 1
 
     def leaf_step(l):
@@ -160,7 +193,7 @@
 
     for c in range(CHUNKS):
         get_leaf[c].wait()
-        grouped(part, 8, leaf_step, leaf_keep, c * part)
+        grouped(part, 16, leaf_step, leaf_keep, c * part)
     get_local.wait()
     depth = count.bit_length() - 1
     for d in range(depth, 0, -1):
@@ -174,7 +207,7 @@
         def climb_keep(j, got):
             coeff[:, lanes(j, rank)], skel[:, lanes(j, rank)] = got
 
-        grouped(2 ** (d - 1), 16, climb, climb_keep, up)
+        grouped(2 ** (d - 1), 32, climb, climb_keep, up)
     root_c, root_s = coeff[:, :rank], skel[:dim, :rank]
     for s in range(spread.shape[0]):
         spread[s, :cols, :] = root_c
@@ -209,10 +242,9 @@
         return carry
 
     lax.fori_loop(0, count // (2 * PAIRS), body, 0)
-    puts.append(copy(terms, terms_hbm, ms.at[3]))
+    put_terms = copy(terms, terms_hbm, ms.at[2])
     near_pairs(count, total, pair, at, b, wt, acc, big)
-    for p in puts:
-        p.wait()
+    put_terms.wait()
 
 
 def put_class(table, low, count, lv, lst, sem):
@@ -221,9 +253,9 @@
     return copy(lv, lst, sem)
 
 
-def upward(pos, xt, dt, ids, leaf_pick, local_pick, leaf_basis, local_basis, subtrees):
+def upward(pos, xt, w, ids, leaf_pick, local_pick, leaf_basis, local_basis, subtrees):
     count, leaf, rank = leaf_basis.shape
-    dim, cols = xt.shape[0], dt.shape[0]
+    dim, cols = xt.shape[0], w.shape[0]
     entries = ids.shape[0]
     return pl.pallas_call(
         functools.partial(up_kernel, (count, leaf, rank, dim, cols)),
@@ -231,10 +263,9 @@
             num_scalar_prefetch=1,
             grid=(1,),
             in_specs=[HBM, HBM, VM, VM, VM, HBM, HBM],
-            out_specs=[HBM, HBM, VM, VM, VM],
+            out_specs=[HBM, VM, VM, VM],
             scratch_shapes=near_scratch(count, entries, leaf, dim, cols)
             + [
-                pltpu.VMEM(dt.shape, f32),
                 pltpu.VMEM((cols, (2 * count - 2) * rank), f32),
                 pltpu.VMEM(leaf_basis.shape, bf16),
                 pltpu.VMEM(local_basis.shape, bf16),
@@ -245,19 +276,19 @@
                 pltpu.SMEM((16, 128), jnp.int32),
                 pltpu.SemaphoreType.DMA((CHUNKS,)),
                 pltpu.SemaphoreType.DMA((CHUNKS,)),
-                pltpu.SemaphoreType.DMA((5,)),
+                pltpu.SemaphoreType.DMA((4,)),
             ],
         ),
         out_shape=[
-            jax.ShapeDtypeStruct((cols, count * leaf), bf16),
             jax.ShapeDtypeStruct((cols, (2 * count - 2) * rank), f32),
             jax.ShapeDtypeStruct((subtrees, cols + dim, rank), bf16),
             jax.ShapeDtypeStruct((16, count), jnp.int32),
             jax.ShapeDtypeStruct((count + 1, cols, leaf), f32),
         ],
         compiler_params=pltpu.CompilerParams(vmem_limit_bytes=60 << 20),
+        cost_estimate=near_cost(12 * count, leaf, cols, 16 << 20),
         name="upward",
-    )(pos, xt, dt, ids, leaf_pick, local_pick, leaf_basis, local_basis)
+    )(pos, xt, w, ids, leaf_pick, local_pick, leaf_basis, local_basis)
 
 
 def scan_leaf(count, entries, lst, pair):
@@ -311,7 +342,7 @@
         pltpu.VMEM((2 * GROUP, leaf, leaf), bf16),
         pltpu.VMEM((count, FEAT, leaf), bf16),
         pltpu.VMEM((count, leaf, FEAT), bf16),
-        pltpu.VMEM((cols, count * leaf), bf16),
+        pltpu.VMEM((cols, count * leaf + 128), bf16),
         pltpu.VMEM((dim, count * leaf), bf16),
     ]
 
@@ -335,21 +366,21 @@
         for c in range(CHUNKS):
             gets[2 * c].wait()
             gets[2 * c + 1].wait()
-            total = grouped(part, 8, prepare, keep, c * part, also, total)
+            total = grouped(part, 16, prepare, keep, c * part, also, total)
         return total
 
     return finish
 
 
-def near_back_kernel(pos_ref, ids, low_hbm, x_hbm, w_hbm, out,
-                     pair, tiles, at, b, w, x, y, acc, lv, lst, xs, sems):
+def near_back_kernel(entries, low_hbm, x_hbm, wlow_hbm, w_hbm, out,
+                     pair, tiles, at, b, w, x, y, acc, lf, lv, lst, xs, sems):
     count, _, leaf = at.shape
-    entries = ids.shape[0]
+    get_list = copy(wlow_hbm.at[:, pl.ds(count * leaf, 128)], lf, sems.at[0])
     finish = two_sided(count, leaf, low_hbm, x_hbm, x, y, at, b, xs)
-    get_w = copy(w_hbm, w, sems.at[0])
-    pos = pos_ref[0]
-    low = jnp.where(pos == 0, -(1 << 24), pos * count)
-    put_list = put_class(ids[...], low, count, lv, lst, sems.at[1])
+    get_w = copy(w_hbm, w, sems.at[1])
+    get_list.wait()
+    lv[...] = lf[...].astype(f32).astype(jnp.int32)
+    put_list = copy(lv, lst, sems.at[2])
     acc[...] = jnp.zeros_like(acc)
     put_list.wait()
     total = finish(scan_leaf(count, entries, lst, pair))
@@ -363,30 +394,35 @@
     grouped(count, 8, lambda l: acc[l], store)
 
 
-def near_back(pos, ids_low, x_low, x, w, count, leaf):
+def near_back(x_low, x, w_low, w, after, count, entries, leaf):
     dim, cols = x.shape[0], w.shape[0]
-    entries = ids_low.shape[0]
+
+    def kernel(low_hbm, x_hbm, wlow_hbm, w_hbm, after_hbm, *rest):
+        near_back_kernel(entries, low_hbm, x_hbm, wlow_hbm, w_hbm, *rest)
+
     return pl.pallas_call(
-        near_back_kernel,
+        kernel,
         grid_spec=pltpu.PrefetchScalarGridSpec(
-            num_scalar_prefetch=1,
+            num_scalar_prefetch=0,
             grid=(1,),
-            in_specs=[VM, ANY, HBM, HBM],
+            in_specs=[ANY, HBM, ANY, HBM, HBM],
             out_specs=VM,
             scratch_shapes=near_scratch(count, entries, leaf, dim, cols)
             + [
                 pltpu.VMEM((dim, count * leaf), bf16),
                 pltpu.VMEM((count + 1, cols, leaf), f32),
-                pltpu.VMEM((16, 128), jnp.int32),
-                pltpu.SMEM((16, 128), jnp.int32),
+                pltpu.VMEM((cols, 128), bf16),
+                pltpu.VMEM((cols, 128), jnp.int32),
+                pltpu.SMEM((cols, 128), jnp.int32),
                 pltpu.SemaphoreType.DMA((2, CHUNKS)),
-                pltpu.SemaphoreType.DMA((2,)),
+                pltpu.SemaphoreType.DMA((3,)),
             ],
         ),
         out_shape=jax.ShapeDtypeStruct((cols, count * leaf), bf16),
         compiler_params=pltpu.CompilerParams(vmem_limit_bytes=52 << 20),
+        cost_estimate=near_cost(4 * count, leaf, cols, 6 << 20),
         name="near_back",
-    )(pos, ids_low, x_low, x, w)
+    )(x_low, x, w_low, w, after)
 
 
 def down_kernel(dims, pos_ref, lst, ridge, gathered, top_pick, low_hbm, x_hbm, wlow_hbm, own_hbm,
@@ -421,7 +457,7 @@
         def climb_keep(j, got):
             tcoeff[:, lanes(j, rank)], tskel[:, lanes(j, rank)] = got
 
-        grouped(2**d, 8, climb, climb_keep, 2**d - 1)
+        grouped(2**d, 16, climb, climb_keep, 2**d - 1)
 
     def half(v):
         return (v.astype(f32) * 0.5).astype(bf16)
@@ -451,7 +487,7 @@
         def descend_keep(j, got):
             value[:, lanes(2 * j + 1, rank, 2)] = got
 
-        grouped(2 ** (d - 1), 8, descend, descend_keep, 2 ** (d - 1) - 1)
+        grouped(2 ** (d - 1), 32, descend, descend_keep, 2 ** (d - 1) - 1)
     row = lax.broadcasted_iota(jnp.int32, (cols, leaf), 0)
     scale = jnp.zeros((cols, leaf), f32)
     for r in range(cols):
@@ -464,7 +500,7 @@
     def finish_keep(l, got):
         out[:, lanes(l, leaf)] = got
 
-    grouped(count, 8, finish, finish_keep)
+    grouped(count, 16, finish, finish_keep)
 
 
 def downward(pos, lst, ridge, gathered, top_pick, x_low, x, w_low, n_own, top_basis, terms, local_basis, leaf_basis,
@@ -493,6 +529,7 @@
         ),
         out_shape=jax.ShapeDtypeStruct(dt.shape, f32),
         compiler_params=pltpu.CompilerParams(vmem_limit_bytes=52 << 20),
+        cost_estimate=near_cost(8 * count, leaf, cols, 20 << 20),
         name="downward",
     )(pos, lst, ridge, gathered, top_pick, x_low, x, w_low, n_own, *big, after)
 
@@ -508,13 +545,13 @@
 
     xt, dt, ids = points.T, direction.T, near_list.T
     x_low = lax.ppermute(xt, AXES, upper)
-    ids_low = lax.ppermute(ids, AXES, upper)
-    w, terms, spread, list_low, n_own = upward(
-        pos, xt, dt, ids, leaf_pick, local_pick, leaf_basis, local_basis, subtrees
+    w = pack(pos, dt, ids)
+    w_low = lax.ppermute(w, AXES, upper)
+    terms, spread, list_low, n_own = upward(
+        pos, xt, w, ids, leaf_pick, local_pick, leaf_basis, local_basis, subtrees
     )
     gathered = lax.all_to_all(spread, AXES, 0, 0)
-    w_low = lax.ppermute(w, AXES, upper)
-    back = near_back(pos, ids_low, x_low, xt, w, count, leaf)
+    back = near_back(x_low, xt, w_low, w, n_own, count, entries, leaf)
     returned = lax.ppermute(back, AXES, lower)
     out = downward(
         pos, list_low, ridge, gathered, top_pick, x_low, xt, w_low, n_own, top_basis, terms, local_basis, leaf_basis,

time: 110 us -> 92.7 us (0.84)
  the two profiles are of different devices: /device:TPU:17 before, /device:TPU:16 now
where the time goes in v7:
time: 92.7 us; the launch traced here: 92 us
  Pallas kernels  66.2 us (71%)
  starting transfers between devices  23.3 us (25%)
  other arithmetic  2.33 us (3%)
    pallas_call x1, Pallas kernels, upward(): pl.pallas_call(functools.partial(up_kernel, (count, leaf, rank, dim, cols...  26.9 us
    pallas_call x1, Pallas kernels, downward(): pl.pallas_call(functools.partial(down_kernel, (count, leaf, rank, dim, co...  21.5 us
    pallas_call x1, Pallas kernels, near_back(): pl.pallas_call(kernel, grid_spec=pltpu.PrefetchScalarGridSpec(num_scalar_...  15.2 us
    all_to_all x1, starting transfers between devices, shards(): gathered = lax.all_to_all(spread, AXES, 0, 0)  13.7 us
    ppermute x1, starting transfers between devices, shards(): returned = lax.ppermute(back, AXES, lower)  4.03 us
    ppermute x1, starting transfers between devices, shards(): x_low = lax.ppermute(xt, AXES, upper)  3.64 us
    pallas_call x1, Pallas kernels, pack(): pl.pallas_call(pack_kernel, grid_spec=pltpu.PrefetchScalarGridSpec(num_sc...  2.74 us
    transpose x1, other arithmetic, shards(): return (out + returned.astype(f32)).T  2.33 us
  transfers between devices with their start and end apart: 4, of which 0 were waited for; matrix products, arithmetic and copies ran while one was open for 0% of the time, Pallas kernels for 69%

profile of v7, /device:TPU:16, one launch (start us, length us, event | category | flops | bytes accessed | tf_op | source)
XLA Modules:
  0.0 92.0 jit_solution(6420206960992416611)
XLA Ops:
  0.0 2.7 %pack.1.w_hbm = bf16[16,16512]{1,0:T(8,128)(2,1)} custom-call(s32[1]{0:T(128)} %bitcast.pos_ref, f32[16,16384]{1,0:T(8,128)} %bitcast.6, s32[10,64]{1,0:T(8,128)} %bitcast.8), custom_call_target="tpu_custom_call" | custom-call | tf_op jit(solution)/shard_map/pack/pallas_call | solution.py:135
  2.7 1.9 %collective-permute-start.1 = (bf16[16,16512]{1,0:T(8,128)(2,1)}, bf16[16,16512]{1,0:T(8,128)(2,1)S(1)}, u32[]{:S(2)}, u32[]{:S(2)}) collective-permute-start(bf16[16,16512]{1,0:T(8,128)(2,1)} %pack.1.w_hbm), channel_id=1, source_target_pairs={{0,1},{1,2},{2,3},{3,4},{4,5},{5,6},{6,7},{7,8},{8,9},{9,10},{10,1... | collective-permute-start | bytes 1585160 | tf_op jit(solution)/shard_map/ppermute | solution.py:549
  4.7 0.0 copy-start
  4.7 3.6 %collective-permute-start = (bf16[64,16384]{1,0:T(8,128)(2,1)}, bf16[64,16384]{1,0:T(8,128)(2,1)}, u32[]{:S(2)}, u32[]{:S(2)}) collective-permute-start(bf16[64,16384]{1,0:T(8,128)(2,1)} %bitcast.10), channel_id=1, source_target_pairs={{0,1},{1,2},{2,3},{3,4},{4,5},{5,6},{6,7},{7,8},{8,9},{9,10},{10,1... | collective-permute-start | bytes 6291464 | tf_op jit(solution)/shard_map/ppermute | solution.py:547
  8.3 26.9 %upward.1 = (f32[16,16128]{1,0:T(8,128)}, bf16[32,80,128]{2,1,0:T(8,128)(2,1)}, s32[16,64]{1,0:T(8,128)}, f32[65,16,256]{2,1,0:T(8,128)}) custom-call(s32[1]{0:T(128)} %bitcast.pos_ref, bf16[64,16384]{1,0:T(8,128)(2,1)} %bitcast.11, bf16[16,16512]{1,0:T(8,128)(2,1)} %pack.1.w_hbm, s32[10,64]{1,0:T(8,128)} %bitcast.9, s32[64,128]{1,0:T(8,128)} %leaf_pick.1, ...), custom_call_target="tpu_custom_call" | custom-call | flops 51539607552 | bytes 16777216 | tf_op jit(solution)/shard_map/upward/pallas_call | solution.py:260
  35.2 13.7 %all-to-all-start = ((bf16[32,80,128]{2,1,0:T(8,128)(2,1)}), bf16[32,80,128]{2,1,0:T(8,128)(2,1)S(1)}, u32[]{:S(2)}, u32[]{:S(2)}) async-start(bf16[32,80,128]{2,1,0:T(8,128)(2,1)} %get-tuple-element.10), calls=%async_computation | async-start | bytes 1310720 | tf_op jit(solution)/shard_map/all_to_all | solution.py:553
  48.9 0.0 collective-permute-done.1.wlow_hbm
  48.9 0.0 collective-permute-done.low_hbm
  48.9 0.0 copy-done
  48.9 0.0 copy-start.1
  48.9 0.0 copy-start.2
  49.0 0.0 copy-start.3
  49.0 15.2 %near_back.1.after = bf16[16,16384]{1,0:T(8,128)(2,1)S(1)} custom-call(bf16[64,16384]{1,0:T(8,128)(2,1)} %collective-permute-done.low_hbm, bf16[64,16384]{1,0:T(8,128)(2,1)} %bitcast.12, bf16[16,16512]{1,0:T(8,128)(2,1)S(1)} %collective-permute-done.1.wlow_hbm, bf16[16,16512]{1,0:T(8,128)(2,1)S(1)} %copy-done, f32[65,16,256]{2,1,0:T(8,128)} %get-tuple-element.11.after_hbm.own_hbm), custom_call_target="tpu_custom_call" | custom-call | flops 17179869184 | bytes 6291456 | tf_op jit(solution)/shard_map/near_back/pallas_call | solution.py:403
  64.1 4.0 %collective-permute-start.2 = (bf16[16,16384]{1,0:T(8,128)(2,1)S(1)}, bf16[16,16384]{1,0:T(8,128)(2,1)S(1)}, u32[]{:S(2)}, u32[]{:S(2)}) collective-permute-start(bf16[16,16384]{1,0:T(8,128)(2,1)S(1)} %near_back.1.after), channel_id=1, source_target_pairs={{1,0},{2,1},{3,2},{4,3},{5,4},{6,5},{7,6},{8,7},{9,8},{10,9},{11,1... | collective-permute-start | bytes 1572872 | tf_op jit(solution)/shard_map/ppermute | solution.py:555
  68.2 0.0 all-to-all-done.gathered
  68.2 0.0 copy-done.1
  68.2 0.0 copy-done.2
  68.2 0.0 copy-done.3
  68.2 21.5 %downward.1 = f32[16,16384]{1,0:T(8,128)} custom-call(s32[1]{0:T(128)} %bitcast.pos_ref, s32[16,64]{1,0:T(8,128)S(1)} %copy-done.3, f32[16]{0:T(128)S(1)} %copy-done.2, bf16[32,80,128]{2,1,0:T(8,128)(2,1)S(1)} %all-to-all-done.gathered, s32[31,128]{1,0:T(8,128)S(1)} %copy-done.1, bf16[64,16384]{1,0:T(8,128)(2,1)} %collective-permute-done.low_hbm, ...), custom_call_target="tpu_custom_call" | custom-call | flops 34359738368 | bytes 20971520 | tf_op jit(solution)/shard_map/downward/pallas_call | solution.py:512
  89.7 0.0 collective-permute-done.2
  89.7 2.3 %add_bitcast_fusion = f32[16384,16]{0,1:T(8,128)} fusion(f32[16,16384]{1,0:T(8,128)} %downward.1, bf16[16,16384]{1,0:T(8,128)(2,1)S(1)} %collective-permute-done.2), kind=kLoop, calls=%fused_computation | loop fusion | flops 524288 | bytes 2621440 | tf_op jit(solution)/shard_map/transpose | solution.py:560
Async XLA Ops:
  2.7 46.2 %collective-permute-start.1 = (bf16[16,16512]{1,0:T(8,128)(2,1)}, bf16[16,16512]{1,0:T(8,128)(2,1)S(1)}, u32[]{:S(2)}, u32[]{:S(2)}) collective-permute-start(bf16[16,16512]{1,0:T(8,128)(2,1)} %pack.1.w_hbm), channel_id=1, source_target_pairs={{0,1},{1,2},{2,3},{3,4},{4,5},{5,6},{6,7},{7,8},{8,9},{9,10},{10,1... | collective-permute-start | bytes 1585160 | tf_op jit(solution)/shard_map/ppermute | solution.py:549
  4.7 44.3 %copy-start = (bf16[16,16512]{1,0:T(8,128)(2,1)S(1)}, bf16[16,16512]{1,0:T(8,128)(2,1)}, u32[]{:S(2)}) copy-start(bf16[16,16512]{1,0:T(8,128)(2,1)} %pack.1.w_hbm) | copy-start | bytes 1585156
  4.7 44.2 %collective-permute-start = (bf16[64,16384]{1,0:T(8,128)(2,1)}, bf16[64,16384]{1,0:T(8,128)(2,1)}, u32[]{:S(2)}, u32[]{:S(2)}) collective-permute-start(bf16[64,16384]{1,0:T(8,128)(2,1)} %bitcast.10), channel_id=1, source_target_pairs={{0,1},{1,2},{2,3},{3,4},{4,5},{5,6},{6,7},{7,8},{8,9},{9,10},{10,1... | collective-permute-start | bytes 6291464 | tf_op jit(solution)/shard_map/ppermute | solution.py:547
  35.2 33.0 %all-to-all-start = ((bf16[32,80,128]{2,1,0:T(8,128)(2,1)}), bf16[32,80,128]{2,1,0:T(8,128)(2,1)S(1)}, u32[]{:S(2)}, u32[]{:S(2)}) async-start(bf16[32,80,128]{2,1,0:T(8,128)(2,1)} %get-tuple-element.10), calls=%async_computation | async-start | bytes 1310720 | tf_op jit(solution)/shard_map/all_to_all | solution.py:553
  48.9 19.3 %copy-start.1 = (s32[31,128]{1,0:T(8,128)S(1)}, s32[31,128]{1,0:T(8,128)}, u32[]{:S(2)}) copy-start(s32[31,128]{1,0:T(8,128)} %top_pick.1) | copy-start | bytes 47620
  48.9 19.3 %copy-start.2 = (f32[16]{0:T(128)S(1)}, f32[16]{0:T(128)}, u32[]{:S(2)}) copy-start(f32[16]{0:T(128)} %ridge.1) | copy-start | bytes 196
  49.0 19.3 %copy-start.3 = (s32[16,64]{1,0:T(8,128)S(1)}, s32[16,64]{1,0:T(8,128)}, u32[]{:S(2)}) copy-start(s32[16,64]{1,0:T(8,128)} %get-tuple-element.9.lst) | copy-start | bytes 12292
  64.1 25.6 %collective-permute-start.2 = (bf16[16,16384]{1,0:T(8,128)(2,1)S(1)}, bf16[16,16384]{1,0:T(8,128)(2,1)S(1)}, u32[]{:S(2)}, u32[]{:S(2)}) collective-permute-start(bf16[16,16384]{1,0:T(8,128)(2,1)S(1)} %near_back.1.after), channel_id=1, source_target_pairs={{1,0},{2,1},{3,2},{4,3},{5,4},{6,5},{7,6},{8,7},{9,8},{10,9},{11,1... | collective-permute-start | bytes 1572872 | tf_op jit(solution)/shard_map/ppermute | solution.py:555

commit v8 on v7

--- a/solution.py
+++ b/solution.py
@@ -14,6 +14,7 @@
 SCALE = math.log2(math.e) / 32.0
 FEAT = 128
 GROUP = 16
+EARLY = 4.5
 
 
 def dot(a, b, ca=1, cb=0):
@@ -148,8 +149,8 @@
 
 
 def up_kernel(dims, pos_ref, x_hbm, w_hbm, ids, leaf_pick, local_pick, leaf_hbm, local_hbm,
-              terms_hbm, spread, list_low, acc,
-              pair, big, at, b, wt, xt, terms, lb, nb, coeff, skel, tiles, lv, lst, xs, ls, ms):
+              terms_hbm, spread, list_low, acc, pair,
+              big, at, b, wt, xt, terms, lb, nb, coeff, skel, tiles, lv, lst, xs, ls, ms):
     count, leaf, rank, dim, cols = dims
     entries = ids.shape[0]
     part = count // CHUNKS
@@ -243,7 +244,8 @@
 
     lax.fori_loop(0, count // (2 * PAIRS), body, 0)
     put_terms = copy(terms, terms_hbm, ms.at[2])
-    near_pairs(count, total, pair, at, b, wt, acc, big)
+    pair[pair.shape[0] - 1] = total
+    near_pairs(count, jnp.minimum(total, early_pairs(count)), pair, at, b, wt, acc, big)
     put_terms.wait()
 
 
@@ -263,8 +265,8 @@
             num_scalar_prefetch=1,
             grid=(1,),
             in_specs=[HBM, HBM, VM, VM, VM, HBM, HBM],
-            out_specs=[HBM, VM, VM, VM],
-            scratch_shapes=near_scratch(count, entries, leaf, dim, cols)
+            out_specs=[HBM, VM, VM, VM, pl.BlockSpec(memory_space=pltpu.SMEM)],
+            scratch_shapes=near_scratch(count, entries, leaf, dim, cols)[1:]
             + [
                 pltpu.VMEM((cols, (2 * count - 2) * rank), f32),
                 pltpu.VMEM(leaf_basis.shape, bf16),
@@ -284,6 +286,7 @@
             jax.ShapeDtypeStruct((subtrees, cols + dim, rank), bf16),
             jax.ShapeDtypeStruct((16, count), jnp.int32),
             jax.ShapeDtypeStruct((count + 1, cols, leaf), f32),
+            jax.ShapeDtypeStruct((pair_slots(count, entries) + 1,), jnp.int32),
         ],
         compiler_params=pltpu.CompilerParams(vmem_limit_bytes=60 << 20),
         cost_estimate=near_cost(12 * count, leaf, cols, 16 << 20),
@@ -305,17 +308,21 @@
         pair[total + u] = count * count
 
 
-def near_pairs(count, total, pair, at, b, w, acc, tiles):
+def early_pairs(count):
+    return int(EARLY * count) // (2 * GROUP) * 2 * GROUP
+
+
+def near_pairs(count, total, pair, at, b, w, acc, tiles, begin=0):
     h = GROUP
     leaf = b.shape[1]
     shift = count.bit_length() - 1
 
     def first(k, slot):
-        code = pair[k]
+        code = pair[begin + k]
         tiles[slot] = gauss(b[code & (count - 1)], at[(code >> shift) & (count - 1)])
 
     def second(k, slot):
-        code = pair[k]
+        code = pair[begin + k]
         return code >> shift, dot(w[:, lanes(code & (count - 1), leaf)], tiles[slot])
 
     for u in range(h):
@@ -332,13 +339,17 @@
                 acc[i] += o
         return carry
 
-    blocks = (total + h - 1) // h
+    blocks = (total - begin + h - 1) // h
     lax.fori_loop(0, (blocks + 1) // 2, body, 0)
+
+
+def pair_slots(count, entries):
+    return count * entries + entries + 4 * GROUP
 
 
 def near_scratch(count, entries, leaf, dim, cols):
     return [
-        pltpu.SMEM((count * entries + entries + 4 * GROUP,), jnp.int32),
+        pltpu.SMEM((pair_slots(count, entries),), jnp.int32),
         pltpu.VMEM((2 * GROUP, leaf, leaf), bf16),
         pltpu.VMEM((count, FEAT, leaf), bf16),
         pltpu.VMEM((count, leaf, FEAT), bf16),
@@ -372,12 +383,13 @@
     return finish
 
 
-def near_back_kernel(entries, low_hbm, x_hbm, wlow_hbm, w_hbm, out,
+def near_back_kernel(entries, left_over, low_hbm, x_hbm, wlow_hbm, w_hbm, own_hbm, out, own,
                      pair, tiles, at, b, w, x, y, acc, lf, lv, lst, xs, sems):
     count, _, leaf = at.shape
     get_list = copy(wlow_hbm.at[:, pl.ds(count * leaf, 128)], lf, sems.at[0])
     finish = two_sided(count, leaf, low_hbm, x_hbm, x, y, at, b, xs)
     get_w = copy(w_hbm, w, sems.at[1])
+    get_own = copy(own_hbm, own, sems.at[3])
     get_list.wait()
     lv[...] = lf[...].astype(f32).astype(jnp.int32)
     put_list = copy(lv, lst, sems.at[2])
@@ -392,21 +404,27 @@
         out[:, lanes(l, leaf)] = got.astype(out.dtype)
 
     grouped(count, 8, lambda l: acc[l], store)
-
-
-def near_back(x_low, x, w_low, w, after, count, entries, leaf):
+    get_own.wait()
+    all_own = left_over[left_over.shape[0] - 1]
+
+    @pl.when(all_own > early_pairs(count))
+    def _():
+        def keep(l, got):
+            at[l] = got
+
+        grouped(count, 16, lambda l: feature_pair(y[:, lanes(l, leaf)])[0], keep)
+        near_pairs(count, all_own, left_over, at, b, w, own, tiles, early_pairs(count))
+
+
+def near_back(left_over, x_low, x, w_low, w, n_own, count, entries, leaf):
     dim, cols = x.shape[0], w.shape[0]
-
-    def kernel(low_hbm, x_hbm, wlow_hbm, w_hbm, after_hbm, *rest):
-        near_back_kernel(entries, low_hbm, x_hbm, wlow_hbm, w_hbm, *rest)
-
     return pl.pallas_call(
-        kernel,
+        functools.partial(near_back_kernel, entries),
         grid_spec=pltpu.PrefetchScalarGridSpec(
-            num_scalar_prefetch=0,
+            num_scalar_prefetch=1,
             grid=(1,),
             in_specs=[ANY, HBM, ANY, HBM, HBM],
-            out_specs=VM,
+            out_specs=[VM, VM],
             scratch_shapes=near_scratch(count, entries, leaf, dim, cols)
             + [
                 pltpu.VMEM((dim, count * leaf), bf16),
@@ -415,14 +433,17 @@
                 pltpu.VMEM((cols, 128), jnp.int32),
                 pltpu.SMEM((cols, 128), jnp.int32),
                 pltpu.SemaphoreType.DMA((2, CHUNKS)),
-                pltpu.SemaphoreType.DMA((3,)),
+                pltpu.SemaphoreType.DMA((4,)),
             ],
         ),
-        out_shape=jax.ShapeDtypeStruct((cols, count * leaf), bf16),
+        out_shape=[
+            jax.ShapeDtypeStruct((cols, count * leaf), bf16),
+            jax.ShapeDtypeStruct((count + 1, cols, leaf), f32),
+        ],
         compiler_params=pltpu.CompilerParams(vmem_limit_bytes=52 << 20),
         cost_estimate=near_cost(4 * count, leaf, cols, 6 << 20),
         name="near_back",
-    )(x_low, x, w_low, w, after)
+    )(left_over, x_low, x, w_low, w, n_own)
 
 
 def down_kernel(dims, pos_ref, lst, ridge, gathered, top_pick, low_hbm, x_hbm, wlow_hbm, own_hbm,
@@ -547,11 +568,11 @@
     x_low = lax.ppermute(xt, AXES, upper)
     w = pack(pos, dt, ids)
     w_low = lax.ppermute(w, AXES, upper)
-    terms, spread, list_low, n_own = upward(
+    terms, spread, list_low, n_own, own_list = upward(
         pos, xt, w, ids, leaf_pick, local_pick, leaf_basis, local_basis, subtrees
     )
     gathered = lax.all_to_all(spread, AXES, 0, 0)
-    back = near_back(x_low, xt, w_low, w, n_own, count, entries, leaf)
+    back, n_own = near_back(own_list, x_low, xt, w_low, w, n_own, count, entries, leaf)
     returned = lax.ppermute(back, AXES, lower)
     out = downward(
         pos, list_low, ridge, gathered, top_pick, x_low, xt, w_low, n_own, top_basis, terms, local_basis, leaf_basis,

time: 92.7 us -> 92.4 us (level)
  the two profiles are of different devices: /device:TPU:16 before, /device:TPU:31 now
where the time goes in v8:
time: 92.4 us; the launch traced here: 91.9 us
  Pallas kernels  76.7 us (83%)
  starting transfers between devices  12.1 us (13%)
  other arithmetic  2.3 us (2%)
    pallas_call x1, Pallas kernels, upward(): pl.pallas_call(functools.partial(up_kernel, (count, leaf, rank, dim, cols...  28.2 us
    pallas_call x1, Pallas kernels, near_back(): pl.pallas_call(functools.partial(near_back_kernel, entries), grid_spec=pl...  26 us
    pallas_call x1, Pallas kernels, downward(): pl.pallas_call(functools.partial(down_kernel, (count, leaf, rank, dim, co...  19.8 us
    all_to_all x1, starting transfers between devices, shards(): gathered = lax.all_to_all(spread, AXES, 0, 0)  8.07 us
    pallas_call x1, Pallas kernels, pack(): pl.pallas_call(pack_kernel, grid_spec=pltpu.PrefetchScalarGridSpec(num_sc...  2.75 us
    transpose x1, other arithmetic, shards(): return (out + returned.astype(f32)).T  2.3 us
  transfers between devices with their start and end apart: 4, of which 0 were waited for; matrix products, arithmetic and copies ran while one was open for 0% of the time, Pallas kernels for 80%

profile of v8, /device:TPU:31, one launch (start us, length us, event | category | flops | bytes accessed | tf_op | source)
XLA Modules:
  0.0 91.9 jit_solution(10480641757428435026)
XLA Ops:
  0.0 2.7 %pack.1.w_hbm = bf16[16,16512]{1,0:T(8,128)(2,1)} custom-call(s32[1]{0:T(128)} %bitcast.pos_ref, f32[16,16384]{1,0:T(8,128)} %bitcast.6, s32[10,64]{1,0:T(8,128)} %bitcast.8), custom_call_target="tpu_custom_call" | custom-call | tf_op jit(solution)/shard_map/pack/pallas_call | solution.py:136
  2.8 1.3 %collective-permute-start.1 = (bf16[16,16512]{1,0:T(8,128)(2,1)}, bf16[16,16512]{1,0:T(8,128)(2,1)S(1)}, u32[]{:S(2)}, u32[]{:S(2)}) collective-permute-start(bf16[16,16512]{1,0:T(8,128)(2,1)} %pack.1.w_hbm), channel_id=1, source_target_pairs={{0,1},{1,2},{2,3},{3,4},{4,5},{5,6},{6,7},{7,8},{8,9},{9,10},{10,1... | collective-permute-start | bytes 1585160 | tf_op jit(solution)/shard_map/ppermute | solution.py:570
  4.1 0.0 copy-start
  4.1 1.4 %collective-permute-start = (bf16[64,16384]{1,0:T(8,128)(2,1)}, bf16[64,16384]{1,0:T(8,128)(2,1)}, u32[]{:S(2)}, u32[]{:S(2)}) collective-permute-start(bf16[64,16384]{1,0:T(8,128)(2,1)} %bitcast.10), channel_id=1, source_target_pairs={{0,1},{1,2},{2,3},{3,4},{4,5},{5,6},{6,7},{7,8},{8,9},{9,10},{10,1... | collective-permute-start | bytes 6291464 | tf_op jit(solution)/shard_map/ppermute | solution.py:568
  5.5 28.2 %upward.1 = (f32[16,16128]{1,0:T(8,128)}, bf16[32,80,128]{2,1,0:T(8,128)(2,1)}, s32[16,64]{1,0:T(8,128)}, f32[65,16,256]{2,1,0:T(8,128)}, s32[715]{0:T(1024)}) custom-call(s32[1]{0:T(128)} %bitcast.pos_ref, bf16[64,16384]{1,0:T(8,128)(2,1)} %bitcast.11, bf16[16,16512]{1,0:T(8,128)(2,1)} %pack.1.w_hbm, s32[10,64]{1,0:T(8,128)} %bitcast.9, ...), custom_call_target="tpu_custom_call" | custom-call | flops 51539607552 | bytes 16777216 | tf_op jit(solution)/shard_map/upward/pallas_call | solution.py:262
  33.7 8.1 %all-to-all-start = ((bf16[32,80,128]{2,1,0:T(8,128)(2,1)}), bf16[32,80,128]{2,1,0:T(8,128)(2,1)S(1)}, u32[]{:S(2)}, u32[]{:S(2)}) async-start(bf16[32,80,128]{2,1,0:T(8,128)(2,1)} %get-tuple-element.13), calls=%async_computation | async-start | bytes 1310720 | tf_op jit(solution)/shard_map/all_to_all | solution.py:574
  41.8 0.0 collective-permute-done.1.wlow_hbm
  41.8 0.0 collective-permute-done.low_hbm
  41.8 0.0 copy-done
  41.8 0.0 copy-start.3
  41.8 0.7 copy-done.3
  42.5 0.0 copy-start.1
  42.5 0.0 copy-start.2
  42.5 0.0 copy-start.4
  42.5 26.0 %near_back.1 = (bf16[16,16384]{1,0:T(8,128)(2,1)S(1)}, f32[65,16,256]{2,1,0:T(8,128)}) custom-call(s32[715]{0:T(1024)S(1)} %copy-done.3, bf16[64,16384]{1,0:T(8,128)(2,1)} %collective-permute-done.low_hbm, bf16[64,16384]{1,0:T(8,128)(2,1)} %bitcast.12, bf16[16,16512]{1,0:T(8,128)(2,1)S(1)} %collective-permute-done.1.wlow_hbm, bf16[16,16512]{1,0:T(8,128)(2,1)S(1)} %copy-done, ...), custom_call_target="tpu_custom_call" | custom-call | flops 17179869184 | bytes 6291456 | tf_op jit(solution)/shard_map/near_back/pallas_call | solution.py:421
  68.5 1.3 %collective-permute-start.2 = (bf16[16,16384]{1,0:T(8,128)(2,1)S(1)}, bf16[16,16384]{1,0:T(8,128)(2,1)S(1)}, u32[]{:S(2)}, u32[]{:S(2)}) collective-permute-start(bf16[16,16384]{1,0:T(8,128)(2,1)S(1)} %get-tuple-element.18.after), channel_id=1, source_target_pairs={{1,0},{2,1},{3,2},{4,3},{5,4},{6,5},{7,6},{8,7},{9,8},{10,9},{11,1... | collective-permute-start | bytes 1572872 | tf_op jit(solution)/shard_map/ppermute | solution.py:576
  69.8 0.0 all-to-all-done.gathered
  69.8 0.0 copy-done.1
  69.8 0.0 copy-done.2
  69.8 0.0 copy-done.4
  69.8 19.8 %downward.1 = f32[16,16384]{1,0:T(8,128)} custom-call(s32[1]{0:T(128)} %bitcast.pos_ref, s32[16,64]{1,0:T(8,128)S(1)} %copy-done.4, f32[16]{0:T(128)S(1)} %copy-done.2, bf16[32,80,128]{2,1,0:T(8,128)(2,1)S(1)} %all-to-all-done.gathered, s32[31,128]{1,0:T(8,128)S(1)} %copy-done.1, bf16[64,16384]{1,0:T(8,128)(2,1)} %collective-permute-done.low_hbm, ...), custom_call_target="tpu_custom_call" | custom-call | flops 34359738368 | bytes 20971520 | tf_op jit(solution)/shard_map/downward/pallas_call | solution.py:533
  89.6 0.0 collective-permute-done.2
  89.6 2.3 %add_bitcast_fusion = f32[16384,16]{0,1:T(8,128)} fusion(f32[16,16384]{1,0:T(8,128)} %downward.1, bf16[16,16384]{1,0:T(8,128)(2,1)S(1)} %collective-permute-done.2), kind=kLoop, calls=%fused_computation | loop fusion | flops 524288 | bytes 2621440 | tf_op jit(solution)/shard_map/transpose | solution.py:581
Async XLA Ops:
  2.8 39.0 %collective-permute-start.1 = (bf16[16,16512]{1,0:T(8,128)(2,1)}, bf16[16,16512]{1,0:T(8,128)(2,1)S(1)}, u32[]{:S(2)}, u32[]{:S(2)}) collective-permute-start(bf16[16,16512]{1,0:T(8,128)(2,1)} %pack.1.w_hbm), channel_id=1, source_target_pairs={{0,1},{1,2},{2,3},{3,4},{4,5},{5,6},{6,7},{7,8},{8,9},{9,10},{10,1... | collective-permute-start | bytes 1585160 | tf_op jit(solution)/shard_map/ppermute | solution.py:570
  4.1 37.7 %copy-start = (bf16[16,16512]{1,0:T(8,128)(2,1)S(1)}, bf16[16,16512]{1,0:T(8,128)(2,1)}, u32[]{:S(2)}) copy-start(bf16[16,16512]{1,0:T(8,128)(2,1)} %pack.1.w_hbm) | copy-start | bytes 1585156
  4.1 37.7 %collective-permute-start = (bf16[64,16384]{1,0:T(8,128)(2,1)}, bf16[64,16384]{1,0:T(8,128)(2,1)}, u32[]{:S(2)}, u32[]{:S(2)}) collective-permute-start(bf16[64,16384]{1,0:T(8,128)(2,1)} %bitcast.10), channel_id=1, source_target_pairs={{0,1},{1,2},{2,3},{3,4},{4,5},{5,6},{6,7},{7,8},{8,9},{9,10},{10,1... | collective-permute-start | bytes 6291464 | tf_op jit(solution)/shard_map/ppermute | solution.py:568
  33.7 36.1 %all-to-all-start = ((bf16[32,80,128]{2,1,0:T(8,128)(2,1)}), bf16[32,80,128]{2,1,0:T(8,128)(2,1)S(1)}, u32[]{:S(2)}, u32[]{:S(2)}) async-start(bf16[32,80,128]{2,1,0:T(8,128)(2,1)} %get-tuple-element.13), calls=%async_computation | async-start | bytes 1310720 | tf_op jit(solution)/shard_map/all_to_all | solution.py:574
  41.8 0.7 copy-start.3
  42.5 27.3 %copy-start.1 = (s32[31,128]{1,0:T(8,128)S(1)}, s32[31,128]{1,0:T(8,128)}, u32[]{:S(2)}) copy-start(s32[31,128]{1,0:T(8,128)} %top_pick.1) | copy-start | bytes 47620
  42.5 27.3 %copy-start.2 = (f32[16]{0:T(128)S(1)}, f32[16]{0:T(128)}, u32[]{:S(2)}) copy-start(f32[16]{0:T(128)} %ridge.1) | copy-start | bytes 196
  42.5 27.3 %copy-start.4 = (s32[16,64]{1,0:T(8,128)S(1)}, s32[16,64]{1,0:T(8,128)}, u32[]{:S(2)}) copy-start(s32[16,64]{1,0:T(8,128)} %get-tuple-element.12.lst) | copy-start | bytes 12292
  68.5 21.2 %collective-permute-start.2 = (bf16[16,16384]{1,0:T(8,128)(2,1)S(1)}, bf16[16,16384]{1,0:T(8,128)(2,1)S(1)}, u32[]{:S(2)}, u32[]{:S(2)}) collective-permute-start(bf16[16,16384]{1,0:T(8,128)(2,1)S(1)} %get-tuple-element.18.after), channel_id=1, source_target_pairs={{1,0},{2,1},{3,2},{4,3},{5,4},{6,5},{7,6},{8,7},{9,8},{10,9},{11,1... | collective-permute-start | bytes 1572872 | tf_op jit(solution)/shard_map/ppermute | solution.py:576

commit v9 on v8

--- a/solution.py
+++ b/solution.py
@@ -14,7 +14,7 @@
 SCALE = math.log2(math.e) / 32.0
 FEAT = 128
 GROUP = 16
-EARLY = 4.5
+EARLY = 5.5
 
 
 def dot(a, b, ca=1, cb=0):

time: 92.4 us -> 92.2 us (level)
  starting transfers between devices: 12.1 us -> 11.1 us
    pallas_call x1, Pallas kernels: 26 us -> 21.3 us  [near_back(): pl.pallas_call(functools.partial(near_back_kernel, entries), grid_spec=pl...]
    pallas_call x1, Pallas kernels: 28.2 us -> 31.3 us  [upward(): pl.pallas_call(functools.partial(up_kernel, (count, leaf, rank, dim, cols...]
    pallas_call x1, Pallas kernels: 19.8 us -> 21.4 us  [downward(): pl.pallas_call(functools.partial(down_kernel, (count, leaf, rank, dim, co...]
    all_to_all x1, starting transfers between devices: 8.07 us -> 7.1 us  [shards(): gathered = lax.all_to_all(spread, AXES, 0, 0)]
  transfers between devices with their start and end apart: 4 -> 4, of which waited for: 0 -> 0; matrix products, arithmetic and copies ran while one was open for 0% -> 0% of each run, Pallas kernels for 80% -> 81%
where the time goes in v9:
time: 92.2 us; the launch traced here: 90.9 us
  Pallas kernels  76.6 us (83%)
  starting transfers between devices  11.1 us (12%)
  other arithmetic  2.3 us (2%)
    pallas_call x1, Pallas kernels, upward(): pl.pallas_call(functools.partial(up_kernel, (count, leaf, rank, dim, cols...  31.3 us
    pallas_call x1, Pallas kernels, downward(): pl.pallas_call(functools.partial(down_kernel, (count, leaf, rank, dim, co...  21.4 us
    pallas_call x1, Pallas kernels, near_back(): pl.pallas_call(functools.partial(near_back_kernel, entries), grid_spec=pl...  21.3 us
    all_to_all x1, starting transfers between devices, shards(): gathered = lax.all_to_all(spread, AXES, 0, 0)  7.1 us
    pallas_call x1, Pallas kernels, pack(): pl.pallas_call(pack_kernel, grid_spec=pltpu.PrefetchScalarGridSpec(num_sc...  2.75 us
    transpose x1, other arithmetic, shards(): return (out + returned.astype(f32)).T  2.3 us
  transfers between devices with their start and end apart: 4, of which 0 were waited for; matrix products, arithmetic and copies ran while one was open for 0% of the time, Pallas kernels for 81%

profile of v9, /device:TPU:31, one launch (start us, length us, event | category | flops | bytes accessed | tf_op | source)
XLA Modules:
  0.0 90.9 jit_solution(2958322224788066102)
XLA Ops:
  0.0 2.7 %pack.1.w_hbm = bf16[16,16512]{1,0:T(8,128)(2,1)} custom-call(s32[1]{0:T(128)} %bitcast.pos_ref, f32[16,16384]{1,0:T(8,128)} %bitcast.6, s32[10,64]{1,0:T(8,128)} %bitcast.8), custom_call_target="tpu_custom_call" | custom-call | tf_op jit(solution)/shard_map/pack/pallas_call | solution.py:136
  2.8 1.3 %collective-permute-start.1 = (bf16[16,16512]{1,0:T(8,128)(2,1)}, bf16[16,16512]{1,0:T(8,128)(2,1)S(1)}, u32[]{:S(2)}, u32[]{:S(2)}) collective-permute-start(bf16[16,16512]{1,0:T(8,128)(2,1)} %pack.1.w_hbm), channel_id=1, source_target_pairs={{0,1},{1,2},{2,3},{3,4},{4,5},{5,6},{6,7},{7,8},{8,9},{9,10},{10,1... | collective-permute-start | bytes 1585160 | tf_op jit(solution)/shard_map/ppermute | solution.py:570
  4.1 0.0 copy-start
  4.1 1.4 %collective-permute-start = (bf16[64,16384]{1,0:T(8,128)(2,1)}, bf16[64,16384]{1,0:T(8,128)(2,1)}, u32[]{:S(2)}, u32[]{:S(2)}) collective-permute-start(bf16[64,16384]{1,0:T(8,128)(2,1)} %bitcast.10), channel_id=1, source_target_pairs={{0,1},{1,2},{2,3},{3,4},{4,5},{5,6},{6,7},{7,8},{8,9},{9,10},{10,1... | collective-permute-start | bytes 6291464 | tf_op jit(solution)/shard_map/ppermute | solution.py:568
  5.5 31.3 %upward.1 = (f32[16,16128]{1,0:T(8,128)}, bf16[32,80,128]{2,1,0:T(8,128)(2,1)}, s32[16,64]{1,0:T(8,128)}, f32[65,16,256]{2,1,0:T(8,128)}, s32[715]{0:T(1024)}) custom-call(s32[1]{0:T(128)} %bitcast.pos_ref, bf16[64,16384]{1,0:T(8,128)(2,1)} %bitcast.11, bf16[16,16512]{1,0:T(8,128)(2,1)} %pack.1.w_hbm, s32[10,64]{1,0:T(8,128)} %bitcast.9, ...), custom_call_target="tpu_custom_call" | custom-call | flops 51539607552 | bytes 16777216 | tf_op jit(solution)/shard_map/upward/pallas_call | solution.py:262
  36.8 7.1 %all-to-all-start = ((bf16[32,80,128]{2,1,0:T(8,128)(2,1)}), bf16[32,80,128]{2,1,0:T(8,128)(2,1)S(1)}, u32[]{:S(2)}, u32[]{:S(2)}) async-start(bf16[32,80,128]{2,1,0:T(8,128)(2,1)} %get-tuple-element.13), calls=%async_computation | async-start | bytes 1310720 | tf_op jit(solution)/shard_map/all_to_all | solution.py:574
  43.9 0.0 collective-permute-done.1.wlow_hbm
  43.9 0.0 collective-permute-done.low_hbm
  43.9 0.0 copy-done
  43.9 0.0 copy-start.3
  43.9 0.7 copy-done.3
  44.6 0.0 copy-start.1
  44.6 0.0 copy-start.2
  44.6 0.0 copy-start.4
  44.6 21.3 %near_back.1 = (bf16[16,16384]{1,0:T(8,128)(2,1)S(1)}, f32[65,16,256]{2,1,0:T(8,128)}) custom-call(s32[715]{0:T(1024)S(1)} %copy-done.3, bf16[64,16384]{1,0:T(8,128)(2,1)} %collective-permute-done.low_hbm, bf16[64,16384]{1,0:T(8,128)(2,1)} %bitcast.12, bf16[16,16512]{1,0:T(8,128)(2,1)S(1)} %collective-permute-done.1.wlow_hbm, bf16[16,16512]{1,0:T(8,128)(2,1)S(1)} %copy-done, ...), custom_call_target="tpu_custom_call" | custom-call | flops 17179869184 | bytes 6291456 | tf_op jit(solution)/shard_map/near_back/pallas_call | solution.py:421
  65.9 1.3 %collective-permute-start.2 = (bf16[16,16384]{1,0:T(8,128)(2,1)S(1)}, bf16[16,16384]{1,0:T(8,128)(2,1)S(1)}, u32[]{:S(2)}, u32[]{:S(2)}) collective-permute-start(bf16[16,16384]{1,0:T(8,128)(2,1)S(1)} %get-tuple-element.18.after), channel_id=1, source_target_pairs={{1,0},{2,1},{3,2},{4,3},{5,4},{6,5},{7,6},{8,7},{9,8},{10,9},{11,1... | collective-permute-start | bytes 1572872 | tf_op jit(solution)/shard_map/ppermute | solution.py:576
  67.2 0.0 all-to-all-done.gathered
  67.2 0.0 copy-done.1
  67.2 0.0 copy-done.2
  67.2 0.0 copy-done.4
  67.3 21.4 %downward.1 = f32[16,16384]{1,0:T(8,128)} custom-call(s32[1]{0:T(128)} %bitcast.pos_ref, s32[16,64]{1,0:T(8,128)S(1)} %copy-done.4, f32[16]{0:T(128)S(1)} %copy-done.2, bf16[32,80,128]{2,1,0:T(8,128)(2,1)S(1)} %all-to-all-done.gathered, s32[31,128]{1,0:T(8,128)S(1)} %copy-done.1, bf16[64,16384]{1,0:T(8,128)(2,1)} %collective-permute-done.low_hbm, ...), custom_call_target="tpu_custom_call" | custom-call | flops 34359738368 | bytes 20971520 | tf_op jit(solution)/shard_map/downward/pallas_call | solution.py:533
  88.6 0.0 collective-permute-done.2
  88.6 2.3 %add_bitcast_fusion = f32[16384,16]{0,1:T(8,128)} fusion(f32[16,16384]{1,0:T(8,128)} %downward.1, bf16[16,16384]{1,0:T(8,128)(2,1)S(1)} %collective-permute-done.2), kind=kLoop, calls=%fused_computation | loop fusion | flops 524288 | bytes 2621440 | tf_op jit(solution)/shard_map/transpose | solution.py:581
Async XLA Ops:
  2.8 41.1 %collective-permute-start.1 = (bf16[16,16512]{1,0:T(8,128)(2,1)}, bf16[16,16512]{1,0:T(8,128)(2,1)S(1)}, u32[]{:S(2)}, u32[]{:S(2)}) collective-permute-start(bf16[16,16512]{1,0:T(8,128)(2,1)} %pack.1.w_hbm), channel_id=1, source_target_pairs={{0,1},{1,2},{2,3},{3,4},{4,5},{5,6},{6,7},{7,8},{8,9},{9,10},{10,1... | collective-permute-start | bytes 1585160 | tf_op jit(solution)/shard_map/ppermute | solution.py:570
  4.1 39.9 %copy-start = (bf16[16,16512]{1,0:T(8,128)(2,1)S(1)}, bf16[16,16512]{1,0:T(8,128)(2,1)}, u32[]{:S(2)}) copy-start(bf16[16,16512]{1,0:T(8,128)(2,1)} %pack.1.w_hbm) | copy-start | bytes 1585156
  4.1 39.8 %collective-permute-start = (bf16[64,16384]{1,0:T(8,128)(2,1)}, bf16[64,16384]{1,0:T(8,128)(2,1)}, u32[]{:S(2)}, u32[]{:S(2)}) collective-permute-start(bf16[64,16384]{1,0:T(8,128)(2,1)} %bitcast.10), channel_id=1, source_target_pairs={{0,1},{1,2},{2,3},{3,4},{4,5},{5,6},{6,7},{7,8},{8,9},{9,10},{10,1... | collective-permute-start | bytes 6291464 | tf_op jit(solution)/shard_map/ppermute | solution.py:568
  36.8 30.4 %all-to-all-start = ((bf16[32,80,128]{2,1,0:T(8,128)(2,1)}), bf16[32,80,128]{2,1,0:T(8,128)(2,1)S(1)}, u32[]{:S(2)}, u32[]{:S(2)}) async-start(bf16[32,80,128]{2,1,0:T(8,128)(2,1)} %get-tuple-element.13), calls=%async_computation | async-start | bytes 1310720 | tf_op jit(solution)/shard_map/all_to_all | solution.py:574
  43.9 0.7 copy-start.3
  44.6 22.6 %copy-start.1 = (s32[31,128]{1,0:T(8,128)S(1)}, s32[31,128]{1,0:T(8,128)}, u32[]{:S(2)}) copy-start(s32[31,128]{1,0:T(8,128)} %top_pick.1) | copy-start | bytes 47620
  44.6 22.6 %copy-start.2 = (f32[16]{0:T(128)S(1)}, f32[16]{0:T(128)}, u32[]{:S(2)}) copy-start(f32[16]{0:T(128)} %ridge.1) | copy-start | bytes 196
  44.6 22.6 %copy-start.4 = (s32[16,64]{1,0:T(8,128)S(1)}, s32[16,64]{1,0:T(8,128)}, u32[]{:S(2)}) copy-start(s32[16,64]{1,0:T(8,128)} %get-tuple-element.12.lst) | copy-start | bytes 12292
  65.9 22.7 %collective-permute-start.2 = (bf16[16,16384]{1,0:T(8,128)(2,1)S(1)}, bf16[16,16384]{1,0:T(8,128)(2,1)S(1)}, u32[]{:S(2)}, u32[]{:S(2)}) collective-permute-start(bf16[16,16384]{1,0:T(8,128)(2,1)S(1)} %get-tuple-element.18.after), channel_id=1, source_target_pairs={{1,0},{2,1},{3,2},{4,3},{5,4},{6,5},{7,6},{8,7},{9,8},{10,9},{11,1... | collective-permute-start | bytes 1572872 | tf_op jit(solution)/shard_map/ppermute | solution.py:576

commit v10 on v9

--- a/solution.py
+++ b/solution.py
@@ -14,7 +14,7 @@
 SCALE = math.log2(math.e) / 32.0
 FEAT = 128
 GROUP = 16
-EARLY = 5.5
+EARLY = 5.0
 
 
 def dot(a, b, ca=1, cb=0):

time: 92.2 us -> 92.2 us (level); the launches traced: 90.9 us -> 92.6 us
  Pallas kernels: 76.6 us -> 78.3 us
    pallas_call x1, Pallas kernels: 21.3 us -> 24.4 us  [near_back(): pl.pallas_call(functools.partial(near_back_kernel, entries), grid_spec=pl...]
    pallas_call x1, Pallas kernels: 31.3 us -> 29.7 us  [upward(): pl.pallas_call(functools.partial(up_kernel, (count, leaf, rank, dim, cols...]
  transfers between devices with their start and end apart: 4 -> 4, of which waited for: 0 -> 0; matrix products, arithmetic and copies ran while one was open for 0% -> 0% of each run, Pallas kernels for 81% -> 82%
where the time goes in v10:
time: 92.2 us; the launch traced here: 92.6 us
  Pallas kernels  78.3 us (85%)
  starting transfers between devices  11.1 us (12%)
  other arithmetic  2.3 us (2%)
    pallas_call x1, Pallas kernels, upward(): pl.pallas_call(functools.partial(up_kernel, (count, leaf, rank, dim, cols...  29.7 us
    pallas_call x1, Pallas kernels, near_back(): pl.pallas_call(functools.partial(near_back_kernel, entries), grid_spec=pl...  24.4 us
    pallas_call x1, Pallas kernels, downward(): pl.pallas_call(functools.partial(down_kernel, (count, leaf, rank, dim, co...  21.4 us
    all_to_all x1, starting transfers between devices, shards(): gathered = lax.all_to_all(spread, AXES, 0, 0)  7.1 us
    pallas_call x1, Pallas kernels, pack(): pl.pallas_call(pack_kernel, grid_spec=pltpu.PrefetchScalarGridSpec(num_sc...  2.75 us
    transpose x1, other arithmetic, shards(): return (out + returned.astype(f32)).T  2.3 us
  transfers between devices with their start and end apart: 4, of which 0 were waited for; matrix products, arithmetic and copies ran while one was open for 0% of the time, Pallas kernels for 82%

profile of v10, /device:TPU:31, one launch (start us, length us, event | category | flops | bytes accessed | tf_op | source)
XLA Modules:
  0.0 92.6 jit_solution(6641337537659918547)
XLA Ops:
  0.0 2.7 %pack.1.w_hbm = bf16[16,16512]{1,0:T(8,128)(2,1)} custom-call(s32[1]{0:T(128)} %bitcast.pos_ref, f32[16,16384]{1,0:T(8,128)} %bitcast.6, s32[10,64]{1,0:T(8,128)} %bitcast.8), custom_call_target="tpu_custom_call" | custom-call | tf_op jit(solution)/shard_map/pack/pallas_call | solution.py:136
  2.8 1.3 %collective-permute-start.1 = (bf16[16,16512]{1,0:T(8,128)(2,1)}, bf16[16,16512]{1,0:T(8,128)(2,1)S(1)}, u32[]{:S(2)}, u32[]{:S(2)}) collective-permute-start(bf16[16,16512]{1,0:T(8,128)(2,1)} %pack.1.w_hbm), channel_id=1, source_target_pairs={{0,1},{1,2},{2,3},{3,4},{4,5},{5,6},{6,7},{7,8},{8,9},{9,10},{10,1... | collective-permute-start | bytes 1585160 | tf_op jit(solution)/shard_map/ppermute | solution.py:570
  4.1 0.0 copy-start
  4.1 1.4 %collective-permute-start = (bf16[64,16384]{1,0:T(8,128)(2,1)}, bf16[64,16384]{1,0:T(8,128)(2,1)}, u32[]{:S(2)}, u32[]{:S(2)}) collective-permute-start(bf16[64,16384]{1,0:T(8,128)(2,1)} %bitcast.10), channel_id=1, source_target_pairs={{0,1},{1,2},{2,3},{3,4},{4,5},{5,6},{6,7},{7,8},{8,9},{9,10},{10,1... | collective-permute-start | bytes 6291464 | tf_op jit(solution)/shard_map/ppermute | solution.py:568
  5.5 29.7 %upward.1 = (f32[16,16128]{1,0:T(8,128)}, bf16[32,80,128]{2,1,0:T(8,128)(2,1)}, s32[16,64]{1,0:T(8,128)}, f32[65,16,256]{2,1,0:T(8,128)}, s32[715]{0:T(1024)}) custom-call(s32[1]{0:T(128)} %bitcast.pos_ref, bf16[64,16384]{1,0:T(8,128)(2,1)} %bitcast.11, bf16[16,16512]{1,0:T(8,128)(2,1)} %pack.1.w_hbm, s32[10,64]{1,0:T(8,128)} %bitcast.9, ...), custom_call_target="tpu_custom_call" | custom-call | flops 51539607552 | bytes 16777216 | tf_op jit(solution)/shard_map/upward/pallas_call | solution.py:262
  35.2 7.1 %all-to-all-start = ((bf16[32,80,128]{2,1,0:T(8,128)(2,1)}), bf16[32,80,128]{2,1,0:T(8,128)(2,1)S(1)}, u32[]{:S(2)}, u32[]{:S(2)}) async-start(bf16[32,80,128]{2,1,0:T(8,128)(2,1)} %get-tuple-element.13), calls=%async_computation | async-start | bytes 1310720 | tf_op jit(solution)/shard_map/all_to_all | solution.py:574
  42.4 0.0 collective-permute-done.1.wlow_hbm
  42.4 0.0 collective-permute-done.low_hbm
  42.4 0.0 copy-done
  42.4 0.0 copy-start.3
  42.4 0.7 copy-done.3
  43.1 0.0 copy-start.1
  43.1 0.0 copy-start.2
  43.1 0.0 copy-start.4
  43.1 24.4 %near_back.1 = (bf16[16,16384]{1,0:T(8,128)(2,1)S(1)}, f32[65,16,256]{2,1,0:T(8,128)}) custom-call(s32[715]{0:T(1024)S(1)} %copy-done.3, bf16[64,16384]{1,0:T(8,128)(2,1)} %collective-permute-done.low_hbm, bf16[64,16384]{1,0:T(8,128)(2,1)} %bitcast.12, bf16[16,16512]{1,0:T(8,128)(2,1)S(1)} %collective-permute-done.1.wlow_hbm, bf16[16,16512]{1,0:T(8,128)(2,1)S(1)} %copy-done, ...), custom_call_target="tpu_custom_call" | custom-call | flops 17179869184 | bytes 6291456 | tf_op jit(solution)/shard_map/near_back/pallas_call | solution.py:421
  67.5 1.3 %collective-permute-start.2 = (bf16[16,16384]{1,0:T(8,128)(2,1)S(1)}, bf16[16,16384]{1,0:T(8,128)(2,1)S(1)}, u32[]{:S(2)}, u32[]{:S(2)}) collective-permute-start(bf16[16,16384]{1,0:T(8,128)(2,1)S(1)} %get-tuple-element.18.after), channel_id=1, source_target_pairs={{1,0},{2,1},{3,2},{4,3},{5,4},{6,5},{7,6},{8,7},{9,8},{10,9},{11,1... | collective-permute-start | bytes 1572872 | tf_op jit(solution)/shard_map/ppermute | solution.py:576
  68.8 0.0 all-to-all-done.gathered
  68.8 0.0 copy-done.1
  68.8 0.0 copy-done.2
  68.8 0.0 copy-done.4
  68.9 21.4 %downward.1 = f32[16,16384]{1,0:T(8,128)} custom-call(s32[1]{0:T(128)} %bitcast.pos_ref, s32[16,64]{1,0:T(8,128)S(1)} %copy-done.4, f32[16]{0:T(128)S(1)} %copy-done.2, bf16[32,80,128]{2,1,0:T(8,128)(2,1)S(1)} %all-to-all-done.gathered, s32[31,128]{1,0:T(8,128)S(1)} %copy-done.1, bf16[64,16384]{1,0:T(8,128)(2,1)} %collective-permute-done.low_hbm, ...), custom_call_target="tpu_custom_call" | custom-call | flops 34359738368 | bytes 20971520 | tf_op jit(solution)/shard_map/downward/pallas_call | solution.py:533
  90.2 0.0 collective-permute-done.2
  90.3 2.3 %add_bitcast_fusion = f32[16384,16]{0,1:T(8,128)} fusion(f32[16,16384]{1,0:T(8,128)} %downward.1, bf16[16,16384]{1,0:T(8,128)(2,1)S(1)} %collective-permute-done.2), kind=kLoop, calls=%fused_computation | loop fusion | flops 524288 | bytes 2621440 | tf_op jit(solution)/shard_map/transpose | solution.py:581
Async XLA Ops:
  2.8 39.6 %collective-permute-start.1 = (bf16[16,16512]{1,0:T(8,128)(2,1)}, bf16[16,16512]{1,0:T(8,128)(2,1)S(1)}, u32[]{:S(2)}, u32[]{:S(2)}) collective-permute-start(bf16[16,16512]{1,0:T(8,128)(2,1)} %pack.1.w_hbm), channel_id=1, source_target_pairs={{0,1},{1,2},{2,3},{3,4},{4,5},{5,6},{6,7},{7,8},{8,9},{9,10},{10,1... | collective-permute-start | bytes 1585160 | tf_op jit(solution)/shard_map/ppermute | solution.py:570
  4.1 38.3 %copy-start = (bf16[16,16512]{1,0:T(8,128)(2,1)S(1)}, bf16[16,16512]{1,0:T(8,128)(2,1)}, u32[]{:S(2)}) copy-start(bf16[16,16512]{1,0:T(8,128)(2,1)} %pack.1.w_hbm) | copy-start | bytes 1585156
  4.1 38.3 %collective-permute-start = (bf16[64,16384]{1,0:T(8,128)(2,1)}, bf16[64,16384]{1,0:T(8,128)(2,1)}, u32[]{:S(2)}, u32[]{:S(2)}) collective-permute-start(bf16[64,16384]{1,0:T(8,128)(2,1)} %bitcast.10), channel_id=1, source_target_pairs={{0,1},{1,2},{2,3},{3,4},{4,5},{5,6},{6,7},{7,8},{8,9},{9,10},{10,1... | collective-permute-start | bytes 6291464 | tf_op jit(solution)/shard_map/ppermute | solution.py:568
  35.2 33.6 %all-to-all-start = ((bf16[32,80,128]{2,1,0:T(8,128)(2,1)}), bf16[32,80,128]{2,1,0:T(8,128)(2,1)S(1)}, u32[]{:S(2)}, u32[]{:S(2)}) async-start(bf16[32,80,128]{2,1,0:T(8,128)(2,1)} %get-tuple-element.13), calls=%async_computation | async-start | bytes 1310720 | tf_op jit(solution)/shard_map/all_to_all | solution.py:574
  42.4 0.7 copy-start.3
  43.1 25.8 %copy-start.1 = (s32[31,128]{1,0:T(8,128)S(1)}, s32[31,128]{1,0:T(8,128)}, u32[]{:S(2)}) copy-start(s32[31,128]{1,0:T(8,128)} %top_pick.1) | copy-start | bytes 47620
  43.1 25.8 %copy-start.2 = (f32[16]{0:T(128)S(1)}, f32[16]{0:T(128)}, u32[]{:S(2)}) copy-start(f32[16]{0:T(128)} %ridge.1) | copy-start | bytes 196
  43.1 25.8 %copy-start.4 = (s32[16,64]{1,0:T(8,128)S(1)}, s32[16,64]{1,0:T(8,128)}, u32[]{:S(2)}) copy-start(s32[16,64]{1,0:T(8,128)} %get-tuple-element.12.lst) | copy-start | bytes 12292
  67.5 22.8 %collective-permute-start.2 = (bf16[16,16384]{1,0:T(8,128)(2,1)S(1)}, bf16[16,16384]{1,0:T(8,128)(2,1)S(1)}, u32[]{:S(2)}, u32[]{:S(2)}) collective-permute-start(bf16[16,16384]{1,0:T(8,128)(2,1)S(1)} %get-tuple-element.18.after), channel_id=1, source_target_pairs={{1,0},{2,1},{3,2},{4,3},{5,4},{6,5},{7,6},{8,7},{9,8},{10,9},{11,1... | collective-permute-start | bytes 1572872 | tf_op jit(solution)/shard_map/ppermute | solution.py:576
